TPU v7x, 32 devices: a whole 2x2x4 slice. The times are simulated.
32 devices in a mesh: fsdp: 8 (over y, x, core), sp: 4 (over z).
Axes of the slice: x: 2, y: 2, z: 4, core: 2. Of those that a mesh axis runs over, the one named last changes fastest.
Arguments:
- inputs: bfloat16 [32, 1024, 768], P('fsdp', 'sp'), may hold values from -6 to 6
- global_pos: int32 [32, 4], P('fsdp'), may hold values from 0 to 1023, as said below
- w_local: bfloat16 [3, 768, 768], P(None, 'fsdp'), may hold values from -0.21875 to 0.21875
- w_global: bfloat16 [3, 768, 768], P(None, 'fsdp'), may hold values from -0.3125 to 0.3125
- w_out: bfloat16 [768, 768], P('fsdp'), may hold values from -2.5 to 2.5
- b_proj: bfloat16 [6, 768], P(None, 'fsdp'), may hold values from -3 to 3
- gains: bfloat16 [2, 768], P(None, 'fsdp'), may hold values from 0.5 to 1.5
- shifts: bfloat16 [2, 768], P(None, 'fsdp'), may hold values from -3 to 3
- w_in: bfloat16 [768, 3072], P('fsdp'), may hold values from -0.21875 to 0.21875
- c_in: bfloat16 [3072], P('fsdp'), may hold values from -3 to 3
- w_back: bfloat16 [3072, 768], P('fsdp'), may hold values from -0.109375 to 0.109375
- cotangent: bfloat16 [32, 1024, 768], P('fsdp', 'sp'), may hold values from -6 to 6
Outputs:
- output: bfloat16 [32, 1024, 768], P('fsdp', 'sp')
- grad_inputs: bfloat16 [32, 1024, 768], P('fsdp', 'sp')
- grad_w_local: float32 [3, 768, 768], P(None, 'fsdp')
- grad_w_global: float32 [3, 768, 768], P(None, 'fsdp')
- grad_w_out: float32 [768, 768], P('fsdp')
- grad_b_proj: float32 [6, 768], P(None, 'fsdp')
- grad_gains: float32 [2, 768], P(None, 'fsdp')
- grad_shifts: float32 [2, 768], P(None, 'fsdp')
- grad_w_in: float32 [768, 3072], P('fsdp')
- grad_c_in: float32 [3072], P('fsdp')
- grad_w_back: float32 [3072, 768], P('fsdp')
Inputs may be any that keep to these rules, and one draw needn't show every extreme that they name: `global_pos`: in each sequence the 4 global positions are different; the first is 0 and the second is 1023.
All inputs are finite; a program needn't handle non-finite values.
Results may differ from a plain program's by a relative error of at most 0.017.
Values may be sent and summed in bfloat16 or wider, within the bound.
No kernel may reach another device: no remote copies, remote signals or barrier semaphores. Data moves between devices by JAX's collectives and lax.ppermute only.
A program may use at most 256 MiB of HBM per device.

v0:
```python
import jax
import jax.numpy as jnp
from jax import lax
from jax.experimental import pallas as pl
from jax.experimental.pallas import tpu as pltpu
from jax.sharding import PartitionSpec as P

HEADS = 12
HEAD_DIM = 64
WIN = 256
QB = 128
NEG = -1e9
GROUPS = 2
COST = 2 * 10**10
NORM_EPS = 1e-05
BF = jnp.bfloat16
F32 = jnp.float32
S = jax.ShapeDtypeStruct


def dot_nn(a,b): return jnp.dot(a,b,preferred_element_type=F32)
def dot_nt(a,b): return lax.dot_general(a,b,(((1,),(1,)),((),())),preferred_element_type=F32)
def dot_tn(a,b): return lax.dot_general(a,b,(((0,),(0,)),((),())),preferred_element_type=F32)

def split_pair(block):
    lane=lax.broadcasted_iota(jnp.int32,block.shape,1)
    zero=jnp.zeros_like(block)
    return jnp.concatenate([jnp.where(lane<HEAD_DIM,block,zero),jnp.where(lane<HEAD_DIM,zero,block)],axis=0)

def far_mask(pos, start):
    place=start+lax.broadcasted_iota(jnp.int32,(16,2*QB),1)%QB
    return (pos>=0)&(jnp.abs(place-pos)>WIN)

def edge_masks():
    row=lax.broadcasted_iota(jnp.int32,(QB,2*QB),0)
    col=lax.broadcasted_iota(jnp.int32,(QB,2*QB),1)%QB
    return row>=col, row<=col

def key_range(start,length):
    return max(0,start-WIN), min(length,start+QB+WIN)

def pick_head(both):
    row=lax.broadcasted_iota(jnp.int32,(2*HEAD_DIM,QB),0)
    return jnp.where(row<HEAD_DIM,both[:,:QB],both[:,QB:])

def masked_scores(raw,start,length,low_ok,high_ok):
    lo,hi=key_range(start,length)
    parts=[]
    for first in range(lo,hi,QB):
        chunk=raw[first-lo:first-lo+QB]
        if first==start-WIN: chunk=jnp.where(low_ok,chunk,NEG)
        elif first==start+WIN: chunk=jnp.where(high_ok,chunk,NEG)
        parts.append(chunk)
    return parts

def fwd_kernel(pos_ref,q_ref,k_ref,v_ref,ctx_ref,lse_ref):
    length=q_ref.shape[0]
    pos=pos_ref[...]
    token=lax.broadcasted_iota(jnp.int32,(16,length),1)
    sel=jnp.where(token==pos,1.0,0.0).astype(BF)
    key_far=dot_nn(sel,k_ref[...]).astype(BF)
    val_far_t=dot_nn(sel,v_ref[...]).astype(BF).T
    val_t=v_ref[...].T
    low_ok,high_ok=edge_masks()
    for start in range(0,length,QB):
        lo,hi=key_range(start,length)
        qq=split_pair(q_ref[start:start+QB,:])
        raw=dot_nt(k_ref[lo:hi,:],qq)
        parts=masked_scores(raw,start,length,low_ok,high_ok)
        far=jnp.where(far_mask(pos,start),dot_nt(key_far,qq),NEG)
        top=jnp.max(far,axis=0,keepdims=True)
        for part in parts: top=jnp.maximum(top,jnp.max(part,axis=0,keepdims=True))
        far_p=jnp.exp(far-top)
        total=jnp.sum(far_p,axis=0,keepdims=True)
        probs=[]
        for part in parts:
            p=jnp.exp(part-top)
            total=total+jnp.sum(p,axis=0,keepdims=True)
            probs.append(p.astype(BF))
        both=dot_nn(val_t[:,lo:hi],jnp.concatenate(probs,axis=0))+dot_nn(val_far_t,far_p.astype(BF))
        both=both*(1.0/total)
        ctx_ref[start:start+QB,:]=pick_head(both).T.astype(BF)
        lse=top+jnp.log(total)
        lse_ref[0,0:1,start:start+QB]=lse[:,:QB]
        lse_ref[0,1:2,start:start+QB]=lse[:,QB:]

def attn_fwd(pos,q,k,v):
    length,width=q.shape
    pairs=width//128
    col=pl.BlockSpec((length,128),lambda i:(0,i))
    return pl.pallas_call(fwd_kernel,grid=(pairs,),
        in_specs=[pl.BlockSpec((16,1),lambda i:(0,0)),col,col,col],
        out_specs=[col,pl.BlockSpec((1,8,length),lambda i:(i,0,0))],
        out_shape=[jax.ShapeDtypeStruct((length,width),BF),jax.ShapeDtypeStruct((pairs,8,length),F32)],
        compiler_params=params(),
        cost_estimate=cost(COST,1<<20),
        name="attend")(pos,q,k,v)

def bwd_kernel(pos_ref,q_ref,k_ref,v_ref,g_ref,ctx_ref,lse_ref,dq_ref,dk_ref,dv_ref,dk_acc,dv_acc,grad_scr):
    length=q_ref.shape[0]
    pos=pos_ref[...]
    token=lax.broadcasted_iota(jnp.int32,(16,length),1)
    sel_bool=token==pos
    sel=jnp.where(sel_bool,1.0,0.0).astype(BF)
    sel_full=jnp.where(sel_bool,1.0,0.0)
    key_far=dot_nn(sel,k_ref[...]).astype(BF)
    val_far=dot_nn(sel,v_ref[...]).astype(BF)
    key_far_t=key_far.T
    key_t=k_ref[...].T
    ones=jnp.ones((16,128),F32)
    is_glob=lax.dot_general(sel_full,ones,(((0,),(0,)),((),())),preferred_element_type=F32)
    grad_scr[...]=jnp.where(is_glob>0.5,0.0,g_ref[...].astype(F32)).astype(BF)
    prod=grad_scr[...].astype(F32)*ctx_ref[...].astype(F32)
    hrow=lax.broadcasted_iota(jnp.int32,(16,128),0)
    hlane=lax.broadcasted_iota(jnp.int32,(16,128),1)//HEAD_DIM
    hsel=jnp.where(hrow==hlane,1.0,0.0)
    delta_all=lax.dot_general(hsel,prod,(((1,),(1,)),((),())),preferred_element_type=F32,precision=lax.Precision.HIGHEST)
    dk_acc[...]=jnp.zeros_like(dk_acc)
    dv_acc[...]=jnp.zeros_like(dv_acc)
    dk_far=jnp.zeros((16,128),F32); dv_far=jnp.zeros((16,128),F32)
    low_ok,high_ok=edge_masks()
    for start in range(0,length,QB):
        lo,hi=key_range(start,length)
        qq=split_pair(q_ref[start:start+QB,:])
        gg=split_pair(grad_scr[start:start+QB,:])
        lse=jnp.concatenate([lse_ref[0,0:1,start:start+QB],lse_ref[0,1:2,start:start+QB]],axis=1)
        delta=jnp.concatenate([delta_all[0:1,start:start+QB],delta_all[1:2,start:start+QB]],axis=1)
        dq_t=jnp.zeros((128,2*QB),F32)
        def one(scores,vals):
            p=jnp.exp(scores-lse)
            dp=dot_nt(vals,gg)
            return p.astype(BF),(p*(dp-delta)).astype(BF)
        far=jnp.where(far_mask(pos,start),dot_nt(key_far,qq),NEG)
        p,ds=one(far,val_far)
        dv_far=dv_far+dot_nn(p,gg); dk_far=dk_far+dot_nn(ds,qq)
        dq_t=dq_t+dot_nn(key_far_t,ds)
        parts=masked_scores(dot_nt(k_ref[lo:hi,:],qq),start,length,low_ok,high_ok)
        plist=[];dlist=[]
        for n,part in enumerate(parts):
            a=lo+n*QB
            p,ds=one(part,v_ref[a:a+QB,:])
            plist.append(p);dlist.append(ds)
        p=jnp.concatenate(plist,axis=0); ds=jnp.concatenate(dlist,axis=0)
        dv_acc[lo:hi,:]+=dot_nn(p,gg)
        dk_acc[lo:hi,:]+=dot_nn(ds,qq)
        dq_t=dq_t+dot_nn(key_t[:,lo:hi],ds)
        dq_ref[start:start+QB,:]=(pick_head(dq_t).T.astype(BF).astype(F32)*(HEAD_DIM**-0.5)).astype(BF)
    dk_ref[...]=(dk_acc[...]+lax.dot_general(sel_full,dk_far,(((0,),(0,)),((),())),preferred_element_type=F32,precision=lax.Precision.HIGHEST)).astype(BF)
    dv_ref[...]=(dv_acc[...]+lax.dot_general(sel_full,dv_far,(((0,),(0,)),((),())),preferred_element_type=F32,precision=lax.Precision.HIGHEST)).astype(BF)

def attn_bwd(pos,q,k,v,grad,ctx,lse,first,pairs):
    length,width=q.shape
    col=pl.BlockSpec((length,128),lambda i:(0,first+i))
    out_col=pl.BlockSpec((length,128),lambda i:(0,i))
    out=jax.ShapeDtypeStruct((length,128*pairs),BF)
    return pl.pallas_call(bwd_kernel,grid=(pairs,),
        in_specs=[pl.BlockSpec((16,1),lambda i:(0,0)),col,col,col,col,col,pl.BlockSpec((1,8,length),lambda i:(first+i,0,0))],
        out_specs=[out_col,out_col,out_col],
        out_shape=[out,out,out],
        scratch_shapes=[pltpu.VMEM((length,128),F32),pltpu.VMEM((length,128),F32),pltpu.VMEM((length,128),BF)],
        compiler_params=params(),
        cost_estimate=cost(COST,1<<20),
        name="attend_back")(pos,q,k,v,grad,ctx,lse)


ANY=pl.BlockSpec(memory_space=pl.ANY)
SMEM=pl.BlockSpec(memory_space=pltpu.SMEM)
RB=256

def cost(flops,nbytes,trans=0):
    return pl.CostEstimate(flops=int(flops),bytes_accessed=int(nbytes),transcendentals=int(trans))

def params(mib=60):
    return pltpu.CompilerParams(vmem_limit_bytes=mib<<20)

def fetches(pieces,place,sems,me,first,rows,sem0):
    out=[]
    for slot,piece in enumerate(pieces):
        owner=me^slot
        out.append(pltpu.make_async_copy(piece.at[pl.ds(first,rows)],place.at[pl.ds(pl.multiple_of(owner*rows,rows),rows)],sems.at[sem0+slot]))
    return out

def ffn_in_copies(refs,place,sems,sem0):
    if len(refs)>1: return [pltpu.make_async_copy(refs[0],place,sems.at[sem0])]
    pack=refs[0]; n,_,width=pack.shape; shard=place.shape[0]//n
    return [pltpu.make_async_copy(pack.at[s,pl.ds(j*shard,shard)],place.at[pl.ds(s*shard,shard),pl.ds(j*width,width)],sems.at[sem0+s*(place.shape[1]//width)+j])
            for s in range(n) for j in range(place.shape[1]//width)]


def ffn_back_copies(refs,place,sems,sem0):
    if len(refs)>1: return [pltpu.make_async_copy(refs[1],place,sems.at[sem0])]
    pack=refs[0]; n,rows,width=pack.shape; shard=place.shape[0]//n; first=rows-4*(width//n)-shard
    return [pltpu.make_async_copy(pack.at[s,pl.ds(first,shard)],place.at[pl.ds(s*shard,shard)],sems.at[sem0+s]) for s in range(n)]


def plane_copies(refs,plane,place,sems,sem0):
    width=place.shape[0]
    if len(refs)>1: return [pltpu.make_async_copy(refs[2].at[pl.ds(plane*width,width)],place,sems.at[sem0])]
    pack=refs[0]; n,rows,_=pack.shape; shard=width//n; first=rows-(4-plane)*shard
    return [pltpu.make_async_copy(pack.at[s,pl.ds(first,shard)],place.at[pl.ds(s*shard,shard)],sems.at[sem0+s]) for s in range(n)]


def stats(value):
    center=value-jnp.mean(value,axis=-1,keepdims=True)
    inverse=lax.rsqrt(jnp.mean(center*center,axis=-1,keepdims=True)+NORM_EPS)
    return center*inverse,inverse

def norm_back(scaled,normed,inverse):
    return inverse*(scaled-jnp.mean(scaled,axis=-1,keepdims=True)-normed*jnp.mean(scaled*normed,axis=-1,keepdims=True))

def gelu_pair(inner):
    cdf=0.5*(1.0+lax.erf(inner*0.7071067811865476))
    return inner*cdf, cdf+inner*(0.3989422804014327*jnp.exp(-0.5*inner*inner))

def chunk_store(chunks,me,value):
    for slot,chunk in enumerate(chunks):
        @pl.when(pl.program_id(0)^me==slot)
        def _(chunk=chunk): chunk[...]=value


def layer(mez,pos,ctx,ctxg,x,upstream,ffw,vecs,c_row,n):
    length,width=x.shape; ff=c_row.shape[1]; w=len(ffw); steps=length//RB; blocks=ff//width; shard=width//n; fs=ff//n
    def body(mez_ref,pos_ref,ctx_ref,glob_ref,x_ref,up_ref,vec_ref,c_ref,*refs):
        ff_w=refs[:w]; chunks=refs[w:w+steps]
        gs_ref,ag_ref,mg_ref,merged_ref,vg_ref,cg_ref,pack,wout,win,wback,acc_in,acc_back,act,slope,stage,sems,out_sems=refs[w+steps:]
        step=pl.program_id(0)
        first=step==0
        co=plane_copies(ff_w,3,wout,sems,0)
        ci=ffn_in_copies(ff_w,win,sems,n)
        cb=ffn_back_copies(ff_w,wback,sems,n+n*blocks)
        @pl.when(first)
        def _():
            for c in co+ci+cb: c.start()
            vg_ref[...]=jnp.zeros_like(vg_ref); cg_ref[...]=jnp.zeros_like(cg_ref)
            acc_in[...]=jnp.zeros_like(acc_in); acc_back[...]=jnp.zeros_like(acc_back)
            for c in co: c.wait()
        token=step*RB+lax.broadcasted_iota(jnp.int32,(16,RB),1)
        hot=jnp.where(token==pos_ref[...],1.0,0.0).astype(BF)
        is_glob=dot_tn(hot,jnp.ones((16,128),BF))[:,0:1]>0.5
        merged=jnp.where(is_glob,dot_tn(hot,glob_ref[...]),ctx_ref[...].astype(F32)).astype(BF)
        merged_ref[...]=merged
        hat1,inv1=stats(x_ref[...].astype(F32)+(dot_nn(merged,wout[...])+vec_ref[4:5,:]))
        norm1=hat1*vec_ref[6:7,:]+vec_ref[8:9,:]
        low=norm1.astype(BF)
        @pl.when(first)
        def _():
            for c in ci: c.wait()
        for a in range(0,ff,width):
            one,two=gelu_pair(dot_nn(low,win[:,a:a+width])+c_ref[:,a:a+width])
            act[:,a:a+width]=one.astype(BF); slope[:,a:a+width]=two.astype(BF)
        @pl.when(first)
        def _():
            for c in cb: c.wait()
        hat2,inv2=stats(norm1+(dot_nn(act[...],wback[...])+vec_ref[5:6,:]))
        chunk_store(chunks,mez_ref[0],(hat2*vec_ref[7:8,:]+vec_ref[9:10,:]).astype(BF))
        up=up_ref[...].astype(F32)
        col=lambda v:jnp.sum(v,axis=0,keepdims=True)
        vg_ref[7:8,:]+=col(up*hat2); vg_ref[9:10,:]+=col(up)
        second=norm_back(up*vec_ref[7:8,:],hat2,inv2)
        bg=second.astype(BF)
        vg_ref[5:6,:]+=col(bg.astype(F32))
        acc=second
        for a in range(0,ff,width):
            ig=(dot_nt(bg,wback[a:a+width,:])*slope[:,a:a+width].astype(F32)).astype(BF)
            cg_ref[:,a:a+width]+=col(ig.astype(F32))
            acc=acc+dot_nt(ig,win[:,a:a+width])
            acc_in[:,a:a+width]+=dot_tn(low,ig)
            acc_back[a:a+width,:]+=dot_tn(act[:,a:a+width],bg)
        vg_ref[6:7,:]+=col(acc*hat1); vg_ref[8:9,:]+=col(acc)
        gs=norm_back(acc*vec_ref[6:7,:],hat1,inv1)
        gs_ref[...]=gs
        ag=gs.astype(BF)
        ag_ref[...]=ag
        vg_ref[4:5,:]+=col(ag.astype(F32))
        mg_ref[...]=dot_nt(ag,wout[...]).astype(BF)
        @pl.when(step==steps-1)
        def _():
            copies=[]
            for b in range(2*blocks):
                slot=b%2
                if b>=2: copies[b-2].wait()
                if b<blocks:
                    stage[slot]=acc_in[:,b*width:(b+1)*width].astype(BF)
                    here=stage.at[slot].reshape(n,shard,width)
                    there=pack.at[:,pl.ds(b*shard,shard)]
                else:
                    at=(b-blocks)*width
                    stage[slot]=acc_back[at:at+width,:].astype(BF)
                    if n==1:
                        here,there=stage.at[slot],pack.at[0,pl.ds(blocks*shard+at,width)]
                    else:
                        here=stage.at[slot].reshape(width//fs,fs,width)
                        there=pack.at[pl.ds(at//fs,width//fs),pl.ds(blocks*shard,fs)]
                copies.append(pltpu.make_async_copy(here,there,out_sems.at[b]))
                copies[b].start()
            for c in copies[-2:]: c.wait()
    blk=lambda w:pl.BlockSpec((RB,w),lambda i:(i,0))
    full=lambda s:pl.BlockSpec(s,lambda i:(0,0))
    return pl.pallas_call(body,grid=(steps,),
        in_specs=[SMEM,full(pos.shape),blk(width),full(ctxg.shape),blk(width),blk(width),full(vecs.shape),full(c_row.shape)]+[ANY]*w,
        out_specs=[full((RB,width))]*steps+[blk(width)]*4+[full((16,width)),full((1,ff)),ANY],
        out_shape=[S((RB,width),BF)]*steps+[S((length,width),F32)]+[S((length,width),BF)]*3+[S((16,width),F32),S((1,ff),F32),S((n,blocks*shard+fs,width),BF)],
        scratch_shapes=[pltpu.VMEM((width,width),BF),pltpu.VMEM((width,ff),BF),pltpu.VMEM((ff,width),BF),pltpu.VMEM((width,ff),F32),pltpu.VMEM((ff,width),F32),
            pltpu.VMEM((RB,ff),BF),pltpu.VMEM((RB,ff),BF),pltpu.VMEM((2,width,width),BF),pltpu.SemaphoreType.DMA((2*n+n*blocks,)),pltpu.SemaphoreType.DMA((2*blocks,))],
        compiler_params=params(),cost_estimate=cost(COST,1<<20),name="layer")(mez,pos,ctx,ctxg,x,upstream,vecs,c_row,*ffw)


def local_grads(me,x,grads,unit=None,vec=None,count=8):
    length,width=x.shape; cols=grads[0].shape[1]; shard=width//count; half=count//2; k=len(grads)
    tail=0 if vec is None else 16
    rows=k*shard+tail
    base=0 if unit is None else unit[0].shape[1]-rows
    extra=([] if vec is None else [vec])+([] if unit is None else list(unit))
    def body(me_ref,x_ref,*refs):
        outs=refs[k+len(extra):]
        keep,send,res,keep_v,send_v,vec_v,sems=outs
        m=me_ref[0]
        xt=x_ref[...].T
        for r in range(k):
            res[...]=dot_nn(xt,refs[r][...])
            for slot in range(count):
                part=res[pl.ds(pl.multiple_of((m^slot)*shard,shard),shard),:]
                (send_v if slot%2 else keep_v)[slot//2,r*shard:(r+1)*shard,:]=part.astype(BF)
        if vec is not None:
            vec_v[...]=jnp.zeros_like(vec_v)
            for s in range(count):
                vec_v[s,:,0:shard]=refs[k][:,s*shard:(s+1)*shard]
            for slot in range(count):
                (send_v if slot%2 else keep_v)[slot//2,k*shard:rows,:]=vec_v[m^slot].astype(BF)
        cps=[pltpu.make_async_copy(v,o.at[:,pl.ds(base,rows)],sems.at[i]) for i,(v,o) in enumerate(((keep_v,keep),(send_v,send)))]
        for c in cps: c.start()
        for c in cps: c.wait()
    o=S((half,base+rows,cols),BF)
    vm=pl.BlockSpec(memory_space=pltpu.VMEM)
    first=1+1+k+(0 if vec is None else 1)
    return pl.pallas_call(body,in_specs=[SMEM]+[vm]*(first-1)+[ANY]*(0 if unit is None else 2),out_specs=[ANY]*2,out_shape=[o,o],
        input_output_aliases={} if unit is None else {first:0,first+1:1},
        scratch_shapes=[pltpu.VMEM((width,cols),F32),pltpu.VMEM((half,rows,cols),BF),pltpu.VMEM((half,rows,cols),BF),pltpu.VMEM((count,16,cols),F32),pltpu.SemaphoreType.DMA((2,))],
        compiler_params=params(),cost_estimate=cost(COST,1<<20),name="local_grads")(me,x,*grads,*extra)


def collect(mez,pieces):
    def body(mez_ref,*refs):
        for slot in range(len(pieces)):
            @pl.when(pl.program_id(0)^mez_ref[0]==slot)
            def _(slot=slot): refs[-1][0]=refs[slot][...]
    rows,width=pieces[0].shape; n=len(pieces)
    return pl.pallas_call(body,grid=(n,),in_specs=[SMEM]+[pl.BlockSpec((rows,width),lambda i:(0,0))]*n,
        out_specs=pl.BlockSpec((1,rows,width),lambda i:(i,0,0)),out_shape=S((n,rows,width),BF),
        compiler_params=params(),cost_estimate=cost(COST,1<<20),name="collect")(mez,*pieces)


def project(me,x,pieces,vecs):
    length,width=x.shape; n=len(pieces); shard=width//n
    def body(me_ref,x_ref,vec_ref,*refs):
        ins=refs[:n]; q_ref,k_ref,v_ref,wts,sems=refs[n:]
        m=me_ref[0]
        cps=[fetches(ins,wts.at[j],sems,m,j*shard,shard,j*n) for j in range(3)]
        for j in range(3):
            for c in cps[j]: c.start()
        for c in cps[0]: c.wait()
        scale=HEAD_DIM**-0.5
        for a in range(0,length,RB):
            q_ref[a:a+RB,:]=((dot_nn(x_ref[a:a+RB,:],wts[0])+vec_ref[0:1,:])*scale).astype(BF)
        for c in cps[1]: c.wait()
        for a in range(0,length,RB):
            k_ref[a:a+RB,:]=dot_nn(x_ref[a:a+RB,:],wts[1]).astype(BF)
        for c in cps[2]: c.wait()
        for a in range(0,length,RB):
            v_ref[a:a+RB,:]=(dot_nn(x_ref[a:a+RB,:],wts[2])+vec_ref[1:2,:]).astype(BF)
    vm=pl.BlockSpec(memory_space=pltpu.VMEM)
    return pl.pallas_call(body,in_specs=[SMEM,vm,vm]+[ANY]*n,out_specs=[vm]*3,out_shape=[S((length,width),BF)]*3,
        scratch_shapes=[pltpu.VMEM((3,width,width),BF),pltpu.SemaphoreType.DMA((3*n,))],
        compiler_params=params(),cost_estimate=cost(COST,1<<20),name="project")(me,x,vecs,*pieces)

def own_mask(width):
    return lax.broadcasted_iota(jnp.int32,(16,width),0)==lax.broadcasted_iota(jnp.int32,(16,width),1)//HEAD_DIM

def one_hot(pos,length):
    return jnp.where(lax.broadcasted_iota(jnp.int32,(16,length),1)==pos,1.0,0.0)

def scatter_heads(rows,own,count):
    zero=jnp.zeros((16,rows.shape[1]),F32)
    return jnp.concatenate([jnp.where(own,jnp.broadcast_to(rows[g:g+1,:].astype(F32),zero.shape),zero) for g in range(count)],axis=0).astype(BF)

def gather_heads(value,own,count):
    rows=[jnp.sum(jnp.where(own,value[16*g:16*g+16],0.0),axis=0,keepdims=True) for g in range(count)]
    rows.append(jnp.zeros((16-count,value.shape[1]),F32))
    return jnp.concatenate(rows,axis=0)

def globals_fwd(pos,x,ffw,vecs,count,n):
    length,width=x.shape; wide=16*count; w=len(ffw)
    def body(pos_ref,x_ref,vec_ref,*refs):
        ins=refs[:w]; ctx_ref,p_ref,u_ref,y_ref,q_ref,r_ref,wts,sems=refs[w:]
        cps=[plane_copies(ins,j,wts.at[j],sems,j*n) for j in range(3)]
        for j in range(3):
            for c in cps[j]: c.start()
        own=own_mask(width)
        sel=one_hot(pos_ref[...],length).astype(BF)
        rows=dot_nn(sel,x_ref[...]).astype(BF)
        r_ref[...]=rows
        for c in cps[0]: c.wait()
        q=((dot_nn(rows,wts[0])+vec_ref[2:3,:])*(HEAD_DIM**-0.5)).astype(BF)
        q_ref[...]=q
        for c in cps[1]: c.wait()
        u=dot_nt(wts[1],scatter_heads(q,own,count)).astype(BF)
        u_ref[...]=u
        s=dot_nn(x_ref[...],u)
        p=jnp.exp(s-jnp.max(s,axis=0,keepdims=True))
        p=p/jnp.sum(p,axis=0,keepdims=True)
        p_ref[...]=p
        low=p.astype(BF)
        y=dot_tn(low,x_ref[...]).astype(BF)
        y_ref[...]=y
        mass=dot_tn(low,jnp.ones((length,128),BF))[:,0:1]
        for c in cps[2]: c.wait()
        ctx_ref[...]=gather_heads(dot_nn(y,wts[2])+mass*vec_ref[3:4,:],own,count).astype(BF)
    vm=pl.BlockSpec(memory_space=pltpu.VMEM)
    return pl.pallas_call(body,in_specs=[vm,vm,vm]+[ANY]*w,out_specs=[vm]*6,
        out_shape=[S((16,width),BF),S((length,wide),F32),S((width,wide),BF),S((wide,width),BF),S((16,width),BF),S((16,width),BF)],
        scratch_shapes=[pltpu.VMEM((3,width,width),BF),pltpu.SemaphoreType.DMA((3*n,))],
        compiler_params=params(),cost_estimate=cost(COST,1<<20),name="globals")(pos,x,vecs,*ffw)

def globals_bwd(me,pos,x,mg,gs,p,u,y,q,rows,merged,ag,ffw,vecs,count,n,extra):
    length,width=x.shape; shard=width//n; half=max(n//2,1); w=len(ffw); cols=width//2
    def body(me_ref,pos_ref,x_ref,mg_ref,gs_ref,p_ref,u_ref,y_ref,q_ref,r_ref,merged_ref,ag_ref,vec_ref,*refs):
        ins=refs[:w]; out_ref,keep,send,keep2,send2,vg_ref,wts,res,keep_v,send_v,sems=refs[w:]
        m=me_ref[0]
        cps=[plane_copies(ins,j,wts.at[j],sems,j*n) for j in range(3)]
        for j in (2,1,0):
            for c in cps[j]: c.start()
        own=own_mask(width)
        hot=one_hot(pos_ref[...],length)
        sel=hot.astype(BF)
        x=x_ref[...]
        cs=scatter_heads(dot_nn(sel,mg_ref[...]).astype(BF),own,count)
        qs=scatter_heads(q_ref[...],own,count)
        for c in cps[2]: c.wait()
        v=dot_nt(wts[2],cs).astype(BF)
        shift=dot_nt(jnp.broadcast_to(vec_ref[3:4,:],(16,width)).astype(BF),cs)[0:1,:]
        dp=dot_nn(x,v)+shift
        p=p_ref[...]
        low=p.astype(BF)
        ds=(p*(dp-jnp.sum(p*dp,axis=0,keepdims=True))).astype(BF)
        a=dot_tn(ds,x).astype(BF)
        for c in cps[1]: c.wait()
        pre=(gather_heads(dot_nn(a,wts[1]),own,count).astype(BF).astype(F32)*(HEAD_DIM**-0.5)).astype(BF)
        for c in cps[0]: c.wait()
        rows_grad=dot_nt(pre,wts[0])
        mass=dot_tn(low,jnp.ones((length,128),BF))[:,0:1]
        vg_ref[...]=jnp.zeros_like(vg_ref)
        vg_ref[2:3,:]=jnp.sum(pre.astype(F32),axis=0,keepdims=True)
        vg_ref[3:4,:]=jnp.sum(mass*cs.astype(F32),axis=0,keepdims=True)
        out_ref[...]=gs_ref[...]+dot_nt(ds,u_ref[...])+dot_nt(low,v)+lax.dot_general(hot,rows_grad,(((0,),(0,)),((),())),preferred_element_type=F32,precision=lax.Precision.HIGHEST)
        for j,(l,r) in enumerate(((r_ref[...],pre),(a,qs),(y_ref[...],cs),(merged_ref[...],ag_ref[...]))):
            res[...]=dot_tn(l,r)
            for slot in range(n):
                for h in range(2):
                    part=res[pl.ds(pl.multiple_of((m^slot)*shard,shard),shard),h*cols:(h+1)*cols]
                    (send_v if slot%2 else keep_v)[slot//2,(2*j+h)*shard:(2*j+h+1)*shard,:]=part.astype(BF)
        cps=[]
        for here,first,there in ((keep_v,0,keep),(keep_v,6*shard,keep2),(send_v,0,send),(send_v,6*shard,send2)):
            if n==1 and here is send_v: continue
            rows_out=6*shard if first==0 else 2*shard
            cps.append(pltpu.make_async_copy(here.at[:,pl.ds(first,rows_out)],there.at[:,pl.ds(0,rows_out)],sems.at[3*n+len(cps)]))
        for c in cps: c.start()
        for c in cps: c.wait()
    vm=pl.BlockSpec(memory_space=pltpu.VMEM)
    o1=S((half,6*shard,cols),BF)
    o2=S((half,2*shard+extra,cols),BF)
    return pl.pallas_call(body,in_specs=[SMEM]+[vm]*12+[ANY]*w,out_specs=[vm,ANY,ANY,ANY,ANY,vm],
        out_shape=[S((length,width),F32),o1,o1,o2,o2,S((16,width),F32)],
        scratch_shapes=[pltpu.VMEM((3,width,width),BF),pltpu.VMEM((width,width),F32),pltpu.VMEM((half,8*shard,cols),BF),pltpu.VMEM((half,8*shard,cols),BF),pltpu.SemaphoreType.DMA((3*n+4,))],
        compiler_params=params(),cost_estimate=cost(COST,1<<20),name="globals_back")(me,pos,x,mg,gs,p,u,y,q,rows,merged,ag,vecs,*ffw)


def inputs_back(me,mez,gs,groups,pieces):
    length,width=gs.shape; n=len(pieces); shard=width//n; g=len(groups); cols=width//g
    steps=length//RB
    def body(me_ref,mez_ref,gs_ref,*refs):
        parts=refs[:3*g]; ins=refs[3*g:3*g+n]; chunks=refs[3*g+n:3*g+n+steps]; vg_ref,wts,sems=refs[3*g+n+steps:]
        m=me_ref[0]
        @pl.when(pl.program_id(0)==0)
        def _():
            cps=sum([fetches(ins,wts.at[j],sems,m,j*shard,shard,j*n) for j in range(3)],[])
            for c in cps: c.start()
            vg_ref[...]=jnp.zeros_like(vg_ref)
            for c in cps: c.wait()
        acc=gs_ref[...]
        for j in range(g):
            a=j*cols
            for w in range(3): acc=acc+dot_nt(parts[3*j+w][...],wts[w,:,a:a+cols])
            vg_ref[0:1,a:a+cols]+=jnp.sum(parts[3*j][...].astype(F32),axis=0,keepdims=True)
            vg_ref[1:2,a:a+cols]+=jnp.sum(parts[3*j+2][...].astype(F32),axis=0,keepdims=True)
        chunk_store(chunks,mez_ref[0],acc.astype(BF))
    blk=pl.BlockSpec((RB,width),lambda i:(i,0))
    part=pl.BlockSpec((RB,cols),lambda i:(i,0))
    return pl.pallas_call(body,grid=(length//RB,),in_specs=[SMEM,SMEM,blk]+[part]*(3*g)+[ANY]*n,
        out_specs=[pl.BlockSpec((RB,width),lambda i:(0,0))]*steps+[pl.BlockSpec((16,width),lambda i:(0,0))],out_shape=[S((RB,width),BF)]*steps+[S((16,width),F32)],
        scratch_shapes=[pltpu.VMEM((3,width,width),BF),pltpu.SemaphoreType.DMA((3*n,))],
        compiler_params=params(),cost_estimate=cost(COST,1<<20),name="inputs_back")(me,mez,gs,*[p for t in groups for p in t],*pieces)


def flip(value, axis, bit):
    count = lax.axis_size(axis)
    return lax.ppermute(value, axis, [(index, index ^ bit) for index in range(count)])


def tie(value, *others):
    return lax.optimization_barrier((value,) + others)[0]


def spread_slots(unit, order):
    slots = {0: unit}
    for bit in order:
        for slot in list(slots):
            slots[slot | bit] = flip(slots[slot], "fsdp", bit)
    return [slots[slot] for slot in range(len(slots))]


def add(one, two):
    return one.astype(F32) + two.astype(F32)


def meet(values, parts, *others):
    flat = [list(part.got) if isinstance(part.got, list) else [part.got] for part in parts]
    joined = tuple(values) + tuple(got for gots in flat for got in gots) + others
    joined = list(lax.optimization_barrier(joined))
    values = [joined.pop(0) for _ in values]
    for part, gots in zip(parts, flat):
        new = [joined.pop(0) for _ in gots]
        part.got = new if isinstance(part.got, list) else new[0]
    return values


class Exchange:
    def __init__(self, chunks):
        self.got = [chunks[0]] + [flip(chunks[k], "sp", k) for k in range(1, len(chunks))]


class Reduction:
    def __init__(self, keep, send, x_first):
        self.keep, self.first, self.step = keep, send, 0
        self.got = flip(send, "fsdp", 1)
        self.x_first = x_first

    def advance(self, *gates):
        got = tie(self.got, *gates)
        x_now = self.x_first == (self.step == 0)
        if self.step == 0:
            keep = self.keep.reshape((2, 2) + self.keep.shape[1:])
            got = got.reshape(keep.shape)
            if self.x_first:
                away, here = (keep[:, 1], got[:, 1]), (keep[:, 0], got[:, 0])
            else:
                away, here = (keep[1], got[1]), (keep[0], got[0])
        else:
            away, here = (self.mine[1], got[1]), (self.mine[0], got[0])
        self.send, self.mine = add(*away).astype(BF), add(*here)
        self.got = flip(self.send, "fsdp", 2 if x_now else 4)
        self.step += 1
        return self.send

    def total(self):
        return add(self.mine, self.got)


class SpSum:
    def __init__(self, value, start=True):
        self.low, self.high = lax.axis_index("sp") & 1, lax.axis_index("sp") >> 1
        rows = value.shape[0] // 4
        self.shape = value.shape
        self.value = value.reshape(2, 2, rows, value.shape[1])
        self.got = self.value
        self.step = 0
        if start:
            self.start()

    def start(self):
        self.value = self.got
        self.exchange(self.low, 1)

    def exchange(self, mine, bit):
        send = lax.dynamic_index_in_dim(self.value, 1 - mine, 0, keepdims=False).astype(BF)
        self.value = lax.dynamic_index_in_dim(self.value, mine, 0, keepdims=False)
        self.send, self.got = send, flip(send, "sp", bit)

    def join(self, mine):
        return jnp.stack(
            [jnp.where(mine == 0, self.value, self.got), jnp.where(mine == 0, self.got, self.value)]
        )

    def advance(self):
        if self.step == 0:
            self.value = add(self.value, self.got)
            self.exchange(self.high, 2)
        elif self.step == 1:
            self.value = add(self.value, self.got).astype(BF)
            self.got = flip(self.value, "sp", 2)
        else:
            self.value = self.join(self.high)
            self.got = flip(self.value, "sp", 1)
        self.step += 1

    def total(self):
        return self.join(self.low).reshape(self.shape).astype(F32)


def per_device(
    inputs,
    global_pos,
    w_local,
    w_global,
    w_out,
    b_proj,
    gains,
    shifts,
    w_in,
    c_in,
    w_back,
    cotangent,
):
    sp_count = lax.axis_size("sp")
    fsdp_count = lax.axis_size("fsdp")
    sp_index = lax.axis_index("sp")
    fsdp_index = lax.axis_index("fsdp")
    own_seqs = inputs.shape[0] // sp_count
    glob_count = global_pos.shape[1]
    shard, width = w_out.shape
    ff_shard = w_back.shape[0]
    ff_width = w_in.shape[1]
    tree = fsdp_count == 8 and sp_count == 4 and own_seqs == 1 and shard % 32 == 0
    tree = tree and inputs.shape[1] == RB

    def to_sequence(value):
        if own_seqs == 1:
            moved = lax.all_to_all(value, "sp", split_axis=0, concat_axis=0)
            return moved.reshape(1, -1, width)
        return lax.all_to_all(value, "sp", split_axis=0, concat_axis=1, tiled=True)

    def to_tokens(values):
        if own_seqs == 1:
            return lax.all_to_all(
                values[0].reshape(sp_count, -1, width), "sp", split_axis=0, concat_axis=0
            )
        return lax.all_to_all(jnp.stack(values), "sp", split_axis=1, concat_axis=0, tiled=True)

    own_pos = lax.dynamic_slice_in_dim(global_pos, sp_index * own_seqs, own_seqs, 0)
    blocks = ff_width // width
    x_all = to_sequence(inputs)
    vec_rows = [b_proj, gains, shifts, c_in.reshape(-1, shard)]
    small = jnp.concatenate(vec_rows, axis=0)
    small = jnp.pad(small, ((0, 16 - small.shape[0]), (0, 0)))
    if tree:
        me = fsdp_index.reshape(1).astype(jnp.int32)
        mez = sp_index.reshape(1).astype(jnp.int32)
        first = jnp.concatenate(
            [w_local.reshape(-1, width), jnp.pad(small, ((0, 0), (0, width - shard)))], axis=0
        )
        local_w = spread_slots(first, (2, 4, 1))
        pack = jnp.concatenate(
            [
                w_in.reshape(shard, blocks, width).transpose(1, 0, 2).reshape(-1, width),
                w_back,
                w_global.reshape(-1, width),
                w_out,
            ],
            axis=0,
        )
        ffw = [lax.all_gather(pack, "fsdp")]
        small_all = jnp.stack([piece[3 * shard :, :shard] for piece in local_w])
        small_all = small_all[me[0] ^ jnp.arange(fsdp_count, dtype=jnp.int32)]
    else:
        me = mez = jnp.zeros((1,), jnp.int32)
        local_w = [lax.all_gather(w_local, "fsdp", axis=1, tiled=True).reshape(-1, width)]
        full_global = lax.all_gather(w_global, "fsdp", axis=1, tiled=True).reshape(-1, width)
        full_out = lax.all_gather(w_out, "fsdp", axis=0, tiled=True)
        ffw = [lax.all_gather(value, "fsdp", axis=0, tiled=True) for value in (w_in, w_back)]
        ffw.append(jnp.concatenate([full_global, full_out], axis=0))
        small_all = lax.all_gather(small, "fsdp")
    count = len(local_w)
    up_all = to_sequence(tie(cotangent, x_all))
    vecs = small_all.transpose(1, 0, 2).reshape(16, width).astype(F32)
    c_rows = small_all[:, 10 : 10 + ff_shard // shard].astype(F32)
    c_row = c_rows.reshape(1, ff_width)

    outs, input_grads, totals = [], [], None
    for index in range(own_seqs):
        x = x_all[index]
        pos = jnp.full((16, 1), -1, jnp.int32).at[:glob_count, 0].set(own_pos[index])
        q, k, v = project(me, x, local_w, vecs)
        ctx, lse = attn_fwd(pos, q, k, v)
        ctx_glob, probs, keys, mixed, query, rows = globals_fwd(
            pos, x, ffw, vecs, glob_count, count
        )
        *out, grad_sum, attn_grad, merged_grad, merged, vec_one, c_grad, ff_pack = layer(
            mez, pos, ctx, ctx_glob, x, up_all[index], ffw, vecs, c_row, count
        )
        if tree:
            out_moved = Exchange(out)
        else:
            outs.append(jnp.concatenate(out, axis=0))
        if tree:
            ff_mine = lax.psum_scatter(ff_pack, "fsdp", scatter_dimension=0, tiled=False)
            merged_grad = tie(merged_grad, ff_pack)
        grad_sum, keep_one, send_one, keep_two, send_two, vec_two = globals_bwd(
            me,
            pos,
            x,
            merged_grad,
            grad_sum,
            probs,
            keys,
            mixed,
            query,
            rows,
            merged,
            attn_grad,
            ffw,
            vecs,
            glob_count,
            count,
            3 * shard if tree else 0,
        )
        group_pairs = width // 128 // GROUPS
        groups = []
        if tree:
            one = Reduction(keep_one, send_one, True)
            merged_grad = tie(merged_grad, send_one)
        for group in range(GROUPS):
            parts = attn_bwd(
                pos, q, k, v, merged_grad, ctx, lse, group * group_pairs, group_pairs
            )
            groups.append(parts)
            if tree and group == 0:
                two = Reduction(*local_grads(me, x, parts, unit=(keep_two, send_two)), False)
                (merged_grad,) = meet([merged_grad], [out_moved], two.first)
        if tree:
            (grad_sum,) = meet([grad_sum], [one, two], parts[0])
            grad_sum = tie(grad_sum, one.advance(), two.advance())
        *input_grad, vec_three = inputs_back(me, mez, grad_sum, groups, local_w)
        if tree:
            grads_moved = Exchange(input_grad)
        else:
            input_grads.append(jnp.concatenate(input_grad, axis=0))
        c_grad = c_grad.reshape(fsdp_count, -1, shard).transpose(1, 0, 2).reshape(-1, width)
        vec = vec_one + vec_two + vec_three + jnp.pad(c_grad, ((10, 6 - c_grad.shape[0]), (0, 0)))
        if not tree:
            g_in = ff_pack[0, :ff_width].reshape(blocks, width, width).transpose(1, 0, 2)
            g_in = g_in.reshape(width, ff_width).astype(F32)
            g_back = ff_pack[0, ff_width:].astype(F32)
            g_mixed = jnp.concatenate([keep_one[0], keep_two[0]], axis=0)
            g_mixed = g_mixed.reshape(4, 2, width, width // 2).transpose(0, 2, 1, 3)
            grads = (
                g_back,
                g_in,
                g_mixed.reshape(4, width, width).astype(F32),
                jnp.stack(
                    [
                        jnp.concatenate([dot_tn(x, part[w]) for part in groups], axis=1)
                        for w in range(3)
                    ]
                ),
                vec,
            )
            totals = grads if totals is None else tuple(a + b for a, b in zip(totals, grads))
    if tree:
        x_late, ff_mine = meet([x, ff_mine], [], *input_grad)
        ff_sum = SpSum(ff_mine.astype(F32))
        x_late = tie(x_late, ff_sum.send)
        late = Reduction(*local_grads(me, x_late, groups[-1], vec=vec), False)
        meet([], [one, two, ff_sum, grads_moved], late.first)
        one.advance()
        two.advance()
        ff_sum.advance()
        meet([], [late], one.send, two.send, ff_sum.send)
        late.advance()
        meet([], [one, two, late, ff_sum])
        early_sum = SpSum(jnp.concatenate([one.total(), two.total()], axis=0))
        late.advance()
        ff_sum.advance()
        out = collect(mez, out_moved.got)
        meet([], [late, ff_sum, early_sum])
        late_sum = SpSum(late.total())
        early_sum.advance()
        ff_sum.advance()
        grad_inputs = collect(mez, grads_moved.got)
        meet([], [early_sum, late_sum, ff_sum])
        early_sum.advance()
        late_sum.advance()
        s_ff = ff_sum.total()
        meet([], [early_sum, late_sum])
        early_sum.advance()
        late_sum.advance()
        meet([], [early_sum, late_sum])
        late_sum.advance()
        s_early, s_late = early_sum.total(), late_sum.total()
        half_mixed = s_early[: 8 * shard].reshape(4, 2, shard, -1).transpose(0, 2, 1, 3)
        s_mixed = half_mixed.reshape(4, shard, width)
        s_local = jnp.concatenate(
            [
                s_early[8 * shard :].reshape(3, shard, -1),
                s_late[: 3 * shard].reshape(3, shard, -1),
            ],
            axis=2,
        )
        mine = s_late[3 * shard :, :shard]
        s_in = s_ff[: blocks * shard].reshape(blocks, shard, width).transpose(1, 0, 2)
        s_in = s_in.reshape(shard, ff_width)
        s_back = s_ff[blocks * shard :]
    else:
        out, grad_inputs = to_tokens(outs), to_tokens(input_grads)
        g_back, g_in, g_mixed, g_local, vec = totals

        def reduce(value, dim):
            mine = lax.psum_scatter(value.astype(BF), "fsdp", scatter_dimension=dim, tiled=True)
            return lax.psum(mine, "sp").astype(F32)

        s_back, s_in = reduce(g_back, 0), reduce(g_in, 0)
        s_mixed = reduce(g_mixed, 1)
        s_local = reduce(g_local, 1)
        vec = lax.psum(vec, ("fsdp", "sp"))
        mine = lax.dynamic_slice_in_dim(vec, fsdp_index * shard, shard, 1)
    c_mine = mine[10 : 10 + ff_shard // shard].reshape(-1)
    return (
        out,
        grad_inputs,
        s_local,
        s_mixed[:3],
        s_mixed[3],
        mine[:6],
        mine[6:8],
        mine[8:10],
        s_in,
        c_mine,
        s_back,
    )


def solution(mesh):
    rows = P("fsdp", None)
    tokens = P("fsdp", "sp", None)
    columns = P(None, "fsdp")
    stacked = P(None, "fsdp", None)
    return jax.shard_map(
        per_device,
        mesh=mesh,
        in_specs=(
            tokens,
            rows,
            stacked,
            stacked,
            rows,
            columns,
            columns,
            columns,
            rows,
            P("fsdp"),
            rows,
            tokens,
        ),
        out_specs=(
            tokens,
            tokens,
            stacked,
            stacked,
            rows,
            columns,
            columns,
            columns,
            rows,
            P("fsdp"),
            rows,
        ),
        check_vma=False,
    )
```

profile of v0, /device:TPU:0, one launch (start us, length us, event | category | flops | bytes accessed | tf_op | source)
XLA Modules:
  0.0 409.8 jit_solution(6523443655280651987)
XLA Ops:
  8.3 2.6 pad_maximum_fusion
  12.1 3.0 collective-permute-start.1
  15.1 1.5 collective-permute-start.3
  16.6 4.9 %all-to-all-start = ((bf16[4,256,768]{2,1,0:T(8,128)(2,1)}), bf16[4,256,768]{2,1,0:T(8,128)(2,1)S(1)}, u32[]{:S(2)}, u32[]{:S(2)}) async-start(bf16[4,256,768]{2,1,0:T(8,128)(2,1)} %param.14), calls=%async_computation | async-start | bytes 3145728 | tf_op jit(solution)/shard_map/all_to_all | solution.py:637
  21.5 6.5 %collective-permute-done.1.refs_2_.refs_8_ = bf16[304,768]{1,0:T(8,128)(2,1)S(1)} collective-permute-done((bf16[304,768]{1,0:T(8,128)(2,1)S(1)}, bf16[304,768]{1,0:T(8,128)(2,1)S(1)}, u32[]{:S(2)}, u32[]{:S(2)}) %collective-permute-start.1) | collective-permute-done | bytes 466976 | tf_op jit(solution)/shard_map/ppermute | solution.py:506
  28.0 1.3 collective-permute-start.5
  30.5 21.0 %collective-permute-done.5.refs_6_.refs_12_ = bf16[304,768]{1,0:T(8,128)(2,1)} collective-permute-done((bf16[304,768]{1,0:T(8,128)(2,1)S(1)}, bf16[304,768]{1,0:T(8,128)(2,1)}, u32[]{:S(2)}, u32[]{:S(2)}) %collective-permute-start.5) | collective-permute-done | bytes 466976 | tf_op jit(solution)/shard_map/ppermute | solution.py:506
  56.4 2.7 all-to-all-done
  59.1 3.6 all-to-all-start.1
  62.7 8.8 %project.1 = (bf16[1024,768]{1,0:T(8,128)(2,1)}, bf16[1024,768]{1,0:T(8,128)(2,1)}, bf16[1024,768]{1,0:T(8,128)(2,1)}) custom-call(s32[1]{0:T(128)} %bitcast.2.me_ref, bf16[1024,768]{1,0:T(8,128)(2,1)} %bitcast.189, f32[16,768]{1,0:T(8,128)} %reshape.231.vec_ref, bf16[304,768]{1,0:T(8,128)(2,1)} %copy-done.16, bf16[304,768]{1,0:T(8,128)(2,1)} %copy-done.27, ...), custom_call_target="tpu_custom_call" | custom-call | flops 20000000000 | bytes 1048576 | tf_op jit(solution)/shard_map/project/pallas_call | solution.py:372
  71.6 25.8 %attend.1 = (bf16[1024,768]{1,0:T(8,128)(2,1)}, f32[6,8,1024]{2,1,0:T(8,128)}) custom-call(s32[16,1]{1,0:T(8,128)} %scatter.4.pos_ref, bf16[1024,768]{1,0:T(8,128)(2,1)} %get-tuple-element.102.q_ref, bf16[1024,768]{1,0:T(8,128)(2,1)} %get-tuple-element.103.k_ref, bf16[1024,768]{1,0:T(8,128)(2,1)} %get-tuple-element.104.v_ref), custom_call_target="tpu_custom_call" | custom-call | flops 20000000000 | bytes 1048576 | tf_op jit(solution)/shard_map/attend/pallas_call | solution.py:91
  97.3 7.1 %all-gather.3.cloned.1.call-done = bf16[9216,768]{1,0:T(8,128)(2,1)} async-done(((bf16[1152,768]{1,0:T(8,128)(2,1)}), bf16[9216,768]{1,0:T(8,128)(2,1)}) %all-gather.3.cloned.1.call-update) | async-done | bytes 14155792 | tf_op jit(solution)/shard_map/all_gather | solution.py:670
  104.5 6.5 %globals.1 = (bf16[16,768]{1,0:T(8,128)(2,1)}, f32[1024,64]{1,0:T(8,128)}, bf16[768,64]{1,0:T(8,128)(2,1)}, bf16[64,768]{1,0:T(8,128)(2,1)}, bf16[16,768]{1,0:T(8,128)(2,1)}, /*index=5*/bf16[16,768]{1,0:T(8,128)(2,1)}) custom-call(s32[16,1]{1,0:T(8,128)} %scatter.4.pos_ref, bf16[1024,768]{1,0:T(8,128)(2,1)} %bitcast.190, f32[16,768]{1,0:T(8,128)} %reshape.231.vec_ref, ...), custom_call_target="tpu_custom_call" | custom-call | flops 20000000000 | bytes 1048576 | tf_op jit(solution)/shard_map/globals/pallas_call | solution.py:419
  111.0 1.2 copy-done.11
  112.3 59.3 %layer.1 = (bf16[256,768]{1,0:T(8,128)(2,1)}, bf16[256,768]{1,0:T(8,128)(2,1)}, bf16[256,768]{1,0:T(8,128)(2,1)}, bf16[256,768]{1,0:T(8,128)(2,1)}, f32[1024,768...) custom-call(s32[1]{0:T(128)} %bitcast.mez_ref, ...), custom_call_target="tpu_custom_call" | custom-call | flops 20000000000 | bytes 1048576 | tf_op jit(solution)/shard_map/layer/pallas_call | solution.py:299
  171.6 18.6 %globals_back.1 = (f32[1024,768]{1,0:T(8,128)}, bf16[4,576,384]{2,1,0:T(8,128)(2,1)}, bf16[4,576,384]{2,1,0:T(8,128)(2,1)}, bf16[4,480,384]{2,1,0:T(8,128)(2,1)}...) custom-call(s32[1]{0:T(128)} %bitcast.2.me_ref, s32[16,1]{1,0:T(8,128)} %scatter.4.pos_ref, ...), custom_call_target="tpu_custom_call" | custom-call | flops 20000000000 | bytes 1048576 | tf_op jit(solution)/shard_map/globals_back/pallas_call | solution.py:471
  190.5 1.5 collective-permute-start.7
  192.0 2.4 collective-permute-start.8
  194.9 19.0 %attend_back.2 = (bf16[1024,384]{1,0:T(8,128)(2,1)}, bf16[1024,384]{1,0:T(8,128)(2,1)}, bf16[1024,384]{1,0:T(8,128)(2,1)}) custom-call(s32[16,1]{1,0:T(8,128)} %scatter.4.pos_ref, bf16[1024,768]{1,0:T(8,128)(2,1)} %get-tuple-element.102.q_ref, bf16[1024,768]{1,0:T(8,128)(2,1)} %get-tuple-element.103.k_ref, bf16[1024,768]{1,0:T(8,128)(2,1)} %get-tuple-element.104.v_ref, ...), custom_call_target="tpu_custom_call" | custom-call | flops 20000000000 | bytes 1048576 | tf_op jit(solution)/shard_map/attend_back/pallas_call | solution.py:156
  213.9 6.1 %local_grads.2 = (bf16[4,480,384]{2,1,0:T(8,128)(2,1)}, bf16[4,480,384]{2,1,0:T(8,128)(2,1)}) custom-call(s32[1]{0:T(128)} %bitcast.2.me_ref, bf16[1024,768]{1,0:T(8,128)(2,1)} %bitcast.193, bf16[1024,384]{1,0:T(8,128)(2,1)} %get-tuple-element.125.refs_0_, ...), custom_call_target="tpu_custom_call", output_to_operand_aliasing={{0}: (5, {}), {1}: (6, {})} | custom-call | flops 20000000000 | bytes 1048576 | tf_op jit(solution)/shard_map/local_grads/pallas_call | solution.py:336
  220.1 1.6 collective-permute-done.8.refs_2_
  223.3 19.2 %attend_back.3 = (bf16[1024,384]{1,0:T(8,128)(2,1)}, bf16[1024,384]{1,0:T(8,128)(2,1)}, bf16[1024,384]{1,0:T(8,128)(2,1)}) custom-call(s32[16,1]{1,0:T(8,128)} %scatter.4.pos_ref, bf16[1024,768]{1,0:T(8,128)(2,1)} %get-tuple-element.102.q_ref, bf16[1024,768]{1,0:T(8,128)(2,1)} %get-tuple-element.103.k_ref, bf16[1024,768]{1,0:T(8,128)(2,1)} %get-tuple-element.104.v_ref, ...), custom_call_target="tpu_custom_call" | custom-call | flops 20000000000 | bytes 1048576 | tf_op jit(solution)/shard_map/attend_back/pallas_call | solution.py:156
  243.6 1.2 copy-done.14
  244.8 3.1 convert_add_fusion.1
  247.9 11.1 %inputs_back.1 = (bf16[256,768]{1,0:T(8,128)(2,1)}, bf16[256,768]{1,0:T(8,128)(2,1)}, bf16[256,768]{1,0:T(8,128)(2,1)}, bf16[256,768]{1,0:T(8,128)(2,1)}, f32[16,768]{1,0:T(8,128)}) custom-call(s32[1]{0:T(128)} %bitcast.2.me_ref, s32[1]{0:T(128)} %bitcast.mez_ref, f32[1024,768]{1,0:T(8,128)} %get-tuple-element.143.gs_ref, ...), custom_call_target="tpu_custom_call" | custom-call | flops 20000000000 | bytes 1048576 | tf_op jit(solution)/shard_map/inputs_back/pallas_call | solution.py:498
  259.0 7.3 %collective-permute-start.15 = (bf16[256,768]{1,0:T(8,128)(2,1)}, bf16[256,768]{1,0:T(8,128)(2,1)S(1)}, u32[]{:S(2)}, u32[]{:S(2)}) collective-permute-start(bf16[256,768]{1,0:T(8,128)(2,1)} %get-tuple-element.147), channel_id=1, source_target_pairs={{0,1},{1,0},{2,3},{3,2},{4,5},{5,4},{6,7},{7,6},{8,9},{9,8},{10,11... | collective-permute-start | bytes 1179656 | tf_op jit(solution)/shard_map/ppermute | solution.py:506
  268.7 1.2 collective-permute-start.12
  270.9 1.4 collective-permute-start.17
  272.4 1.4 pad_add_fusion.refs_3_
  273.8 1.5 convert.6
  276.1 3.9 collective-permute-done.15.refs_1_
  280.1 6.2 %local_grads.3 = (bf16[4,304,384]{2,1,0:T(8,128)(2,1)}, bf16[4,304,384]{2,1,0:T(8,128)(2,1)}) custom-call(s32[1]{0:T(128)} %bitcast.2.me_ref, bf16[1024,768]{1,0:T(8,128)(2,1)} %bitcast.194, bf16[1024,384]{1,0:T(8,128)(2,1)} %get-tuple-element.138.refs_3_.refs_0_, bf16[1024,384]{1,0:T(8,128)(2,1)} %get-tuple-element.144.refs_4_.refs_1_, ...), custom_call_target="tpu_custom_call" | custom-call | flops 20000000000 | bytes 1048576 | tf_op jit(solution)/shard_map/local_grads/pallas_call | solution.py:336
  286.3 13.8 %collective-permute-done.16.refs_2_ = bf16[256,768]{1,0:T(8,128)(2,1)S(1)} collective-permute-done((bf16[256,768]{1,0:T(8,128)(2,1)}, bf16[256,768]{1,0:T(8,128)(2,1)S(1)}, u32[]{:S(2)}, u32[]{:S(2)}) %collective-permute-start.16) | collective-permute-done | bytes 393248 | tf_op jit(solution)/shard_map/ppermute | solution.py:506
  300.8 1.6 convert_add_fusion
  302.5 2.8 collective-permute-done.14
  305.3 1.2 bitcast_add_fusion
  306.5 2.2 fusion.19
  308.7 1.9 fusion.16
  310.6 1.3 add_convert_fusion.2
  313.9 2.1 collective-permute-start.19
  316.0 1.3 collective-permute-start.22
  317.4 12.1 %collective-permute-done.22 = bf16[192,768]{1,0:T(8,128)(2,1)} collective-permute-done((bf16[192,768]{1,0:T(8,128)(2,1)S(1)}, bf16[192,768]{1,0:T(8,128)(2,1)}, u32[]{:S(2)}, u32[]{:S(2)}) %collective-permute-start.22) | collective-permute-done | bytes 294944 | tf_op jit(solution)/shard_map/ppermute | solution.py:506
  329.5 2.6 collective-permute-done.18
  332.0 1.3 fusion.6
  333.3 1.2 fusion.8
  334.7 1.6 collective-permute-start.25
  337.3 2.0 collective-permute-start.24
  340.3 2.0 collective-permute-start.23
  342.3 3.0 collect.2
  345.4 1.2 collective-permute-done.23
  346.6 2.1 collective-permute-done.24
  351.3 2.7 collective-permute-start.28
  354.1 1.9 fusion.14
  358.0 2.1 collective-permute-start.26
  360.1 3.0 collect.3
  363.1 8.2 %collective-permute-done.27 = bf16[2,76,384]{2,1,0:T(8,128)(2,1)S(1)} collective-permute-done((bf16[2,76,384]{2,1,0:T(8,128)(2,1)}, bf16[2,76,384]{2,1,0:T(8,128)(2,1)S(1)}, u32[]{:S(2)}, u32[]{:S(2)}) %collective-permute-start.27) | collective-permute-done | bytes 116768 | tf_op jit(solution)/shard_map/ppermute | solution.py:506
  371.6 3.5 collective-permute-start.30
  377.7 6.2 %collective-permute-done.29 = bf16[264,384]{1,0:T(8,128)(2,1)S(1)} collective-permute-done((bf16[264,384]{1,0:T(8,128)(2,1)S(1)}, bf16[264,384]{1,0:T(8,128)(2,1)S(1)}, u32[]{:S(2)}, u32[]{:S(2)}) %collective-permute-start.29) | collective-permute-done | bytes 202784 | tf_op jit(solution)/shard_map/ppermute | solution.py:506
  384.2 2.9 collective-permute-start.32
  387.1 1.2 fusion.35
  389.0 1.2 copy.52
  390.2 1.3 collective-permute-done.32
  391.5 2.5 collective-permute-done.31
  397.5 2.0 collective-permute-done.33
  (186 shorter events, 35.9 us)
Async XLA Ops:
  7.2 22.2 %copy-start = (s32[4,4]{1,0:T(4,128)S(1)}, s32[4,4]{1,0:T(4,128)}, u32[]{:S(2)}) copy-start(s32[4,4]{1,0:T(4,128)} %param.15) | copy-start | bytes 196
  7.2 97.3 %all-gather.3.cloned.1.call-start = ((), (), s32[]{:S(2)}) async-start(), calls=%async_computation.4 | async-start | bytes 15925248 | tf_op jit(solution)/shard_map/all_gather | solution.py:670
  12.0 42.3 %copy-start.16 = (bf16[304,768]{1,0:T(8,128)(2,1)}, bf16[304,768]{1,0:T(8,128)(2,1)S(1)}, u32[]{:S(2)}) copy-start(bf16[304,768]{1,0:T(8,128)(2,1)S(1)} %fusion.12.refs_0_.refs_6_) | copy-start | bytes 1400836
  12.1 16.0 %collective-permute-start.1 = (bf16[304,768]{1,0:T(8,128)(2,1)S(1)}, bf16[304,768]{1,0:T(8,128)(2,1)S(1)}, u32[]{:S(2)}, u32[]{:S(2)}) collective-permute-start(bf16[304,768]{1,0:T(8,128)(2,1)S(1)} %fusion.12.refs_0_.refs_6_), channel_id=1, source_target_pairs={{0,8},{4,12},{8,0},{12,4},{16,24},{20,28},{24,16},{28,20},{1,9},{5... | collective-permute-start | bytes 1400840 | tf_op jit(solution)/shard_map/ppermute | solution.py:506
  15.1 15.4 %collective-permute-start.3 = (bf16[304,768]{1,0:T(8,128)(2,1)S(1)}, bf16[304,768]{1,0:T(8,128)(2,1)S(1)}, u32[]{:S(2)}, u32[]{:S(2)}) collective-permute-start(bf16[304,768]{1,0:T(8,128)(2,1)S(1)} %fusion.12.refs_0_.refs_6_), channel_id=1, source_target_pairs={{0,16},{4,20},{8,24},{12,28},{16,0},{20,4},{24,8},{28,12},{1,17},{... | collective-permute-start | bytes 1400840 | tf_op jit(solution)/shard_map/ppermute | solution.py:506
  16.6 13.9 %collective-permute-start = (bf16[304,768]{1,0:T(8,128)(2,1)S(1)}, bf16[304,768]{1,0:T(8,128)(2,1)S(1)}, u32[]{:S(2)}, u32[]{:S(2)}) collective-permute-start(bf16[304,768]{1,0:T(8,128)(2,1)S(1)} %fusion.12.refs_0_.refs_6_), channel_id=1, source_target_pairs={{0,4},{4,0},{8,12},{12,8},{16,20},{20,16},{24,28},{28,24},{1,5},{5... | collective-permute-start | bytes 1400840 | tf_op jit(solution)/shard_map/ppermute | solution.py:506
  16.6 42.5 %all-to-all-start = ((bf16[4,256,768]{2,1,0:T(8,128)(2,1)}), bf16[4,256,768]{2,1,0:T(8,128)(2,1)S(1)}, u32[]{:S(2)}, u32[]{:S(2)}) async-start(bf16[4,256,768]{2,1,0:T(8,128)(2,1)} %param.14), calls=%async_computation | async-start | bytes 3145728 | tf_op jit(solution)/shard_map/all_to_all | solution.py:637
  28.0 31.1 %copy-start.25 = (bf16[304,768]{1,0:T(8,128)(2,1)}, bf16[304,768]{1,0:T(8,128)(2,1)S(1)}, u32[]{:S(2)}) copy-start(bf16[304,768]{1,0:T(8,128)(2,1)S(1)} %collective-permute-done.1.refs_2_.refs_8_) | copy-start | bytes 1400836
  28.0 23.5 %collective-permute-start.2 = (bf16[304,768]{1,0:T(8,128)(2,1)S(1)}, bf16[304,768]{1,0:T(8,128)(2,1)}, u32[]{:S(2)}, u32[]{:S(2)}) collective-permute-start(bf16[304,768]{1,0:T(8,128)(2,1)S(1)} %collective-permute-done.1.refs_2_.refs_8_), channel_id=1, source_target_pairs={{0,4},{4,0},{8,12},{12,8},{16,20},{20,16},{24,28},{28,24},{1,5},{5... | collective-permute-start | bytes 1400840 | tf_op jit(solution)/shard_map/ppermute | solution.py:506
  28.0 23.5 %collective-permute-start.5 = (bf16[304,768]{1,0:T(8,128)(2,1)S(1)}, bf16[304,768]{1,0:T(8,128)(2,1)}, u32[]{:S(2)}, u32[]{:S(2)}) collective-permute-start(bf16[304,768]{1,0:T(8,128)(2,1)S(1)} %collective-permute-done.1.refs_2_.refs_8_), channel_id=1, source_target_pairs={{0,16},{4,20},{8,24},{12,28},{16,0},{20,4},{24,8},{28,12},{1,17},{... | collective-permute-start | bytes 1400840 | tf_op jit(solution)/shard_map/ppermute | solution.py:506
  30.4 28.6 %copy-start.26 = (bf16[304,768]{1,0:T(8,128)(2,1)}, bf16[304,768]{1,0:T(8,128)(2,1)S(1)}, u32[]{:S(2)}) copy-start(bf16[304,768]{1,0:T(8,128)(2,1)S(1)} %collective-permute-done.3.refs_4_.refs_10_) | copy-start | bytes 1400836
  30.4 21.8 %collective-permute-start.4 = (bf16[304,768]{1,0:T(8,128)(2,1)S(1)}, bf16[304,768]{1,0:T(8,128)(2,1)S(1)}, u32[]{:S(2)}, u32[]{:S(2)}) collective-permute-start(bf16[304,768]{1,0:T(8,128)(2,1)S(1)} %collective-permute-done.3.refs_4_.refs_10_), channel_id=1, source_target_pairs={{0,4},{4,0},{8,12},{12,8},{16,20},{20,16},{24,28},{28,24},{1,5},{5... | collective-permute-start | bytes 1400840 | tf_op jit(solution)/shard_map/ppermute | solution.py:506
  30.5 28.6 %copy-start.27 = (bf16[304,768]{1,0:T(8,128)(2,1)}, bf16[304,768]{1,0:T(8,128)(2,1)S(1)}, u32[]{:S(2)}) copy-start(bf16[304,768]{1,0:T(8,128)(2,1)S(1)} %collective-permute-done.refs_1_.refs_7_) | copy-start | bytes 1400836
  51.5 2.0 collective-permute-start.6
  52.2 1.3 copy-start.28
  59.1 3.6 copy-start.10
  59.1 51.9 %all-to-all-start.1 = ((bf16[4,256,768]{2,1,0:T(8,128)(2,1)}), bf16[4,256,768]{2,1,0:T(8,128)(2,1)S(1)}, u32[]{:S(2)}, u32[]{:S(2)}) async-start(bf16[4,256,768]{2,1,0:T(8,128)(2,1)} %param.25), calls=%async_computation.1 | async-start | bytes 3145728 | tf_op jit(solution)/shard_map/all_to_all | solution.py:637
  62.7 211.1 %reduce-scatter.2.cloned.1.call-start = ((), (), s32[]{:S(2)}) async-start(), calls=%async_computation.3 | async-start | bytes 10616832 | tf_op jit(solution)/shard_map/reduce_scatter | solution.py:704
  171.6 20.5 %copy-start.36 = (bf16[256,768]{1,0:T(8,128)(2,1)S(1)}, bf16[256,768]{1,0:T(8,128)(2,1)}, u32[]{:S(2)}) copy-start(bf16[256,768]{1,0:T(8,128)(2,1)} %get-tuple-element.122) | copy-start | bytes 1179652
  171.6 22.8 %copy-start.35 = (bf16[256,768]{1,0:T(8,128)(2,1)S(1)}, bf16[256,768]{1,0:T(8,128)(2,1)}, u32[]{:S(2)}) copy-start(bf16[256,768]{1,0:T(8,128)(2,1)} %get-tuple-element.123) | copy-start | bytes 1179652
  190.2 52.3 %collective-permute-start.10 = (bf16[4,576,384]{2,1,0:T(8,128)(2,1)}, bf16[4,576,384]{2,1,0:T(8,128)(2,1)S(1)}, u32[]{:S(2)}, u32[]{:S(2)}) collective-permute-start(bf16[4,576,384]{2,1,0:T(8,128)(2,1)} %get-tuple-element.118), channel_id=1, source_target_pairs={{0,4},{4,0},{8,12},{12,8},{16,20},{20,16},{24,28},{28,24},{1,5},{5... | collective-permute-start | bytes 5308424 | tf_op jit(solution)/shard_map/ppermute | solution.py:506
  190.5 29.6 %collective-permute-start.7 = (bf16[256,768]{1,0:T(8,128)(2,1)}, bf16[256,768]{1,0:T(8,128)(2,1)S(1)}, u32[]{:S(2)}, u32[]{:S(2)}) collective-permute-start(bf16[256,768]{1,0:T(8,128)(2,1)} %get-tuple-element.121), channel_id=1, source_target_pairs={{0,1},{1,0},{2,3},{3,2},{4,5},{5,4},{6,7},{7,6},{8,9},{9,8},{10,11... | collective-permute-start | bytes 1179656 | tf_op jit(solution)/shard_map/ppermute | solution.py:506
  192.0 29.7 %collective-permute-start.8 = (bf16[256,768]{1,0:T(8,128)(2,1)S(1)}, bf16[256,768]{1,0:T(8,128)(2,1)S(1)}, u32[]{:S(2)}, u32[]{:S(2)}) collective-permute-start(bf16[256,768]{1,0:T(8,128)(2,1)S(1)} %copy-done.36), channel_id=1, source_target_pairs={{0,2},{1,3},{2,0},{3,1},{4,6},{5,7},{6,4},{7,5},{8,10},{9,11},{10,... | collective-permute-start | bytes 1179656 | tf_op jit(solution)/shard_map/ppermute | solution.py:506
  194.4 27.3 %collective-permute-start.9 = (bf16[256,768]{1,0:T(8,128)(2,1)S(1)}, bf16[256,768]{1,0:T(8,128)(2,1)S(1)}, u32[]{:S(2)}, u32[]{:S(2)}) collective-permute-start(bf16[256,768]{1,0:T(8,128)(2,1)S(1)} %copy-done.35), channel_id=1, source_target_pairs={{0,3},{1,2},{2,1},{3,0},{4,7},{5,6},{6,5},{7,4},{8,11},{9,10},{10,... | collective-permute-start | bytes 1179656 | tf_op jit(solution)/shard_map/ppermute | solution.py:506
  220.0 22.4 %collective-permute-start.11 = (bf16[4,480,384]{2,1,0:T(8,128)(2,1)}, bf16[4,480,384]{2,1,0:T(8,128)(2,1)}, u32[]{:S(2)}, u32[]{:S(2)}) collective-permute-start(bf16[4,480,384]{2,1,0:T(8,128)(2,1)} %get-tuple-element.130), channel_id=1, source_target_pairs={{0,4},{4,0},{8,12},{12,8},{16,20},{20,16},{24,28},{28,24},{1,5},{5... | collective-permute-start | bytes 4423688 | tf_op jit(solution)/shard_map/ppermute | solution.py:506
  220.1 1.6 copy-start.30
  223.3 19.2 %copy-start.8 = (bf16[4,576,384]{2,1,0:T(8,128)(2,1)S(1)}, bf16[4,576,384]{2,1,0:T(8,128)(2,1)}, u32[]{:S(2)}) copy-start(bf16[4,576,384]{2,1,0:T(8,128)(2,1)} %get-tuple-element.135) | copy-start | bytes 5308420
  242.4 2.3 copy-start.14
  242.5 5.4 %copy-start.9 = (bf16[4,576,384]{2,1,0:T(8,128)(2,1)}, bf16[4,576,384]{2,1,0:T(8,128)(2,1)S(1)}, u32[]{:S(2)}) copy-start(bf16[4,576,384]{2,1,0:T(8,128)(2,1)S(1)} %collective-permute-done.10) | copy-start | bytes 5308420
  247.9 19.0 %copy-start.20 = (f32[1,3072]{1,0:T(1,128)S(1)}, f32[1,3072]{1,0:T(1,128)}, u32[]{:S(2)}) copy-start(f32[1,3072]{1,0:T(1,128)} %get-tuple-element.156) | copy-start | bytes 36868
  247.9 24.5 %copy-start.18 = (f32[16,768]{1,0:T(8,128)S(1)}, f32[16,768]{1,0:T(8,128)}, u32[]{:S(2)}) copy-start(f32[16,768]{1,0:T(8,128)} %get-tuple-element.153) | copy-start | bytes 147460
  247.9 24.5 %copy-start.19 = (f32[16,768]{1,0:T(8,128)S(1)}, f32[16,768]{1,0:T(8,128)}, u32[]{:S(2)}) copy-start(f32[16,768]{1,0:T(8,128)} %get-tuple-element.154) | copy-start | bytes 147460
  259.0 21.1 %collective-permute-start.15 = (bf16[256,768]{1,0:T(8,128)(2,1)}, bf16[256,768]{1,0:T(8,128)(2,1)S(1)}, u32[]{:S(2)}, u32[]{:S(2)}) collective-permute-start(bf16[256,768]{1,0:T(8,128)(2,1)} %get-tuple-element.147), channel_id=1, source_target_pairs={{0,1},{1,0},{2,3},{3,2},{4,5},{5,4},{6,7},{7,6},{8,9},{9,8},{10,11... | collective-permute-start | bytes 1179656 | tf_op jit(solution)/shard_map/ppermute | solution.py:506
  267.7 34.8 %collective-permute-start.13 = (bf16[2,480,384]{2,1,0:T(8,128)(2,1)}, bf16[2,480,384]{2,1,0:T(8,128)(2,1)}, u32[]{:S(2)}, u32[]{:S(2)}) collective-permute-start(bf16[2,480,384]{2,1,0:T(8,128)(2,1)} %get-tuple-element.182), channel_id=1, source_target_pairs={{0,16},{4,20},{8,24},{12,28},{16,0},{20,4},{24,8},{28,12},{1,17},{... | collective-permute-start | bytes 2211848 | tf_op jit(solution)/shard_map/ppermute | solution.py:506
  268.7 33.7 %collective-permute-start.12 = (bf16[2,576,384]{2,1,0:T(8,128)(2,1)}, bf16[2,576,384]{2,1,0:T(8,128)(2,1)}, u32[]{:S(2)}, u32[]{:S(2)}) collective-permute-start(bf16[2,576,384]{2,1,0:T(8,128)(2,1)} %fusion.1), channel_id=1, source_target_pairs={{0,8},{4,12},{8,0},{12,4},{16,24},{20,28},{24,16},{28,20},{1,9},{5... | collective-permute-start | bytes 2654216 | tf_op jit(solution)/shard_map/ppermute | solution.py:506
  270.0 30.1 %collective-permute-start.16 = (bf16[256,768]{1,0:T(8,128)(2,1)}, bf16[256,768]{1,0:T(8,128)(2,1)S(1)}, u32[]{:S(2)}, u32[]{:S(2)}) collective-permute-start(bf16[256,768]{1,0:T(8,128)(2,1)} %get-tuple-element.148), channel_id=1, source_target_pairs={{0,2},{1,3},{2,0},{3,1},{4,6},{5,7},{6,4},{7,5},{8,10},{9,11},{10,... | collective-permute-start | bytes 1179656 | tf_op jit(solution)/shard_map/ppermute | solution.py:506
  270.9 31.5 %collective-permute-start.17 = (bf16[256,768]{1,0:T(8,128)(2,1)}, bf16[256,768]{1,0:T(8,128)(2,1)}, u32[]{:S(2)}, u32[]{:S(2)}) collective-permute-start(bf16[256,768]{1,0:T(8,128)(2,1)} %get-tuple-element.149), channel_id=1, source_target_pairs={{0,3},{1,2},{2,1},{3,0},{4,7},{5,6},{6,5},{7,4},{8,11},{9,10},{10,... | collective-permute-start | bytes 1179656 | tf_op jit(solution)/shard_map/ppermute | solution.py:506
  280.1 6.2 %copy-start.33 = (bf16[256,768]{1,0:T(8,128)(2,1)}, bf16[256,768]{1,0:T(8,128)(2,1)S(1)}, u32[]{:S(2)}) copy-start(bf16[256,768]{1,0:T(8,128)(2,1)S(1)} %collective-permute-done.15.refs_1_) | copy-start | bytes 1179652
  280.1 25.2 %collective-permute-start.14 = (bf16[2,192,768]{2,1,0:T(8,128)(2,1)}, bf16[2,192,768]{2,1,0:T(8,128)(2,1)}, u32[]{:S(2)}, u32[]{:S(2)}) collective-permute-start(bf16[2,192,768]{2,1,0:T(8,128)(2,1)} %fusion.10), channel_id=1, source_target_pairs={{0,1},{1,0},{2,3},{3,2},{4,5},{5,4},{6,7},{7,6},{8,9},{9,8},{10,11... | collective-permute-start | bytes 1769480 | tf_op jit(solution)/shard_map/ppermute | solution.py:506
  300.8 9.8 %collective-permute-start.20 = (bf16[4,304,384]{2,1,0:T(8,128)(2,1)}, bf16[4,304,384]{2,1,0:T(8,128)(2,1)S(1)}, u32[]{:S(2)}, u32[]{:S(2)}) collective-permute-start(bf16[4,304,384]{2,1,0:T(8,128)(2,1)} %get-tuple-element.157), channel_id=1, source_target_pairs={{0,4},{4,0},{8,12},{12,8},{16,20},{20,16},{24,28},{28,24},{1,5},{5... | collective-permute-start | bytes 2801672 | tf_op jit(solution)/shard_map/ppermute | solution.py:506
  302.4 4.1 %copy-start.3 = (f32[2,480,384]{2,1,0:T(8,128)S(1)}, f32[2,480,384]{2,1,0:T(8,128)}, u32[]{:S(2)}) copy-start(f32[2,480,384]{2,1,0:T(8,128)} %get-tuple-element.181) | copy-start | bytes 4423684
  306.5 4.1 %copy-start.6 = (f32[2,192,768]{2,1,0:T(8,128)}, f32[2,192,768]{2,1,0:T(8,128)S(1)}, u32[]{:S(2)}) copy-start(f32[2,192,768]{2,1,0:T(8,128)S(1)} %bitcast_add_fusion) | copy-start | bytes 3538948
  306.5 4.0 copy-start.15
  311.8 21.5 %copy-start.4 = (f32[2,480,384]{2,1,0:T(8,128)S(1)}, f32[2,480,384]{2,1,0:T(8,128)}, u32[]{:S(2)}) copy-start(f32[2,480,384]{2,1,0:T(8,128)} %get-tuple-element.181) | copy-start | bytes 4423684
  311.9 20.2 %collective-permute-start.21 = (bf16[2,304,384]{2,1,0:T(8,128)(2,1)}, bf16[2,304,384]{2,1,0:T(8,128)(2,1)}, u32[]{:S(2)}, u32[]{:S(2)}) collective-permute-start(bf16[2,304,384]{2,1,0:T(8,128)(2,1)} %get-tuple-element.185), channel_id=1, source_target_pairs={{0,16},{4,20},{8,24},{12,28},{16,0},{20,4},{24,8},{28,12},{1,17},{... | collective-permute-start | bytes 1400840 | tf_op jit(solution)/shard_map/ppermute | solution.py:506
  312.8 19.2 %collective-permute-start.18 = (bf16[576,384]{1,0:T(8,128)(2,1)}, bf16[576,384]{1,0:T(8,128)(2,1)}, u32[]{:S(2)}, u32[]{:S(2)}) collective-permute-start(bf16[576,384]{1,0:T(8,128)(2,1)} %fusion.16), channel_id=1, source_target_pairs={{0,16},{4,20},{8,24},{12,28},{16,0},{20,4},{24,8},{28,12},{1,17},{... | collective-permute-start | bytes 1327112 | tf_op jit(solution)/shard_map/ppermute | solution.py:506
  313.9 15.6 %collective-permute-start.19 = (bf16[480,384]{1,0:T(8,128)(2,1)}, bf16[480,384]{1,0:T(8,128)(2,1)}, u32[]{:S(2)}, u32[]{:S(2)}) collective-permute-start(bf16[480,384]{1,0:T(8,128)(2,1)} %fusion.19), channel_id=1, source_target_pairs={{0,8},{4,12},{8,0},{12,4},{16,24},{20,28},{24,16},{28,20},{1,9},{5... | collective-permute-start | bytes 1105928 | tf_op jit(solution)/shard_map/ppermute | solution.py:506
  316.0 13.5 %collective-permute-start.22 = (bf16[192,768]{1,0:T(8,128)(2,1)S(1)}, bf16[192,768]{1,0:T(8,128)(2,1)}, u32[]{:S(2)}, u32[]{:S(2)}) collective-permute-start(bf16[192,768]{1,0:T(8,128)(2,1)S(1)} %fusion.20), channel_id=1, source_target_pairs={{0,2},{1,3},{2,0},{3,1},{4,6},{5,7},{6,4},{7,5},{8,10},{9,11},{10,... | collective-permute-start | bytes 884744 | tf_op jit(solution)/shard_map/ppermute | solution.py:506
  334.5 1.8 copy-start.7
  334.7 4.7 %copy-start.5 = (f32[2,304,384]{2,1,0:T(8,128)S(1)}, f32[2,304,384]{2,1,0:T(8,128)}, u32[]{:S(2)}) copy-start(f32[2,304,384]{2,1,0:T(8,128)} %get-tuple-element.186) | copy-start | bytes 2801668
  334.7 14.7 %collective-permute-start.25 = (bf16[2,264,384]{2,1,0:T(8,128)(2,1)S(1)}, bf16[2,264,384]{2,1,0:T(8,128)(2,1)S(1)}, u32[]{:S(2)}, u32[]{:S(2)}) collective-permute-start(bf16[2,264,384]{2,1,0:T(8,128)(2,1)S(1)} %fusion.17), channel_id=1, source_target_pairs={{0,1},{1,0},{2,3},{3,2},{4,5},{5,4},{6,7},{7,6},{8,9},{9,8},{10,11... | collective-permute-start | bytes 1216520 | tf_op jit(solution)/shard_map/ppermute | solution.py:506
  337.3 11.3 %collective-permute-start.24 = (bf16[192,768]{1,0:T(8,128)(2,1)S(1)}, bf16[192,768]{1,0:T(8,128)(2,1)}, u32[]{:S(2)}, u32[]{:S(2)}) collective-permute-start(bf16[192,768]{1,0:T(8,128)(2,1)S(1)} %fusion.11), channel_id=1, source_target_pairs={{0,2},{1,3},{2,0},{3,1},{4,6},{5,7},{6,4},{7,5},{8,10},{9,11},{10,... | collective-permute-start | bytes 884744 | tf_op jit(solution)/shard_map/ppermute | solution.py:506
  340.3 6.2 %collective-permute-start.23 = (bf16[304,384]{1,0:T(8,128)(2,1)S(1)}, bf16[304,384]{1,0:T(8,128)(2,1)}, u32[]{:S(2)}, u32[]{:S(2)}) collective-permute-start(bf16[304,384]{1,0:T(8,128)(2,1)S(1)} %fusion.21), channel_id=1, source_target_pairs={{0,8},{4,12},{8,0},{12,4},{16,24},{20,28},{24,16},{28,20},{1,9},{5... | collective-permute-start | bytes 700424 | tf_op jit(solution)/shard_map/ppermute | solution.py:506
  351.3 20.2 %collective-permute-start.28 = (bf16[2,192,768]{2,1,0:T(8,128)(2,1)}, bf16[2,192,768]{2,1,0:T(8,128)(2,1)}, u32[]{:S(2)}, u32[]{:S(2)}) collective-permute-start(bf16[2,192,768]{2,1,0:T(8,128)(2,1)} %pad_maximum_fusion.4), channel_id=1, source_target_pairs={{0,1},{1,0},{2,3},{3,2},{4,5},{5,4},{6,7},{7,6},{8,9},{9,8},{10,11... | collective-permute-start | bytes 1769480 | tf_op jit(solution)/shard_map/ppermute | solution.py:506
  357.8 13.5 %collective-permute-start.27 = (bf16[2,76,384]{2,1,0:T(8,128)(2,1)}, bf16[2,76,384]{2,1,0:T(8,128)(2,1)S(1)}, u32[]{:S(2)}, u32[]{:S(2)}) collective-permute-start(bf16[2,76,384]{2,1,0:T(8,128)(2,1)} %fusion.23), channel_id=1, source_target_pairs={{0,1},{1,0},{2,3},{3,2},{4,5},{5,4},{6,7},{7,6},{8,9},{9,8},{10,11... | collective-permute-start | bytes 350216 | tf_op jit(solution)/shard_map/ppermute | solution.py:506
  358.0 13.6 %copy-start.13 = (f32[2,2,76,384]{3,2,1,0:T(8,128)S(1)}, f32[2,2,76,384]{3,2,1,0:T(8,128)}, u32[]{:S(2)}) copy-start(f32[2,2,76,384]{3,2,1,0:T(8,128)} %copy-done.12) | copy-start | bytes 1400836
  358.0 13.6 %collective-permute-start.26 = (bf16[264,384]{1,0:T(8,128)(2,1)S(1)}, bf16[264,384]{1,0:T(8,128)(2,1)S(1)}, u32[]{:S(2)}, u32[]{:S(2)}) collective-permute-start(bf16[264,384]{1,0:T(8,128)(2,1)S(1)} %fusion.22), channel_id=1, source_target_pairs={{0,2},{1,3},{2,0},{3,1},{4,6},{5,7},{6,4},{7,5},{8,10},{9,11},{10,... | collective-permute-start | bytes 608264 | tf_op jit(solution)/shard_map/ppermute | solution.py:506
  371.6 6.1 %collective-permute-start.30 = (bf16[76,384]{1,0:T(8,128)(2,1)S(1)}, bf16[76,384]{1,0:T(8,128)(2,1)S(1)}, u32[]{:S(2)}, u32[]{:S(2)}) collective-permute-start(bf16[76,384]{1,0:T(8,128)(2,1)S(1)} %fusion.25), channel_id=1, source_target_pairs={{0,2},{1,3},{2,0},{3,1},{4,6},{5,7},{6,4},{7,5},{8,10},{9,11},{10,... | collective-permute-start | bytes 175112 | tf_op jit(solution)/shard_map/ppermute | solution.py:506
  375.2 8.8 %collective-permute-start.29 = (bf16[264,384]{1,0:T(8,128)(2,1)S(1)}, bf16[264,384]{1,0:T(8,128)(2,1)S(1)}, u32[]{:S(2)}, u32[]{:S(2)}) collective-permute-start(bf16[264,384]{1,0:T(8,128)(2,1)S(1)} %fusion.18), channel_id=1, source_target_pairs={{0,2},{1,3},{2,0},{3,1},{4,6},{5,7},{6,4},{7,5},{8,10},{9,11},{10,... | collective-permute-start | bytes 608264 | tf_op jit(solution)/shard_map/ppermute | solution.py:506
  384.0 9.9 %collective-permute-start.31 = (bf16[2,264,384]{2,1,0:T(8,128)(2,1)S(1)}, bf16[2,264,384]{2,1,0:T(8,128)(2,1)S(1)}, u32[]{:S(2)}, u32[]{:S(2)}) collective-permute-start(bf16[2,264,384]{2,1,0:T(8,128)(2,1)S(1)} %pad_maximum_fusion.5), channel_id=1, source_target_pairs={{0,1},{1,0},{2,3},{3,2},{4,5},{5,4},{6,7},{7,6},{8,9},{9,8},{10,11... | collective-permute-start | bytes 1216520 | tf_op jit(solution)/shard_map/ppermute | solution.py:506
  384.2 7.4 %collective-permute-start.32 = (bf16[76,384]{1,0:T(8,128)(2,1)S(1)}, bf16[76,384]{1,0:T(8,128)(2,1)S(1)}, u32[]{:S(2)}, u32[]{:S(2)}) collective-permute-start(bf16[76,384]{1,0:T(8,128)(2,1)S(1)} %fusion.24), channel_id=1, source_target_pairs={{0,2},{1,3},{2,0},{3,1},{4,6},{5,7},{6,4},{7,5},{8,10},{9,11},{10,... | collective-permute-start | bytes 175112 | tf_op jit(solution)/shard_map/ppermute | solution.py:506
  394.5 4.9 %collective-permute-start.33 = (bf16[2,76,384]{2,1,0:T(8,128)(2,1)S(1)}, bf16[2,76,384]{2,1,0:T(8,128)(2,1)S(1)}, u32[]{:S(2)}, u32[]{:S(2)}) collective-permute-start(bf16[2,76,384]{2,1,0:T(8,128)(2,1)S(1)} %pad_maximum_fusion.6), channel_id=1, source_target_pairs={{0,1},{1,0},{2,3},{3,2},{4,5},{5,4},{6,7},{7,6},{8,9},{9,8},{10,11... | collective-permute-start | bytes 350216 | tf_op jit(solution)/shard_map/ppermute | solution.py:506
  397.5 4.0 slice-start
  399.5 3.0 copy-start.1
  (12 other events, 10.3 us)
Sparse Core Ops, SparseCore 0:
  11.1 93.3 all-gather.2
  171.7 76.4 reduce-scatter.1
where the time goes:
time: 418 us; the launch traced here: 410 us
  Pallas kernels  187 us (45%)
  waiting for transfers between devices  101 us (24%)
  starting transfers between devices  54.6 us (13%)
  other arithmetic  29.9 us (7%)
  local copies, waits for them, and re-layouts  22.5 us (5%)
  between operations  15.2 us (4%)
    ppermute x34, waiting for transfers between devices, flip(): lax.ppermute(value, axis, [(index, index ^ bit) for index in range(count)])  91.1 us
    pallas_call x1, Pallas kernels, layer(): pl.pallas_call(body, grid=(steps,), in_specs=[SMEM, full(pos.shape), blk(...  59.3 us
    ppermute x34, starting transfers between devices, flip(): lax.ppermute(value, axis, [(index, index ^ bit) for index in range(count)])  46 us
    pallas_call x2, Pallas kernels, attn_bwd(): pl.pallas_call(bwd_kernel, grid=(pairs,), in_specs=[pl.BlockSpec((16, 1),...  38.2 us
    pallas_call x1, Pallas kernels, attn_fwd(): pl.pallas_call(fwd_kernel, grid=(pairs,), in_specs=[pl.BlockSpec((16, 1),...  25.8 us
    pallas_call x1, Pallas kernels, globals_bwd(): pl.pallas_call(body, in_specs=[SMEM] + [vm] * 12 + [ANY] * w, out_specs=[...  18.6 us
    pallas_call x2, Pallas kernels, local_grads(): pl.pallas_call(body, in_specs=[SMEM] + [vm] * (first - 1) + [ANY] * (0 if...  12.3 us
    pallas_call x1, Pallas kernels, inputs_back(): pl.pallas_call(body, grid=(length // RB,), in_specs=[SMEM, SMEM, blk] + [...  11.1 us
  transfers between devices with their start and end apart: 38, of which 22 were waited for; matrix products, arithmetic and copies ran while one was open for 8% of the time, Pallas kernels for 31%

commit v1 on v0

--- a/solution.py
+++ b/solution.py
@@ -62,12 +62,17 @@
     val_far_t=dot_nn(sel,v_ref[...]).astype(BF).T
     val_t=v_ref[...].T
     low_ok,high_ok=edge_masks()
+    def products(start):
+        lo,hi=key_range(start,length)
+        qq=split_pair(q_ref[start:start+QB,:])
+        return dot_nt(k_ref[lo:hi,:],qq),dot_nt(key_far,qq)
+    ahead=products(0)
     for start in range(0,length,QB):
         lo,hi=key_range(start,length)
-        qq=split_pair(q_ref[start:start+QB,:])
-        raw=dot_nt(k_ref[lo:hi,:],qq)
+        raw,raw_far=ahead
+        if start+QB<length: ahead=products(start+QB)
         parts=masked_scores(raw,start,length,low_ok,high_ok)
-        far=jnp.where(far_mask(pos,start),dot_nt(key_far,qq),NEG)
+        far=jnp.where(far_mask(pos,start),raw_far,NEG)
         top=jnp.max(far,axis=0,keepdims=True)
         for part in parts: top=jnp.maximum(top,jnp.max(part,axis=0,keepdims=True))
         far_p=jnp.exp(far-top)
@@ -119,31 +124,34 @@
     dv_acc[...]=jnp.zeros_like(dv_acc)
     dk_far=jnp.zeros((16,128),F32); dv_far=jnp.zeros((16,128),F32)
     low_ok,high_ok=edge_masks()
-    for start in range(0,length,QB):
+    def products(start):
         lo,hi=key_range(start,length)
         qq=split_pair(q_ref[start:start+QB,:])
         gg=split_pair(grad_scr[start:start+QB,:])
+        raw=dot_nt(jnp.concatenate([k_ref[lo:hi,:],key_far],axis=0),qq)
+        dp=dot_nt(jnp.concatenate([v_ref[lo:hi,:],val_far],axis=0),gg)
+        return qq,gg,raw[:hi-lo],dp[:hi-lo],raw[hi-lo:],dp[hi-lo:]
+    ahead=products(0)
+    for start in range(0,length,QB):
+        lo,hi=key_range(start,length)
+        qq,gg,raw,dp_all,raw_far,dp_far=ahead
+        if start+QB<length: ahead=products(start+QB)
         lse=jnp.concatenate([lse_ref[0,0:1,start:start+QB],lse_ref[0,1:2,start:start+QB]],axis=1)
         delta=jnp.concatenate([delta_all[0:1,start:start+QB],delta_all[1:2,start:start+QB]],axis=1)
-        dq_t=jnp.zeros((128,2*QB),F32)
-        def one(scores,vals):
+        def one(scores,dp):
             p=jnp.exp(scores-lse)
-            dp=dot_nt(vals,gg)
             return p.astype(BF),(p*(dp-delta)).astype(BF)
-        far=jnp.where(far_mask(pos,start),dot_nt(key_far,qq),NEG)
-        p,ds=one(far,val_far)
-        dv_far=dv_far+dot_nn(p,gg); dk_far=dk_far+dot_nn(ds,qq)
-        dq_t=dq_t+dot_nn(key_far_t,ds)
-        parts=masked_scores(dot_nt(k_ref[lo:hi,:],qq),start,length,low_ok,high_ok)
-        plist=[];dlist=[]
-        for n,part in enumerate(parts):
-            a=lo+n*QB
-            p,ds=one(part,v_ref[a:a+QB,:])
-            plist.append(p);dlist.append(ds)
-        p=jnp.concatenate(plist,axis=0); ds=jnp.concatenate(dlist,axis=0)
-        dv_acc[lo:hi,:]+=dot_nn(p,gg)
-        dk_acc[lo:hi,:]+=dot_nn(ds,qq)
-        dq_t=dq_t+dot_nn(key_t[:,lo:hi],ds)
+        far=jnp.where(far_mask(pos,start),raw_far,NEG)
+        p_far,ds_far=one(far,dp_far)
+        parts=masked_scores(raw,start,length,low_ok,high_ok)
+        both=[one(part,dp_all[n*QB:(n+1)*QB]) for n,part in enumerate(parts)]
+        p=jnp.concatenate([pair[0] for pair in both]+[p_far],axis=0)
+        ds=jnp.concatenate([pair[1] for pair in both]+[ds_far],axis=0)
+        dv_all,dk_all=dot_nn(p,gg),dot_nn(ds,qq)
+        dv_acc[lo:hi,:]+=dv_all[:hi-lo]
+        dk_acc[lo:hi,:]+=dk_all[:hi-lo]
+        dv_far=dv_far+dv_all[hi-lo:]; dk_far=dk_far+dk_all[hi-lo:]
+        dq_t=dot_nn(jnp.concatenate([key_t[:,lo:hi],key_far_t],axis=1),ds)
         dq_ref[start:start+QB,:]=(pick_head(dq_t).T.astype(BF).astype(F32)*(HEAD_DIM**-0.5)).astype(BF)
     dk_ref[...]=(dk_acc[...]+lax.dot_general(sel_full,dk_far,(((0,),(0,)),((),())),preferred_element_type=F32,precision=lax.Precision.HIGHEST)).astype(BF)
     dv_ref[...]=(dv_acc[...]+lax.dot_general(sel_full,dv_far,(((0,),(0,)),((),())),preferred_element_type=F32,precision=lax.Precision.HIGHEST)).astype(BF)
@@ -218,11 +226,12 @@
         def _(chunk=chunk): chunk[...]=value
 
 
-def layer(mez,pos,ctx,ctxg,x,upstream,ffw,vecs,c_row,n):
+def layer(me,mez,pos,ctx,ctxg,x,upstream,ffw,vecs,c_row,n,extra):
+    half=max(n//2,1); cols=x.shape[1]//2
     length,width=x.shape; ff=c_row.shape[1]; w=len(ffw); steps=length//RB; blocks=ff//width; shard=width//n; fs=ff//n
-    def body(mez_ref,pos_ref,ctx_ref,glob_ref,x_ref,up_ref,vec_ref,c_ref,*refs):
+    def body(me_ref,mez_ref,pos_ref,ctx_ref,glob_ref,x_ref,up_ref,vec_ref,c_ref,*refs):
         ff_w=refs[:w]; chunks=refs[w:w+steps]
-        gs_ref,ag_ref,mg_ref,merged_ref,vg_ref,cg_ref,pack,wout,win,wback,acc_in,acc_back,act,slope,stage,sems,out_sems=refs[w+steps:]
+        gs_ref,mg_ref,vg_ref,cg_ref,pack,keep,send,wout,win,wback,acc_in,acc_back,acc_out,act,slope,stage,keep_v,send_v,sems,out_sems=refs[w+steps:]
         step=pl.program_id(0)
         first=step==0
         co=plane_copies(ff_w,3,wout,sems,0)
@@ -233,12 +242,12 @@
             for c in co+ci+cb: c.start()
             vg_ref[...]=jnp.zeros_like(vg_ref); cg_ref[...]=jnp.zeros_like(cg_ref)
             acc_in[...]=jnp.zeros_like(acc_in); acc_back[...]=jnp.zeros_like(acc_back)
+            acc_out[...]=jnp.zeros_like(acc_out)
             for c in co: c.wait()
         token=step*RB+lax.broadcasted_iota(jnp.int32,(16,RB),1)
         hot=jnp.where(token==pos_ref[...],1.0,0.0).astype(BF)
         is_glob=dot_tn(hot,jnp.ones((16,128),BF))[:,0:1]>0.5
         merged=jnp.where(is_glob,dot_tn(hot,glob_ref[...]),ctx_ref[...].astype(F32)).astype(BF)
-        merged_ref[...]=merged
         hat1,inv1=stats(x_ref[...].astype(F32)+(dot_nn(merged,wout[...])+vec_ref[4:5,:]))
         norm1=hat1*vec_ref[6:7,:]+vec_ref[8:9,:]
         low=norm1.astype(BF)
@@ -270,11 +279,19 @@
         gs=norm_back(acc*vec_ref[6:7,:],hat1,inv1)
         gs_ref[...]=gs
         ag=gs.astype(BF)
-        ag_ref[...]=ag
+        acc_out[...]+=dot_tn(merged,ag)
         vg_ref[4:5,:]+=col(ag.astype(F32))
         mg_ref[...]=dot_nt(ag,wout[...]).astype(BF)
         @pl.when(step==steps-1)
         def _():
+            m=me_ref[0]
+            for slot in range(n):
+                for h in range(2):
+                    part=acc_out[pl.ds(pl.multiple_of((m^slot)*shard,shard),shard),h*cols:(h+1)*cols]
+                    (send_v if slot%2 else keep_v)[slot//2,h*shard:(h+1)*shard,:]=part.astype(BF)
+            sides=[pltpu.make_async_copy(keep_v,keep.at[:,pl.ds(0,2*shard)],out_sems.at[2*blocks])]
+            if n>1: sides.append(pltpu.make_async_copy(send_v,send.at[:,pl.ds(0,2*shard)],out_sems.at[2*blocks+1]))
+            for c in sides: c.start()
             copies=[]
             for b in range(2*blocks):
                 slot=b%2
@@ -293,16 +310,16 @@
                         there=pack.at[pl.ds(at//fs,width//fs),pl.ds(blocks*shard,fs)]
                 copies.append(pltpu.make_async_copy(here,there,out_sems.at[b]))
                 copies[b].start()
-            for c in copies[-2:]: c.wait()
+            for c in copies[-2:]+sides: c.wait()
     blk=lambda w:pl.BlockSpec((RB,w),lambda i:(i,0))
     full=lambda s:pl.BlockSpec(s,lambda i:(0,0))
     return pl.pallas_call(body,grid=(steps,),
-        in_specs=[SMEM,full(pos.shape),blk(width),full(ctxg.shape),blk(width),blk(width),full(vecs.shape),full(c_row.shape)]+[ANY]*w,
-        out_specs=[full((RB,width))]*steps+[blk(width)]*4+[full((16,width)),full((1,ff)),ANY],
-        out_shape=[S((RB,width),BF)]*steps+[S((length,width),F32)]+[S((length,width),BF)]*3+[S((16,width),F32),S((1,ff),F32),S((n,blocks*shard+fs,width),BF)],
-        scratch_shapes=[pltpu.VMEM((width,width),BF),pltpu.VMEM((width,ff),BF),pltpu.VMEM((ff,width),BF),pltpu.VMEM((width,ff),F32),pltpu.VMEM((ff,width),F32),
-            pltpu.VMEM((RB,ff),BF),pltpu.VMEM((RB,ff),BF),pltpu.VMEM((2,width,width),BF),pltpu.SemaphoreType.DMA((2*n+n*blocks,)),pltpu.SemaphoreType.DMA((2*blocks,))],
-        compiler_params=params(),cost_estimate=cost(COST,1<<20),name="layer")(mez,pos,ctx,ctxg,x,upstream,vecs,c_row,*ffw)
+        in_specs=[SMEM,SMEM,full(pos.shape),blk(width),full(ctxg.shape),blk(width),blk(width),full(vecs.shape),full(c_row.shape)]+[ANY]*w,
+        out_specs=[full((RB,width))]*steps+[blk(width)]*2+[full((16,width)),full((1,ff)),ANY,ANY,ANY],
+        out_shape=[S((RB,width),BF)]*steps+[S((length,width),F32),S((length,width),BF),S((16,width),F32),S((1,ff),F32),S((n,blocks*shard+fs,width),BF)]+[S((half,2*shard+extra,cols),BF)]*2,
+        scratch_shapes=[pltpu.VMEM((width,width),BF),pltpu.VMEM((width,ff),BF),pltpu.VMEM((ff,width),BF),pltpu.VMEM((width,ff),F32),pltpu.VMEM((ff,width),F32),pltpu.VMEM((width,width),F32),
+            pltpu.VMEM((RB,ff),BF),pltpu.VMEM((RB,ff),BF),pltpu.VMEM((2,width,width),BF),pltpu.VMEM((half,2*shard,cols),BF),pltpu.VMEM((half,2*shard,cols),BF),pltpu.SemaphoreType.DMA((2*n+n*blocks,)),pltpu.SemaphoreType.DMA((2*blocks+2,))],
+        compiler_params=params(),cost_estimate=cost(COST,1<<20),name="layer")(me,mez,pos,ctx,ctxg,x,upstream,vecs,c_row,*ffw)
 
 
 def local_grads(me,x,grads,unit=None,vec=None,count=8):
@@ -403,9 +420,9 @@
         q=((dot_nn(rows,wts[0])+vec_ref[2:3,:])*(HEAD_DIM**-0.5)).astype(BF)
         q_ref[...]=q
         for c in cps[1]: c.wait()
-        u=dot_nt(wts[1],scatter_heads(q,own,count)).astype(BF)
+        u=dot_nt(scatter_heads(q,own,count),wts[1]).astype(BF)
         u_ref[...]=u
-        s=dot_nn(x_ref[...],u)
+        s=dot_nt(x_ref[...],u)
         p=jnp.exp(s-jnp.max(s,axis=0,keepdims=True))
         p=p/jnp.sum(p,axis=0,keepdims=True)
         p_ref[...]=p
@@ -417,14 +434,14 @@
         ctx_ref[...]=gather_heads(dot_nn(y,wts[2])+mass*vec_ref[3:4,:],own,count).astype(BF)
     vm=pl.BlockSpec(memory_space=pltpu.VMEM)
     return pl.pallas_call(body,in_specs=[vm,vm,vm]+[ANY]*w,out_specs=[vm]*6,
-        out_shape=[S((16,width),BF),S((length,wide),F32),S((width,wide),BF),S((wide,width),BF),S((16,width),BF),S((16,width),BF)],
+        out_shape=[S((16,width),BF),S((length,wide),F32),S((wide,width),BF),S((wide,width),BF),S((16,width),BF),S((16,width),BF)],
         scratch_shapes=[pltpu.VMEM((3,width,width),BF),pltpu.SemaphoreType.DMA((3*n,))],
         compiler_params=params(),cost_estimate=cost(COST,1<<20),name="globals")(pos,x,vecs,*ffw)
 
-def globals_bwd(me,pos,x,mg,gs,p,u,y,q,rows,merged,ag,ffw,vecs,count,n,extra):
+def globals_bwd(me,pos,x,mg,p,u,y,q,rows,ffw,vecs,count,n):
     length,width=x.shape; shard=width//n; half=max(n//2,1); w=len(ffw); cols=width//2
-    def body(me_ref,pos_ref,x_ref,mg_ref,gs_ref,p_ref,u_ref,y_ref,q_ref,r_ref,merged_ref,ag_ref,vec_ref,*refs):
-        ins=refs[:w]; out_ref,keep,send,keep2,send2,vg_ref,wts,res,keep_v,send_v,sems=refs[w:]
+    def body(me_ref,pos_ref,x_ref,mg_ref,p_ref,u_ref,y_ref,q_ref,r_ref,vec_ref,*refs):
+        ins=refs[:w]; f_ref,g_ref,keep,send,vg_ref,wts,res,keep_v,send_v,sems=refs[w:]
         m=me_ref[0]
         cps=[plane_copies(ins,j,wts.at[j],sems,j*n) for j in range(3)]
         for j in (2,1,0):
@@ -436,9 +453,9 @@
         cs=scatter_heads(dot_nn(sel,mg_ref[...]).astype(BF),own,count)
         qs=scatter_heads(q_ref[...],own,count)
         for c in cps[2]: c.wait()
-        v=dot_nt(wts[2],cs).astype(BF)
+        v=dot_nt(cs,wts[2]).astype(BF)
         shift=dot_nt(jnp.broadcast_to(vec_ref[3:4,:],(16,width)).astype(BF),cs)[0:1,:]
-        dp=dot_nn(x,v)+shift
+        dp=dot_nt(x,v)+shift
         p=p_ref[...]
         low=p.astype(BF)
         ds=(p*(dp-jnp.sum(p*dp,axis=0,keepdims=True))).astype(BF)
@@ -451,33 +468,36 @@
         vg_ref[...]=jnp.zeros_like(vg_ref)
         vg_ref[2:3,:]=jnp.sum(pre.astype(F32),axis=0,keepdims=True)
         vg_ref[3:4,:]=jnp.sum(mass*cs.astype(F32),axis=0,keepdims=True)
-        out_ref[...]=gs_ref[...]+dot_nt(ds,u_ref[...])+dot_nt(low,v)+lax.dot_general(hot,rows_grad,(((0,),(0,)),((),())),preferred_element_type=F32,precision=lax.Precision.HIGHEST)
-        for j,(l,r) in enumerate(((r_ref[...],pre),(a,qs),(y_ref[...],cs),(merged_ref[...],ag_ref[...]))):
+        wide=16*count
+        twice=jnp.concatenate([pos_ref[...],pos_ref[...],jnp.full((96,1),-1,jnp.int32)],axis=0)
+        hots=jnp.where(lax.broadcasted_iota(jnp.int32,(128,length),1)==twice,1.0,0.0)
+        high=rows_grad.astype(BF)
+        f_ref[:,0:wide]=ds; f_ref[:,wide:2*wide]=low; f_ref[:,2*wide:2*wide+128]=hots.T.astype(BF)
+        g_ref[...]=jnp.zeros_like(g_ref)
+        g_ref[0:wide,:]=u_ref[...]; g_ref[wide:2*wide,:]=v
+        g_ref[2*wide:2*wide+16,:]=high; g_ref[2*wide+16:2*wide+32,:]=(rows_grad-high.astype(F32)).astype(BF)
+        for j,(l,r) in enumerate(((r_ref[...],pre),(a,qs),(y_ref[...],cs))):
             res[...]=dot_tn(l,r)
             for slot in range(n):
                 for h in range(2):
                     part=res[pl.ds(pl.multiple_of((m^slot)*shard,shard),shard),h*cols:(h+1)*cols]
                     (send_v if slot%2 else keep_v)[slot//2,(2*j+h)*shard:(2*j+h+1)*shard,:]=part.astype(BF)
-        cps=[]
-        for here,first,there in ((keep_v,0,keep),(keep_v,6*shard,keep2),(send_v,0,send),(send_v,6*shard,send2)):
-            if n==1 and here is send_v: continue
-            rows_out=6*shard if first==0 else 2*shard
-            cps.append(pltpu.make_async_copy(here.at[:,pl.ds(first,rows_out)],there.at[:,pl.ds(0,rows_out)],sems.at[3*n+len(cps)]))
+        cps=[pltpu.make_async_copy(keep_v,keep,sems.at[3*n])]
+        if n>1: cps.append(pltpu.make_async_copy(send_v,send,sems.at[3*n+1]))
         for c in cps: c.start()
         for c in cps: c.wait()
     vm=pl.BlockSpec(memory_space=pltpu.VMEM)
-    o1=S((half,6*shard,cols),BF)
-    o2=S((half,2*shard+extra,cols),BF)
-    return pl.pallas_call(body,in_specs=[SMEM]+[vm]*12+[ANY]*w,out_specs=[vm,ANY,ANY,ANY,ANY,vm],
-        out_shape=[S((length,width),F32),o1,o1,o2,o2,S((16,width),F32)],
-        scratch_shapes=[pltpu.VMEM((3,width,width),BF),pltpu.VMEM((width,width),F32),pltpu.VMEM((half,8*shard,cols),BF),pltpu.VMEM((half,8*shard,cols),BF),pltpu.SemaphoreType.DMA((3*n+4,))],
-        compiler_params=params(),cost_estimate=cost(COST,1<<20),name="globals_back")(me,pos,x,mg,gs,p,u,y,q,rows,merged,ag,vecs,*ffw)
-
-
-def inputs_back(me,mez,gs,groups,pieces):
+    o=S((half,6*shard,cols),BF)
+    return pl.pallas_call(body,in_specs=[SMEM]+[vm]*9+[ANY]*w,out_specs=[vm,vm,ANY,ANY,vm],
+        out_shape=[S((length,32*count+128),BF),S((32*count+128,width),BF),o,o,S((16,width),F32)],
+        scratch_shapes=[pltpu.VMEM((3,width,width),BF),pltpu.VMEM((width,width),F32),pltpu.VMEM((half,6*shard,cols),BF),pltpu.VMEM((half,6*shard,cols),BF),pltpu.SemaphoreType.DMA((3*n+2,))],
+        compiler_params=params(),cost_estimate=cost(COST,1<<20),name="globals_back")(me,pos,x,mg,p,u,y,q,rows,vecs,*ffw)
+
+
+def inputs_back(me,mez,gs,glob,groups,pieces):
     length,width=gs.shape; n=len(pieces); shard=width//n; g=len(groups); cols=width//g
     steps=length//RB
-    def body(me_ref,mez_ref,gs_ref,*refs):
+    def body(me_ref,mez_ref,gs_ref,f_ref,g_ref,*refs):
         parts=refs[:3*g]; ins=refs[3*g:3*g+n]; chunks=refs[3*g+n:3*g+n+steps]; vg_ref,wts,sems=refs[3*g+n+steps:]
         m=me_ref[0]
         @pl.when(pl.program_id(0)==0)
@@ -486,7 +506,7 @@
             for c in cps: c.start()
             vg_ref[...]=jnp.zeros_like(vg_ref)
             for c in cps: c.wait()
-        acc=gs_ref[...]
+        acc=gs_ref[...]+dot_nn(f_ref[...],g_ref[...])
         for j in range(g):
             a=j*cols
             for w in range(3): acc=acc+dot_nt(parts[3*j+w][...],wts[w,:,a:a+cols])
@@ -495,10 +515,10 @@
         chunk_store(chunks,mez_ref[0],acc.astype(BF))
     blk=pl.BlockSpec((RB,width),lambda i:(i,0))
     part=pl.BlockSpec((RB,cols),lambda i:(i,0))
-    return pl.pallas_call(body,grid=(length//RB,),in_specs=[SMEM,SMEM,blk]+[part]*(3*g)+[ANY]*n,
+    return pl.pallas_call(body,grid=(length//RB,),in_specs=[SMEM,SMEM,blk,pl.BlockSpec((RB,glob[0].shape[1]),lambda i:(i,0)),pl.BlockSpec(glob[1].shape,lambda i:(0,0))]+[part]*(3*g)+[ANY]*n,
         out_specs=[pl.BlockSpec((RB,width),lambda i:(0,0))]*steps+[pl.BlockSpec((16,width),lambda i:(0,0))],out_shape=[S((RB,width),BF)]*steps+[S((16,width),F32)],
         scratch_shapes=[pltpu.VMEM((3,width,width),BF),pltpu.SemaphoreType.DMA((3*n,))],
-        compiler_params=params(),cost_estimate=cost(COST,1<<20),name="inputs_back")(me,mez,gs,*[p for t in groups for p in t],*pieces)
+        compiler_params=params(),cost_estimate=cost(COST,1<<20),name="inputs_back")(me,mez,gs,*glob,*[p for t in groups for p in t],*pieces)
 
 
 def flip(value, axis, bit):
@@ -693,8 +713,9 @@
         ctx_glob, probs, keys, mixed, query, rows = globals_fwd(
             pos, x, ffw, vecs, glob_count, count
         )
-        *out, grad_sum, attn_grad, merged_grad, merged, vec_one, c_grad, ff_pack = layer(
-            mez, pos, ctx, ctx_glob, x, up_all[index], ffw, vecs, c_row, count
+        *out, grad_sum, merged_grad, vec_one, c_grad, ff_pack, keep_two, send_two = layer(
+            me, mez, pos, ctx, ctx_glob, x, up_all[index], ffw, vecs, c_row, count,
+            3 * shard if tree else 0,
         )
         if tree:
             out_moved = Exchange(out)
@@ -703,24 +724,8 @@
         if tree:
             ff_mine = lax.psum_scatter(ff_pack, "fsdp", scatter_dimension=0, tiled=False)
             merged_grad = tie(merged_grad, ff_pack)
-        grad_sum, keep_one, send_one, keep_two, send_two, vec_two = globals_bwd(
-            me,
-            pos,
-            x,
-            merged_grad,
-            grad_sum,
-            probs,
-            keys,
-            mixed,
-            query,
-            rows,
-            merged,
-            attn_grad,
-            ffw,
-            vecs,
-            glob_count,
-            count,
-            3 * shard if tree else 0,
+        *glob, keep_one, send_one, vec_two = globals_bwd(
+            me, pos, x, merged_grad, probs, keys, mixed, query, rows, ffw, vecs, glob_count, count
         )
         group_pairs = width // 128 // GROUPS
         groups = []
@@ -738,7 +743,7 @@
         if tree:
             (grad_sum,) = meet([grad_sum], [one, two], parts[0])
             grad_sum = tie(grad_sum, one.advance(), two.advance())
-        *input_grad, vec_three = inputs_back(me, mez, grad_sum, groups, local_w)
+        *input_grad, vec_three = inputs_back(me, mez, grad_sum, glob, groups, local_w)
         if tree:
             grads_moved = Exchange(input_grad)
         else:

time: 418 us -> 410 us (0.981)
  Pallas kernels: 187 us -> 166 us
  waiting for transfers between devices: 101 us -> 116 us
    all_gather x1, waiting for transfers between devices: 7.12 us -> 17.1 us  [per_device(): ffw = [lax.all_gather(pack, 'fsdp')]]
    pallas_call x1, Pallas kernels: 25.8 us -> 15.8 us  [attn_fwd(): pl.pallas_call(fwd_kernel, grid=(pairs,), in_specs=[pl.BlockSpec((16, 1),...]
    pallas_call x3, Pallas kernels: 89 us -> 83.2 us  [the longest x1 60.4 us: layer(): pl.pallas_call(body, grid=(steps,), in_specs=[SMEM, SMEM, full(pos.shape)...]
    ppermute x34, waiting for transfers between devices: 91.1 us -> 96.4 us  [flip(): lax.ppermute(value, axis, [(index, index ^ bit) for index in range(count)])]
    pallas_call x2, Pallas kernels: 38.2 us -> 33.7 us  [attn_bwd(): pl.pallas_call(bwd_kernel, grid=(pairs,), in_specs=[pl.BlockSpec((16, 1),...]
  transfers between devices with their start and end apart: 38 -> 38, of which waited for: 22 -> 22; matrix products, arithmetic and copies ran while one was open for 8% -> 8% of each run, Pallas kernels for 31% -> 26%
where the time goes in v1:
time: 410 us; the launch traced here: 402 us
  Pallas kernels  166 us (40%)
  waiting for transfers between devices  116 us (28%)
  starting transfers between devices  51.2 us (12%)
  other arithmetic  29.8 us (7%)
  local copies, waits for them, and re-layouts  23.4 us (6%)
  between operations  15 us (4%)
    ppermute x34, waiting for transfers between devices, flip(): lax.ppermute(value, axis, [(index, index ^ bit) for index in range(count)])  96.4 us
    pallas_call x1, Pallas kernels, layer(): pl.pallas_call(body, grid=(steps,), in_specs=[SMEM, SMEM, full(pos.shape)...  60.4 us
    ppermute x34, starting transfers between devices, flip(): lax.ppermute(value, axis, [(index, index ^ bit) for index in range(count)])  42.7 us
    pallas_call x2, Pallas kernels, attn_bwd(): pl.pallas_call(bwd_kernel, grid=(pairs,), in_specs=[pl.BlockSpec((16, 1),...  33.7 us
    all_gather x1, waiting for transfers between devices, per_device(): ffw = [lax.all_gather(pack, 'fsdp')]  17.1 us
    pallas_call x1, Pallas kernels, attn_fwd(): pl.pallas_call(fwd_kernel, grid=(pairs,), in_specs=[pl.BlockSpec((16, 1),...  15.8 us
    pallas_call x2, Pallas kernels, local_grads(): pl.pallas_call(body, in_specs=[SMEM] + [vm] * (first - 1) + [ANY] * (0 if...  12.2 us
    pallas_call x1, Pallas kernels, inputs_back(): pl.pallas_call(body, grid=(length // RB,), in_specs=[SMEM, SMEM, blk, pl....  11.8 us
  transfers between devices with their start and end apart: 38, of which 22 were waited for; matrix products, arithmetic and copies ran while one was open for 8% of the time, Pallas kernels for 26%

profile of v1, /device:TPU:0, one launch (start us, length us, event | category | flops | bytes accessed | tf_op | source)
XLA Modules:
  0.0 402.1 jit_solution(17675521903136849945)
XLA Ops:
  8.3 2.6 pad_maximum_fusion
  12.1 3.0 collective-permute-start.1
  15.1 1.5 collective-permute-start.3
  16.6 4.9 %all-to-all-start = ((bf16[4,256,768]{2,1,0:T(8,128)(2,1)}), bf16[4,256,768]{2,1,0:T(8,128)(2,1)S(1)}, u32[]{:S(2)}, u32[]{:S(2)}) async-start(bf16[4,256,768]{2,1,0:T(8,128)(2,1)} %param.14), calls=%async_computation | async-start | bytes 3145728 | tf_op jit(solution)/shard_map/all_to_all | solution.py:657
  21.5 6.5 %collective-permute-done.1.refs_2_.refs_8_ = bf16[304,768]{1,0:T(8,128)(2,1)S(1)} collective-permute-done((bf16[304,768]{1,0:T(8,128)(2,1)S(1)}, bf16[304,768]{1,0:T(8,128)(2,1)S(1)}, u32[]{:S(2)}, u32[]{:S(2)}) %collective-permute-start.1) | collective-permute-done | bytes 466976 | tf_op jit(solution)/shard_map/ppermute | solution.py:526
  28.0 1.3 collective-permute-start.5
  30.5 21.0 %collective-permute-done.5.refs_6_.refs_12_ = bf16[304,768]{1,0:T(8,128)(2,1)} collective-permute-done((bf16[304,768]{1,0:T(8,128)(2,1)S(1)}, bf16[304,768]{1,0:T(8,128)(2,1)}, u32[]{:S(2)}, u32[]{:S(2)}) %collective-permute-start.5) | collective-permute-done | bytes 466976 | tf_op jit(solution)/shard_map/ppermute | solution.py:526
  56.4 2.7 all-to-all-done
  59.1 3.6 all-to-all-start.1
  62.7 8.8 %project.1 = (bf16[1024,768]{1,0:T(8,128)(2,1)}, bf16[1024,768]{1,0:T(8,128)(2,1)}, bf16[1024,768]{1,0:T(8,128)(2,1)}) custom-call(s32[1]{0:T(128)} %bitcast.1.me_ref, bf16[1024,768]{1,0:T(8,128)(2,1)} %bitcast.189, f32[16,768]{1,0:T(8,128)} %reshape.231.vec_ref, bf16[304,768]{1,0:T(8,128)(2,1)} %copy-done.16, bf16[304,768]{1,0:T(8,128)(2,1)} %copy-done.27, ...), custom_call_target="tpu_custom_call" | custom-call | flops 20000000000 | bytes 1048576 | tf_op jit(solution)/shard_map/project/pallas_call | solution.py:389
  71.5 15.8 %attend.1 = (bf16[1024,768]{1,0:T(8,128)(2,1)}, f32[6,8,1024]{2,1,0:T(8,128)}) custom-call(s32[16,1]{1,0:T(8,128)} %scatter.4.pos_ref, bf16[1024,768]{1,0:T(8,128)(2,1)} %get-tuple-element.101.q_ref, bf16[1024,768]{1,0:T(8,128)(2,1)} %get-tuple-element.102.k_ref, bf16[1024,768]{1,0:T(8,128)(2,1)} %get-tuple-element.103.v_ref), custom_call_target="tpu_custom_call" | custom-call | flops 20000000000 | bytes 1048576 | tf_op jit(solution)/shard_map/attend/pallas_call | solution.py:96
  87.4 17.1 %all-gather.3.cloned.1.call-done = bf16[9216,768]{1,0:T(8,128)(2,1)} async-done(((bf16[1152,768]{1,0:T(8,128)(2,1)}), bf16[9216,768]{1,0:T(8,128)(2,1)}) %all-gather.3.cloned.1.call-update) | async-done | bytes 14155792 | tf_op jit(solution)/shard_map/all_gather | solution.py:690
  104.5 6.4 %globals.1 = (bf16[16,768]{1,0:T(8,128)(2,1)}, f32[1024,64]{1,0:T(8,128)}, bf16[64,768]{1,0:T(8,128)(2,1)}, bf16[64,768]{1,0:T(8,128)(2,1)}, bf16[16,768]{1,0:T(8,128)(2,1)}, /*index=5*/bf16[16,768]{1,0:T(8,128)(2,1)}) custom-call(s32[16,1]{1,0:T(8,128)} %scatter.4.pos_ref, bf16[1024,768]{1,0:T(8,128)(2,1)} %bitcast.190, f32[16,768]{1,0:T(8,128)} %reshape.231.vec_ref, ...), custom_call_target="tpu_custom_call" | custom-call | flops 20000000000 | bytes 1048576 | tf_op jit(solution)/shard_map/globals/pallas_call | solution.py:436
  110.9 1.2 copy-done.11
  112.1 60.4 %layer.1 = (bf16[256,768]{1,0:T(8,128)(2,1)}, bf16[256,768]{1,0:T(8,128)(2,1)}, bf16[256,768]{1,0:T(8,128)(2,1)}, bf16[256,768]{1,0:T(8,128)(2,1)}, f32[1024,768...) custom-call(s32[1]{0:T(128)} %bitcast.1.me_ref, ...), custom_call_target="tpu_custom_call" | custom-call | flops 20000000000 | bytes 1048576 | tf_op jit(solution)/shard_map/layer/pallas_call | solution.py:316
  172.5 11.0 %globals_back.1 = (bf16[1024,256]{1,0:T(8,128)(2,1)}, bf16[256,768]{1,0:T(8,128)(2,1)}, bf16[4,576,384]{2,1,0:T(8,128)(2,1)}, bf16[4,576,384]{2,1,0:T(8,128)(2,1)}, f32[16,768]{1,0:T(8,128)}) custom-call(s32[1]{0:T(128)} %bitcast.1.me_ref, s32[16,1]{1,0:T(8,128)} %scatter.4.pos_ref, bf16[1024,768]{1,0:T(8,128)(2,1)} %bitcast.192, ...), custom_call_target="tpu_custom_call" | custom-call | flops 20000000000 | bytes 1048576 | tf_op jit(solution)/shard_map/globals_back/pallas_call | solution.py:491
  183.9 1.6 collective-permute-start.7
  185.4 2.4 collective-permute-start.8
  188.3 16.8 %attend_back.2 = (bf16[1024,384]{1,0:T(8,128)(2,1)}, bf16[1024,384]{1,0:T(8,128)(2,1)}, bf16[1024,384]{1,0:T(8,128)(2,1)}) custom-call(s32[16,1]{1,0:T(8,128)} %scatter.4.pos_ref, bf16[1024,768]{1,0:T(8,128)(2,1)} %get-tuple-element.101.q_ref, bf16[1024,768]{1,0:T(8,128)(2,1)} %get-tuple-element.102.k_ref, bf16[1024,768]{1,0:T(8,128)(2,1)} %get-tuple-element.103.v_ref, ...), custom_call_target="tpu_custom_call" | custom-call | flops 20000000000 | bytes 1048576 | tf_op jit(solution)/shard_map/attend_back/pallas_call | solution.py:164
  205.1 6.0 %local_grads.2 = (bf16[4,480,384]{2,1,0:T(8,128)(2,1)}, bf16[4,480,384]{2,1,0:T(8,128)(2,1)}) custom-call(s32[1]{0:T(128)} %bitcast.1.me_ref, bf16[1024,768]{1,0:T(8,128)(2,1)} %bitcast.193, bf16[1024,384]{1,0:T(8,128)(2,1)} %get-tuple-element.121.refs_0_, ...), custom_call_target="tpu_custom_call", output_to_operand_aliasing={{0}: (5, {}), {1}: (6, {})} | custom-call | flops 20000000000 | bytes 1048576 | tf_op jit(solution)/shard_map/local_grads/pallas_call | solution.py:353
  211.3 3.9 collective-permute-done.8.refs_2_
  216.8 16.8 %attend_back.3 = (bf16[1024,384]{1,0:T(8,128)(2,1)}, bf16[1024,384]{1,0:T(8,128)(2,1)}, bf16[1024,384]{1,0:T(8,128)(2,1)}) custom-call(s32[16,1]{1,0:T(8,128)} %scatter.4.pos_ref, bf16[1024,768]{1,0:T(8,128)(2,1)} %get-tuple-element.101.q_ref, bf16[1024,768]{1,0:T(8,128)(2,1)} %get-tuple-element.102.k_ref, bf16[1024,768]{1,0:T(8,128)(2,1)} %get-tuple-element.103.v_ref, ...), custom_call_target="tpu_custom_call" | custom-call | flops 20000000000 | bytes 1048576 | tf_op jit(solution)/shard_map/attend_back/pallas_call | solution.py:164
  234.7 1.2 copy-done.14
  236.0 3.0 convert_add_fusion.1
  239.0 11.8 %inputs_back.1 = (bf16[256,768]{1,0:T(8,128)(2,1)}, bf16[256,768]{1,0:T(8,128)(2,1)}, bf16[256,768]{1,0:T(8,128)(2,1)}, bf16[256,768]{1,0:T(8,128)(2,1)}, f32[16,768]{1,0:T(8,128)}) custom-call(s32[1]{0:T(128)} %bitcast.1.me_ref, s32[1]{0:T(128)} %bitcast.mez_ref, f32[1024,768]{1,0:T(8,128)} %get-tuple-element.139.gs_ref, ...), custom_call_target="tpu_custom_call" | custom-call | flops 20000000000 | bytes 1048576 | tf_op jit(solution)/shard_map/inputs_back/pallas_call | solution.py:518
  250.8 7.2 %collective-permute-start.15 = (bf16[256,768]{1,0:T(8,128)(2,1)}, bf16[256,768]{1,0:T(8,128)(2,1)S(1)}, u32[]{:S(2)}, u32[]{:S(2)}) collective-permute-start(bf16[256,768]{1,0:T(8,128)(2,1)} %get-tuple-element.145), channel_id=1, source_target_pairs={{0,1},{1,0},{2,3},{3,2},{4,5},{5,4},{6,7},{7,6},{8,9},{9,8},{10,11... | collective-permute-start | bytes 1179656 | tf_op jit(solution)/shard_map/ppermute | solution.py:526
  260.1 1.2 collective-permute-start.12
  262.2 1.4 collective-permute-start.17
  263.6 1.4 pad_add_fusion.refs_3_
  265.1 1.5 convert.6
  267.4 5.0 %collective-permute-done.15.refs_1_ = bf16[256,768]{1,0:T(8,128)(2,1)S(1)} collective-permute-done((bf16[256,768]{1,0:T(8,128)(2,1)}, bf16[256,768]{1,0:T(8,128)(2,1)S(1)}, u32[]{:S(2)}, u32[]{:S(2)}) %collective-permute-start.15) | collective-permute-done | bytes 393248 | tf_op jit(solution)/shard_map/ppermute | solution.py:526
  272.4 6.2 %local_grads.3 = (bf16[4,304,384]{2,1,0:T(8,128)(2,1)}, bf16[4,304,384]{2,1,0:T(8,128)(2,1)}) custom-call(s32[1]{0:T(128)} %bitcast.1.me_ref, bf16[1024,768]{1,0:T(8,128)(2,1)} %bitcast.194, bf16[1024,384]{1,0:T(8,128)(2,1)} %get-tuple-element.134.refs_3_.refs_0_, bf16[1024,384]{1,0:T(8,128)(2,1)} %get-tuple-element.142.refs_4_.refs_1_, ...), custom_call_target="tpu_custom_call" | custom-call | flops 20000000000 | bytes 1048576 | tf_op jit(solution)/shard_map/local_grads/pallas_call | solution.py:353
  278.6 12.7 %collective-permute-done.16.refs_2_ = bf16[256,768]{1,0:T(8,128)(2,1)S(1)} collective-permute-done((bf16[256,768]{1,0:T(8,128)(2,1)}, bf16[256,768]{1,0:T(8,128)(2,1)S(1)}, u32[]{:S(2)}, u32[]{:S(2)}) %collective-permute-start.16) | collective-permute-done | bytes 393248 | tf_op jit(solution)/shard_map/ppermute | solution.py:526
  292.1 1.6 convert_add_fusion
  293.7 4.2 %collective-permute-done.14 = bf16[2,192,768]{2,1,0:T(8,128)(2,1)} collective-permute-done((bf16[2,192,768]{2,1,0:T(8,128)(2,1)}, bf16[2,192,768]{2,1,0:T(8,128)(2,1)}, u32[]{:S(2)}, u32[]{:S(2)}) %collective-permute-start.14) | collective-permute-done | bytes 589856 | tf_op jit(solution)/shard_map/ppermute | solution.py:526
  297.9 1.2 bitcast_add_fusion
  299.2 2.2 fusion.19
  301.3 1.9 fusion.16
  303.2 1.3 add_convert_fusion.2
  304.5 2.0 collective-permute-start.18
  306.5 1.5 collective-permute-start.19
  308.0 1.2 collective-permute-start.22
  309.2 12.4 %collective-permute-done.22 = bf16[192,768]{1,0:T(8,128)(2,1)} collective-permute-done((bf16[192,768]{1,0:T(8,128)(2,1)S(1)}, bf16[192,768]{1,0:T(8,128)(2,1)}, u32[]{:S(2)}, u32[]{:S(2)}) %collective-permute-start.22) | collective-permute-done | bytes 294944 | tf_op jit(solution)/shard_map/ppermute | solution.py:526
  321.6 3.3 collective-permute-done.18
  324.9 1.3 fusion.6
  326.2 1.2 fusion.8
  329.7 2.0 collective-permute-start.24
  332.8 1.9 collective-permute-start.23
  334.7 3.3 collect.2
  339.0 1.9 collective-permute-done.24
  340.8 1.6 collective-permute-done.25
  344.3 1.9 collective-permute-start.28
  346.2 1.9 fusion.14
  350.2 2.1 collective-permute-start.26
  352.3 3.0 collect.3
  355.3 8.1 %collective-permute-done.27 = bf16[2,76,384]{2,1,0:T(8,128)(2,1)S(1)} collective-permute-done((bf16[2,76,384]{2,1,0:T(8,128)(2,1)}, bf16[2,76,384]{2,1,0:T(8,128)(2,1)S(1)}, u32[]{:S(2)}, u32[]{:S(2)}) %collective-permute-start.27) | collective-permute-done | bytes 116768 | tf_op jit(solution)/shard_map/ppermute | solution.py:526
  363.8 3.5 collective-permute-start.30
  368.7 1.5 collective-permute-done.30
  370.2 5.9 %collective-permute-done.29 = bf16[264,384]{1,0:T(8,128)(2,1)S(1)} collective-permute-done((bf16[264,384]{1,0:T(8,128)(2,1)S(1)}, bf16[264,384]{1,0:T(8,128)(2,1)S(1)}, u32[]{:S(2)}, u32[]{:S(2)}) %collective-permute-start.29) | collective-permute-done | bytes 202784 | tf_op jit(solution)/shard_map/ppermute | solution.py:526
  376.3 2.9 collective-permute-start.32
  379.2 1.2 fusion.35
  381.2 1.2 copy.52
  383.1 3.4 collective-permute-done.31
  390.0 2.0 collective-permute-done.33
  (186 shorter events, 34.6 us)
Async XLA Ops:
  7.2 22.2 %copy-start = (s32[4,4]{1,0:T(4,128)S(1)}, s32[4,4]{1,0:T(4,128)}, u32[]{:S(2)}) copy-start(s32[4,4]{1,0:T(4,128)} %param.15) | copy-start | bytes 196
  7.2 97.3 %all-gather.3.cloned.1.call-start = ((), (), s32[]{:S(2)}) async-start(), calls=%async_computation.4 | async-start | bytes 15925248 | tf_op jit(solution)/shard_map/all_gather | solution.py:690
  12.0 42.3 %copy-start.16 = (bf16[304,768]{1,0:T(8,128)(2,1)}, bf16[304,768]{1,0:T(8,128)(2,1)S(1)}, u32[]{:S(2)}) copy-start(bf16[304,768]{1,0:T(8,128)(2,1)S(1)} %fusion.12.refs_0_.refs_6_) | copy-start | bytes 1400836
  12.1 16.0 %collective-permute-start.1 = (bf16[304,768]{1,0:T(8,128)(2,1)S(1)}, bf16[304,768]{1,0:T(8,128)(2,1)S(1)}, u32[]{:S(2)}, u32[]{:S(2)}) collective-permute-start(bf16[304,768]{1,0:T(8,128)(2,1)S(1)} %fusion.12.refs_0_.refs_6_), channel_id=1, source_target_pairs={{0,8},{4,12},{8,0},{12,4},{16,24},{20,28},{24,16},{28,20},{1,9},{5... | collective-permute-start | bytes 1400840 | tf_op jit(solution)/shard_map/ppermute | solution.py:526
  15.1 15.4 %collective-permute-start.3 = (bf16[304,768]{1,0:T(8,128)(2,1)S(1)}, bf16[304,768]{1,0:T(8,128)(2,1)S(1)}, u32[]{:S(2)}, u32[]{:S(2)}) collective-permute-start(bf16[304,768]{1,0:T(8,128)(2,1)S(1)} %fusion.12.refs_0_.refs_6_), channel_id=1, source_target_pairs={{0,16},{4,20},{8,24},{12,28},{16,0},{20,4},{24,8},{28,12},{1,17},{... | collective-permute-start | bytes 1400840 | tf_op jit(solution)/shard_map/ppermute | solution.py:526
  16.6 13.9 %collective-permute-start = (bf16[304,768]{1,0:T(8,128)(2,1)S(1)}, bf16[304,768]{1,0:T(8,128)(2,1)S(1)}, u32[]{:S(2)}, u32[]{:S(2)}) collective-permute-start(bf16[304,768]{1,0:T(8,128)(2,1)S(1)} %fusion.12.refs_0_.refs_6_), channel_id=1, source_target_pairs={{0,4},{4,0},{8,12},{12,8},{16,20},{20,16},{24,28},{28,24},{1,5},{5... | collective-permute-start | bytes 1400840 | tf_op jit(solution)/shard_map/ppermute | solution.py:526
  16.6 42.5 %all-to-all-start = ((bf16[4,256,768]{2,1,0:T(8,128)(2,1)}), bf16[4,256,768]{2,1,0:T(8,128)(2,1)S(1)}, u32[]{:S(2)}, u32[]{:S(2)}) async-start(bf16[4,256,768]{2,1,0:T(8,128)(2,1)} %param.14), calls=%async_computation | async-start | bytes 3145728 | tf_op jit(solution)/shard_map/all_to_all | solution.py:657
  28.0 31.1 %copy-start.25 = (bf16[304,768]{1,0:T(8,128)(2,1)}, bf16[304,768]{1,0:T(8,128)(2,1)S(1)}, u32[]{:S(2)}) copy-start(bf16[304,768]{1,0:T(8,128)(2,1)S(1)} %collective-permute-done.1.refs_2_.refs_8_) | copy-start | bytes 1400836
  28.0 23.5 %collective-permute-start.2 = (bf16[304,768]{1,0:T(8,128)(2,1)S(1)}, bf16[304,768]{1,0:T(8,128)(2,1)}, u32[]{:S(2)}, u32[]{:S(2)}) collective-permute-start(bf16[304,768]{1,0:T(8,128)(2,1)S(1)} %collective-permute-done.1.refs_2_.refs_8_), channel_id=1, source_target_pairs={{0,4},{4,0},{8,12},{12,8},{16,20},{20,16},{24,28},{28,24},{1,5},{5... | collective-permute-start | bytes 1400840 | tf_op jit(solution)/shard_map/ppermute | solution.py:526
  28.0 23.5 %collective-permute-start.5 = (bf16[304,768]{1,0:T(8,128)(2,1)S(1)}, bf16[304,768]{1,0:T(8,128)(2,1)}, u32[]{:S(2)}, u32[]{:S(2)}) collective-permute-start(bf16[304,768]{1,0:T(8,128)(2,1)S(1)} %collective-permute-done.1.refs_2_.refs_8_), channel_id=1, source_target_pairs={{0,16},{4,20},{8,24},{12,28},{16,0},{20,4},{24,8},{28,12},{1,17},{... | collective-permute-start | bytes 1400840 | tf_op jit(solution)/shard_map/ppermute | solution.py:526
  30.4 28.6 %copy-start.26 = (bf16[304,768]{1,0:T(8,128)(2,1)}, bf16[304,768]{1,0:T(8,128)(2,1)S(1)}, u32[]{:S(2)}) copy-start(bf16[304,768]{1,0:T(8,128)(2,1)S(1)} %collective-permute-done.3.refs_4_.refs_10_) | copy-start | bytes 1400836
  30.4 21.8 %collective-permute-start.4 = (bf16[304,768]{1,0:T(8,128)(2,1)S(1)}, bf16[304,768]{1,0:T(8,128)(2,1)S(1)}, u32[]{:S(2)}, u32[]{:S(2)}) collective-permute-start(bf16[304,768]{1,0:T(8,128)(2,1)S(1)} %collective-permute-done.3.refs_4_.refs_10_), channel_id=1, source_target_pairs={{0,4},{4,0},{8,12},{12,8},{16,20},{20,16},{24,28},{28,24},{1,5},{5... | collective-permute-start | bytes 1400840 | tf_op jit(solution)/shard_map/ppermute | solution.py:526
  30.5 28.6 %copy-start.27 = (bf16[304,768]{1,0:T(8,128)(2,1)}, bf16[304,768]{1,0:T(8,128)(2,1)S(1)}, u32[]{:S(2)}) copy-start(bf16[304,768]{1,0:T(8,128)(2,1)S(1)} %collective-permute-done.refs_1_.refs_7_) | copy-start | bytes 1400836
  51.5 2.0 collective-permute-start.6
  52.2 1.3 copy-start.28
  59.1 3.6 copy-start.10
  59.1 51.8 %all-to-all-start.1 = ((bf16[4,256,768]{2,1,0:T(8,128)(2,1)}), bf16[4,256,768]{2,1,0:T(8,128)(2,1)S(1)}, u32[]{:S(2)}, u32[]{:S(2)}) async-start(bf16[4,256,768]{2,1,0:T(8,128)(2,1)} %param.25), calls=%async_computation.1 | async-start | bytes 3145728 | tf_op jit(solution)/shard_map/all_to_all | solution.py:657
  62.7 202.4 %reduce-scatter.2.cloned.1.call-start = ((), (), s32[]{:S(2)}) async-start(), calls=%async_computation.3 | async-start | bytes 10616832 | tf_op jit(solution)/shard_map/reduce_scatter | solution.py:725
  172.5 12.9 %copy-start.36 = (bf16[256,768]{1,0:T(8,128)(2,1)S(1)}, bf16[256,768]{1,0:T(8,128)(2,1)}, u32[]{:S(2)}) copy-start(bf16[256,768]{1,0:T(8,128)(2,1)} %get-tuple-element.118) | copy-start | bytes 1179652
  172.5 15.3 %copy-start.35 = (bf16[256,768]{1,0:T(8,128)(2,1)S(1)}, bf16[256,768]{1,0:T(8,128)(2,1)}, u32[]{:S(2)}) copy-start(bf16[256,768]{1,0:T(8,128)(2,1)} %get-tuple-element.119) | copy-start | bytes 1179652
  183.5 50.0 %collective-permute-start.10 = (bf16[4,576,384]{2,1,0:T(8,128)(2,1)}, bf16[4,576,384]{2,1,0:T(8,128)(2,1)S(1)}, u32[]{:S(2)}, u32[]{:S(2)}) collective-permute-start(bf16[4,576,384]{2,1,0:T(8,128)(2,1)} %get-tuple-element.114), channel_id=1, source_target_pairs={{0,4},{4,0},{8,12},{12,8},{16,20},{20,16},{24,28},{28,24},{1,5},{5... | collective-permute-start | bytes 5308424 | tf_op jit(solution)/shard_map/ppermute | solution.py:526
  183.9 27.4 %collective-permute-start.7 = (bf16[256,768]{1,0:T(8,128)(2,1)}, bf16[256,768]{1,0:T(8,128)(2,1)S(1)}, u32[]{:S(2)}, u32[]{:S(2)}) collective-permute-start(bf16[256,768]{1,0:T(8,128)(2,1)} %get-tuple-element.117), channel_id=1, source_target_pairs={{0,1},{1,0},{2,3},{3,2},{4,5},{5,4},{6,7},{7,6},{8,9},{9,8},{10,11... | collective-permute-start | bytes 1179656 | tf_op jit(solution)/shard_map/ppermute | solution.py:526
  185.4 29.7 %collective-permute-start.8 = (bf16[256,768]{1,0:T(8,128)(2,1)S(1)}, bf16[256,768]{1,0:T(8,128)(2,1)S(1)}, u32[]{:S(2)}, u32[]{:S(2)}) collective-permute-start(bf16[256,768]{1,0:T(8,128)(2,1)S(1)} %copy-done.36), channel_id=1, source_target_pairs={{0,2},{1,3},{2,0},{3,1},{4,6},{5,7},{6,4},{7,5},{8,10},{9,11},{10,... | collective-permute-start | bytes 1179656 | tf_op jit(solution)/shard_map/ppermute | solution.py:526
  187.9 27.3 %collective-permute-start.9 = (bf16[256,768]{1,0:T(8,128)(2,1)S(1)}, bf16[256,768]{1,0:T(8,128)(2,1)S(1)}, u32[]{:S(2)}, u32[]{:S(2)}) collective-permute-start(bf16[256,768]{1,0:T(8,128)(2,1)S(1)} %copy-done.35), channel_id=1, source_target_pairs={{0,3},{1,2},{2,1},{3,0},{4,7},{5,6},{6,5},{7,4},{8,11},{9,10},{10,... | collective-permute-start | bytes 1179656 | tf_op jit(solution)/shard_map/ppermute | solution.py:526
  211.2 22.4 %collective-permute-start.11 = (bf16[4,480,384]{2,1,0:T(8,128)(2,1)}, bf16[4,480,384]{2,1,0:T(8,128)(2,1)}, u32[]{:S(2)}, u32[]{:S(2)}) collective-permute-start(bf16[4,480,384]{2,1,0:T(8,128)(2,1)} %get-tuple-element.126), channel_id=1, source_target_pairs={{0,4},{4,0},{8,12},{12,8},{16,20},{20,16},{24,28},{28,24},{1,5},{5... | collective-permute-start | bytes 4423688 | tf_op jit(solution)/shard_map/ppermute | solution.py:526
  211.2 4.0 copy-start.30
  216.8 16.9 %copy-start.8 = (bf16[4,576,384]{2,1,0:T(8,128)(2,1)S(1)}, bf16[4,576,384]{2,1,0:T(8,128)(2,1)}, u32[]{:S(2)}) copy-start(bf16[4,576,384]{2,1,0:T(8,128)(2,1)} %get-tuple-element.131) | copy-start | bytes 5308420
  233.6 2.4 copy-start.14
  233.6 5.4 %copy-start.9 = (bf16[4,576,384]{2,1,0:T(8,128)(2,1)}, bf16[4,576,384]{2,1,0:T(8,128)(2,1)S(1)}, u32[]{:S(2)}) copy-start(bf16[4,576,384]{2,1,0:T(8,128)(2,1)S(1)} %collective-permute-done.10) | copy-start | bytes 5308420
  239.0 19.6 %copy-start.20 = (f32[1,3072]{1,0:T(1,128)S(1)}, f32[1,3072]{1,0:T(1,128)}, u32[]{:S(2)}) copy-start(f32[1,3072]{1,0:T(1,128)} %get-tuple-element.154) | copy-start | bytes 36868
  239.0 24.6 %copy-start.18 = (f32[16,768]{1,0:T(8,128)S(1)}, f32[16,768]{1,0:T(8,128)}, u32[]{:S(2)}) copy-start(f32[16,768]{1,0:T(8,128)} %get-tuple-element.151) | copy-start | bytes 147460
  239.0 24.6 %copy-start.19 = (f32[16,768]{1,0:T(8,128)S(1)}, f32[16,768]{1,0:T(8,128)}, u32[]{:S(2)}) copy-start(f32[16,768]{1,0:T(8,128)} %get-tuple-element.152) | copy-start | bytes 147460
  250.8 21.6 %collective-permute-start.15 = (bf16[256,768]{1,0:T(8,128)(2,1)}, bf16[256,768]{1,0:T(8,128)(2,1)S(1)}, u32[]{:S(2)}, u32[]{:S(2)}) collective-permute-start(bf16[256,768]{1,0:T(8,128)(2,1)} %get-tuple-element.145), channel_id=1, source_target_pairs={{0,1},{1,0},{2,3},{3,2},{4,5},{5,4},{6,7},{7,6},{8,9},{9,8},{10,11... | collective-permute-start | bytes 1179656 | tf_op jit(solution)/shard_map/ppermute | solution.py:526
  259.4 34.3 %collective-permute-start.13 = (bf16[2,480,384]{2,1,0:T(8,128)(2,1)}, bf16[2,480,384]{2,1,0:T(8,128)(2,1)}, u32[]{:S(2)}, u32[]{:S(2)}) collective-permute-start(bf16[2,480,384]{2,1,0:T(8,128)(2,1)} %get-tuple-element.180), channel_id=1, source_target_pairs={{0,16},{4,20},{8,24},{12,28},{16,0},{20,4},{24,8},{28,12},{1,17},{... | collective-permute-start | bytes 2211848 | tf_op jit(solution)/shard_map/ppermute | solution.py:526
  260.1 33.7 %collective-permute-start.12 = (bf16[2,576,384]{2,1,0:T(8,128)(2,1)}, bf16[2,576,384]{2,1,0:T(8,128)(2,1)}, u32[]{:S(2)}, u32[]{:S(2)}) collective-permute-start(bf16[2,576,384]{2,1,0:T(8,128)(2,1)} %fusion.1), channel_id=1, source_target_pairs={{0,8},{4,12},{8,0},{12,4},{16,24},{20,28},{24,16},{28,20},{1,9},{5... | collective-permute-start | bytes 2654216 | tf_op jit(solution)/shard_map/ppermute | solution.py:526
  261.2 30.1 %collective-permute-start.16 = (bf16[256,768]{1,0:T(8,128)(2,1)}, bf16[256,768]{1,0:T(8,128)(2,1)S(1)}, u32[]{:S(2)}, u32[]{:S(2)}) collective-permute-start(bf16[256,768]{1,0:T(8,128)(2,1)} %get-tuple-element.146), channel_id=1, source_target_pairs={{0,2},{1,3},{2,0},{3,1},{4,6},{5,7},{6,4},{7,5},{8,10},{9,11},{10,... | collective-permute-start | bytes 1179656 | tf_op jit(solution)/shard_map/ppermute | solution.py:526
  262.2 31.5 %collective-permute-start.17 = (bf16[256,768]{1,0:T(8,128)(2,1)}, bf16[256,768]{1,0:T(8,128)(2,1)}, u32[]{:S(2)}, u32[]{:S(2)}) collective-permute-start(bf16[256,768]{1,0:T(8,128)(2,1)} %get-tuple-element.147), channel_id=1, source_target_pairs={{0,3},{1,2},{2,1},{3,0},{4,7},{5,6},{6,5},{7,4},{8,11},{9,10},{10,... | collective-permute-start | bytes 1179656 | tf_op jit(solution)/shard_map/ppermute | solution.py:526
  272.4 6.2 %copy-start.33 = (bf16[256,768]{1,0:T(8,128)(2,1)}, bf16[256,768]{1,0:T(8,128)(2,1)S(1)}, u32[]{:S(2)}) copy-start(bf16[256,768]{1,0:T(8,128)(2,1)S(1)} %collective-permute-done.15.refs_1_) | copy-start | bytes 1179652
  272.4 25.5 %collective-permute-start.14 = (bf16[2,192,768]{2,1,0:T(8,128)(2,1)}, bf16[2,192,768]{2,1,0:T(8,128)(2,1)}, u32[]{:S(2)}, u32[]{:S(2)}) collective-permute-start(bf16[2,192,768]{2,1,0:T(8,128)(2,1)} %fusion.10), channel_id=1, source_target_pairs={{0,1},{1,0},{2,3},{3,2},{4,5},{5,4},{6,7},{7,6},{8,9},{9,8},{10,11... | collective-permute-start | bytes 1769480 | tf_op jit(solution)/shard_map/ppermute | solution.py:526
  292.1 11.1 %collective-permute-start.20 = (bf16[4,304,384]{2,1,0:T(8,128)(2,1)}, bf16[4,304,384]{2,1,0:T(8,128)(2,1)S(1)}, u32[]{:S(2)}, u32[]{:S(2)}) collective-permute-start(bf16[4,304,384]{2,1,0:T(8,128)(2,1)} %get-tuple-element.155), channel_id=1, source_target_pairs={{0,4},{4,0},{8,12},{12,8},{16,20},{20,16},{24,28},{28,24},{1,5},{5... | collective-permute-start | bytes 2801672 | tf_op jit(solution)/shard_map/ppermute | solution.py:526
  293.7 5.5 %copy-start.3 = (f32[2,480,384]{2,1,0:T(8,128)S(1)}, f32[2,480,384]{2,1,0:T(8,128)}, u32[]{:S(2)}) copy-start(f32[2,480,384]{2,1,0:T(8,128)} %get-tuple-element.179) | copy-start | bytes 4423684
  299.1 4.1 %copy-start.6 = (f32[2,192,768]{2,1,0:T(8,128)}, f32[2,192,768]{2,1,0:T(8,128)S(1)}, u32[]{:S(2)}) copy-start(f32[2,192,768]{2,1,0:T(8,128)S(1)} %bitcast_add_fusion) | copy-start | bytes 3538948
  299.2 4.0 %copy-start.15 = (bf16[4,304,384]{2,1,0:T(8,128)(2,1)S(1)}, bf16[4,304,384]{2,1,0:T(8,128)(2,1)}, u32[]{:S(2)}) copy-start(bf16[4,304,384]{2,1,0:T(8,128)(2,1)} %get-tuple-element.162) | copy-start | bytes 2801668
  304.5 21.7 %copy-start.4 = (f32[2,480,384]{2,1,0:T(8,128)S(1)}, f32[2,480,384]{2,1,0:T(8,128)}, u32[]{:S(2)}) copy-start(f32[2,480,384]{2,1,0:T(8,128)} %get-tuple-element.179) | copy-start | bytes 4423684
  304.5 20.4 %collective-permute-start.21 = (bf16[2,304,384]{2,1,0:T(8,128)(2,1)}, bf16[2,304,384]{2,1,0:T(8,128)(2,1)}, u32[]{:S(2)}, u32[]{:S(2)}) collective-permute-start(bf16[2,304,384]{2,1,0:T(8,128)(2,1)} %get-tuple-element.183), channel_id=1, source_target_pairs={{0,16},{4,20},{8,24},{12,28},{16,0},{20,4},{24,8},{28,12},{1,17},{... | collective-permute-start | bytes 1400840 | tf_op jit(solution)/shard_map/ppermute | solution.py:526
  304.5 20.4 %collective-permute-start.18 = (bf16[576,384]{1,0:T(8,128)(2,1)}, bf16[576,384]{1,0:T(8,128)(2,1)}, u32[]{:S(2)}, u32[]{:S(2)}) collective-permute-start(bf16[576,384]{1,0:T(8,128)(2,1)} %fusion.16), channel_id=1, source_target_pairs={{0,16},{4,20},{8,24},{12,28},{16,0},{20,4},{24,8},{28,12},{1,17},{... | collective-permute-start | bytes 1327112 | tf_op jit(solution)/shard_map/ppermute | solution.py:526
  306.5 15.1 %collective-permute-start.19 = (bf16[480,384]{1,0:T(8,128)(2,1)}, bf16[480,384]{1,0:T(8,128)(2,1)}, u32[]{:S(2)}, u32[]{:S(2)}) collective-permute-start(bf16[480,384]{1,0:T(8,128)(2,1)} %fusion.19), channel_id=1, source_target_pairs={{0,8},{4,12},{8,0},{12,4},{16,24},{20,28},{24,16},{28,20},{1,9},{5... | collective-permute-start | bytes 1105928 | tf_op jit(solution)/shard_map/ppermute | solution.py:526
  308.0 13.5 %collective-permute-start.22 = (bf16[192,768]{1,0:T(8,128)(2,1)S(1)}, bf16[192,768]{1,0:T(8,128)(2,1)}, u32[]{:S(2)}, u32[]{:S(2)}) collective-permute-start(bf16[192,768]{1,0:T(8,128)(2,1)S(1)} %fusion.20), channel_id=1, source_target_pairs={{0,2},{1,3},{2,0},{3,1},{4,6},{5,7},{6,4},{7,5},{8,10},{9,11},{10,... | collective-permute-start | bytes 884744 | tf_op jit(solution)/shard_map/ppermute | solution.py:526
  327.4 1.3 copy-start.7
  327.5 4.2 %copy-start.5 = (f32[2,304,384]{2,1,0:T(8,128)S(1)}, f32[2,304,384]{2,1,0:T(8,128)}, u32[]{:S(2)}) copy-start(f32[2,304,384]{2,1,0:T(8,128)} %get-tuple-element.184) | copy-start | bytes 2801668
  327.6 14.8 %collective-permute-start.25 = (bf16[2,264,384]{2,1,0:T(8,128)(2,1)S(1)}, bf16[2,264,384]{2,1,0:T(8,128)(2,1)S(1)}, u32[]{:S(2)}, u32[]{:S(2)}) collective-permute-start(bf16[2,264,384]{2,1,0:T(8,128)(2,1)S(1)} %fusion.17), channel_id=1, source_target_pairs={{0,1},{1,0},{2,3},{3,2},{4,5},{5,4},{6,7},{7,6},{8,9},{9,8},{10,11... | collective-permute-start | bytes 1216520 | tf_op jit(solution)/shard_map/ppermute | solution.py:526
  329.7 11.1 %collective-permute-start.24 = (bf16[192,768]{1,0:T(8,128)(2,1)S(1)}, bf16[192,768]{1,0:T(8,128)(2,1)}, u32[]{:S(2)}, u32[]{:S(2)}) collective-permute-start(bf16[192,768]{1,0:T(8,128)(2,1)S(1)} %fusion.11), channel_id=1, source_target_pairs={{0,2},{1,3},{2,0},{3,1},{4,6},{5,7},{6,4},{7,5},{8,10},{9,11},{10,... | collective-permute-start | bytes 884744 | tf_op jit(solution)/shard_map/ppermute | solution.py:526
  332.8 6.2 %collective-permute-start.23 = (bf16[304,384]{1,0:T(8,128)(2,1)S(1)}, bf16[304,384]{1,0:T(8,128)(2,1)}, u32[]{:S(2)}, u32[]{:S(2)}) collective-permute-start(bf16[304,384]{1,0:T(8,128)(2,1)S(1)} %fusion.21), channel_id=1, source_target_pairs={{0,8},{4,12},{8,0},{12,4},{16,24},{20,28},{24,16},{28,20},{1,9},{5... | collective-permute-start | bytes 700424 | tf_op jit(solution)/shard_map/ppermute | solution.py:526
  344.3 19.4 %collective-permute-start.28 = (bf16[2,192,768]{2,1,0:T(8,128)(2,1)}, bf16[2,192,768]{2,1,0:T(8,128)(2,1)}, u32[]{:S(2)}, u32[]{:S(2)}) collective-permute-start(bf16[2,192,768]{2,1,0:T(8,128)(2,1)} %pad_maximum_fusion.4), channel_id=1, source_target_pairs={{0,1},{1,0},{2,3},{3,2},{4,5},{5,4},{6,7},{7,6},{8,9},{9,8},{10,11... | collective-permute-start | bytes 1769480 | tf_op jit(solution)/shard_map/ppermute | solution.py:526
  350.0 13.4 %collective-permute-start.27 = (bf16[2,76,384]{2,1,0:T(8,128)(2,1)}, bf16[2,76,384]{2,1,0:T(8,128)(2,1)S(1)}, u32[]{:S(2)}, u32[]{:S(2)}) collective-permute-start(bf16[2,76,384]{2,1,0:T(8,128)(2,1)} %fusion.23), channel_id=1, source_target_pairs={{0,1},{1,0},{2,3},{3,2},{4,5},{5,4},{6,7},{7,6},{8,9},{9,8},{10,11... | collective-permute-start | bytes 350216 | tf_op jit(solution)/shard_map/ppermute | solution.py:526
  350.2 13.5 %copy-start.13 = (f32[2,2,76,384]{3,2,1,0:T(8,128)S(1)}, f32[2,2,76,384]{3,2,1,0:T(8,128)}, u32[]{:S(2)}) copy-start(f32[2,2,76,384]{3,2,1,0:T(8,128)} %copy-done.12) | copy-start | bytes 1400836
  350.2 13.5 %collective-permute-start.26 = (bf16[264,384]{1,0:T(8,128)(2,1)S(1)}, bf16[264,384]{1,0:T(8,128)(2,1)S(1)}, u32[]{:S(2)}, u32[]{:S(2)}) collective-permute-start(bf16[264,384]{1,0:T(8,128)(2,1)S(1)} %fusion.22), channel_id=1, source_target_pairs={{0,2},{1,3},{2,0},{3,1},{4,6},{5,7},{6,4},{7,5},{8,10},{9,11},{10,... | collective-permute-start | bytes 608264 | tf_op jit(solution)/shard_map/ppermute | solution.py:526
  363.8 6.4 %collective-permute-start.30 = (bf16[76,384]{1,0:T(8,128)(2,1)S(1)}, bf16[76,384]{1,0:T(8,128)(2,1)S(1)}, u32[]{:S(2)}, u32[]{:S(2)}) collective-permute-start(bf16[76,384]{1,0:T(8,128)(2,1)S(1)} %fusion.25), channel_id=1, source_target_pairs={{0,2},{1,3},{2,0},{3,1},{4,6},{5,7},{6,4},{7,5},{8,10},{9,11},{10,... | collective-permute-start | bytes 175112 | tf_op jit(solution)/shard_map/ppermute | solution.py:526
  367.3 8.8 %collective-permute-start.29 = (bf16[264,384]{1,0:T(8,128)(2,1)S(1)}, bf16[264,384]{1,0:T(8,128)(2,1)S(1)}, u32[]{:S(2)}, u32[]{:S(2)}) collective-permute-start(bf16[264,384]{1,0:T(8,128)(2,1)S(1)} %fusion.18), channel_id=1, source_target_pairs={{0,2},{1,3},{2,0},{3,1},{4,6},{5,7},{6,4},{7,5},{8,10},{9,11},{10,... | collective-permute-start | bytes 608264 | tf_op jit(solution)/shard_map/ppermute | solution.py:526
  376.2 10.3 %collective-permute-start.31 = (bf16[2,264,384]{2,1,0:T(8,128)(2,1)S(1)}, bf16[2,264,384]{2,1,0:T(8,128)(2,1)S(1)}, u32[]{:S(2)}, u32[]{:S(2)}) collective-permute-start(bf16[2,264,384]{2,1,0:T(8,128)(2,1)S(1)} %pad_maximum_fusion.5), channel_id=1, source_target_pairs={{0,1},{1,0},{2,3},{3,2},{4,5},{5,4},{6,7},{7,6},{8,9},{9,8},{10,11... | collective-permute-start | bytes 1216520 | tf_op jit(solution)/shard_map/ppermute | solution.py:526
  376.3 6.8 %collective-permute-start.32 = (bf16[76,384]{1,0:T(8,128)(2,1)S(1)}, bf16[76,384]{1,0:T(8,128)(2,1)S(1)}, u32[]{:S(2)}, u32[]{:S(2)}) collective-permute-start(bf16[76,384]{1,0:T(8,128)(2,1)S(1)} %fusion.24), channel_id=1, source_target_pairs={{0,2},{1,3},{2,0},{3,1},{4,6},{5,7},{6,4},{7,5},{8,10},{9,11},{10,... | collective-permute-start | bytes 175112 | tf_op jit(solution)/shard_map/ppermute | solution.py:526
  387.0 4.9 %collective-permute-start.33 = (bf16[2,76,384]{2,1,0:T(8,128)(2,1)S(1)}, bf16[2,76,384]{2,1,0:T(8,128)(2,1)S(1)}, u32[]{:S(2)}, u32[]{:S(2)}) collective-permute-start(bf16[2,76,384]{2,1,0:T(8,128)(2,1)S(1)} %pad_maximum_fusion.6), channel_id=1, source_target_pairs={{0,1},{1,0},{2,3},{3,2},{4,5},{5,4},{6,7},{7,6},{8,9},{9,8},{10,11... | collective-permute-start | bytes 350216 | tf_op jit(solution)/shard_map/ppermute | solution.py:526
  390.0 4.0 slice-start
  392.0 3.0 copy-start.1
  (12 other events, 10.3 us)
Sparse Core Ops, SparseCore 0:
  11.1 93.3 all-gather.2
  172.6 78.3 reduce-scatter.1

commit v2 on v1

--- a/solution.py
+++ b/solution.py
@@ -269,11 +269,12 @@
         bg=second.astype(BF)
         vg_ref[5:6,:]+=col(bg.astype(F32))
         acc=second
+        low_t=low.T
         for a in range(0,ff,width):
             ig=(dot_nt(bg,wback[a:a+width,:])*slope[:,a:a+width].astype(F32)).astype(BF)
             cg_ref[:,a:a+width]+=col(ig.astype(F32))
             acc=acc+dot_nt(ig,win[:,a:a+width])
-            acc_in[:,a:a+width]+=dot_tn(low,ig)
+            acc_in[:,a:a+width]+=dot_nn(low_t,ig)
             acc_back[a:a+width,:]+=dot_tn(act[:,a:a+width],bg)
         vg_ref[6:7,:]+=col(acc*hat1); vg_ref[8:9,:]+=col(acc)
         gs=norm_back(acc*vec_ref[6:7,:],hat1,inv1)
@@ -553,6 +554,11 @@
     return values
 
 
+class Held:
+    def __init__(self, got):
+        self.got = got
+
+
 class Exchange:
     def __init__(self, chunks):
         self.got = [chunks[0]] + [flip(chunks[k], "sp", k) for k in range(1, len(chunks))]
@@ -719,6 +725,7 @@
         )
         if tree:
             out_moved = Exchange(out)
+            out_two, out_rest = Held(out_moved.got[2]), Held(out_moved.got[1::2])
         else:
             outs.append(jnp.concatenate(out, axis=0))
         if tree:
@@ -739,9 +746,9 @@
             groups.append(parts)
             if tree and group == 0:
                 two = Reduction(*local_grads(me, x, parts, unit=(keep_two, send_two)), False)
-                (merged_grad,) = meet([merged_grad], [out_moved], two.first)
+                (merged_grad,) = meet([merged_grad], [out_two], two.first)
         if tree:
-            (grad_sum,) = meet([grad_sum], [one, two], parts[0])
+            (grad_sum,) = meet([grad_sum], [one, two, out_rest], parts[0])
             grad_sum = tie(grad_sum, one.advance(), two.advance())
         *input_grad, vec_three = inputs_back(me, mez, grad_sum, glob, groups, local_w)
         if tree:
@@ -784,7 +791,8 @@
         early_sum = SpSum(jnp.concatenate([one.total(), two.total()], axis=0))
         late.advance()
         ff_sum.advance()
-        out = collect(mez, out_moved.got)
+        near, far = out_rest.got
+        out = collect(mez, [out_moved.got[0], near, out_two.got, far])
         meet([], [late, ff_sum, early_sum])
         late_sum = SpSum(late.total())
         early_sum.advance()

time: 410 us -> 404 us (0.985)
  starting transfers between devices: 51.2 us -> 42.7 us
  waiting for transfers between devices: 116 us -> 121 us
    ppermute x34, starting transfers between devices: 42.7 us -> 34.2 us  [flip(): lax.ppermute(value, axis, [(index, index ^ bit) for index in range(count)])]
    ppermute x34, waiting for transfers between devices: 96.4 us -> 101 us  [flip(): lax.ppermute(value, axis, [(index, index ^ bit) for index in range(count)])]
    unnamed x83 -> x75, local copies, waits for them, and re-layouts: 10.8 us -> 8.74 us
  transfers between devices with their start and end apart: 38 -> 38, of which waited for: 22 -> 20; matrix products, arithmetic and copies ran while one was open for 8% -> 8% of each run, Pallas kernels for 26% -> 27%
where the time goes in v2:
time: 404 us; the launch traced here: 397 us
  Pallas kernels  166 us (41%)
  waiting for transfers between devices  121 us (30%)
  starting transfers between devices  42.7 us (11%)
  other arithmetic  30.1 us (7%)
  local copies, waits for them, and re-layouts  21.3 us (5%)
  between operations  15 us (4%)
    ppermute x34, waiting for transfers between devices, flip(): lax.ppermute(value, axis, [(index, index ^ bit) for index in range(count)])  101 us
    pallas_call x1, Pallas kernels, layer(): pl.pallas_call(body, grid=(steps,), in_specs=[SMEM, SMEM, full(pos.shape)...  60.4 us
    ppermute x34, starting transfers between devices, flip(): lax.ppermute(value, axis, [(index, index ^ bit) for index in range(count)])  34.2 us
    pallas_call x2, Pallas kernels, attn_bwd(): pl.pallas_call(bwd_kernel, grid=(pairs,), in_specs=[pl.BlockSpec((16, 1),...  33.5 us
    all_gather x1, waiting for transfers between devices, per_device(): ffw = [lax.all_gather(pack, 'fsdp')]  17.1 us
    pallas_call x1, Pallas kernels, attn_fwd(): pl.pallas_call(fwd_kernel, grid=(pairs,), in_specs=[pl.BlockSpec((16, 1),...  15.8 us
    pallas_call x2, Pallas kernels, local_grads(): pl.pallas_call(body, in_specs=[SMEM] + [vm] * (first - 1) + [ANY] * (0 if...  12.2 us
    pallas_call x1, Pallas kernels, inputs_back(): pl.pallas_call(body, grid=(length // RB,), in_specs=[SMEM, SMEM, blk, pl....  11.9 us
  transfers between devices with their start and end apart: 38, of which 20 were waited for; matrix products, arithmetic and copies ran while one was open for 8% of the time, Pallas kernels for 27%

profile of v2, /device:TPU:0, one launch (start us, length us, event | category | flops | bytes accessed | tf_op | source)
XLA Modules:
  0.0 396.5 jit_solution(7171072422422655770)
XLA Ops:
  8.3 2.6 pad_maximum_fusion
  12.1 3.0 collective-permute-start.1
  15.1 1.5 collective-permute-start.3
  16.6 4.9 %all-to-all-start = ((bf16[4,256,768]{2,1,0:T(8,128)(2,1)}), bf16[4,256,768]{2,1,0:T(8,128)(2,1)S(1)}, u32[]{:S(2)}, u32[]{:S(2)}) async-start(bf16[4,256,768]{2,1,0:T(8,128)(2,1)} %param.14), calls=%async_computation | async-start | bytes 3145728 | tf_op jit(solution)/shard_map/all_to_all | solution.py:663
  21.5 6.5 %collective-permute-done.1.refs_2_.refs_8_ = bf16[304,768]{1,0:T(8,128)(2,1)S(1)} collective-permute-done((bf16[304,768]{1,0:T(8,128)(2,1)S(1)}, bf16[304,768]{1,0:T(8,128)(2,1)S(1)}, u32[]{:S(2)}, u32[]{:S(2)}) %collective-permute-start.1) | collective-permute-done | bytes 466976 | tf_op jit(solution)/shard_map/ppermute | solution.py:527
  28.0 1.3 collective-permute-start.5
  30.5 21.0 %collective-permute-done.5.refs_6_.refs_12_ = bf16[304,768]{1,0:T(8,128)(2,1)} collective-permute-done((bf16[304,768]{1,0:T(8,128)(2,1)S(1)}, bf16[304,768]{1,0:T(8,128)(2,1)}, u32[]{:S(2)}, u32[]{:S(2)}) %collective-permute-start.5) | collective-permute-done | bytes 466976 | tf_op jit(solution)/shard_map/ppermute | solution.py:527
  56.4 2.7 all-to-all-done
  59.1 3.6 all-to-all-start.1
  62.8 8.8 %project.1 = (bf16[1024,768]{1,0:T(8,128)(2,1)}, bf16[1024,768]{1,0:T(8,128)(2,1)}, bf16[1024,768]{1,0:T(8,128)(2,1)}) custom-call(s32[1]{0:T(128)} %bitcast.1.me_ref, bf16[1024,768]{1,0:T(8,128)(2,1)} %bitcast.189, f32[16,768]{1,0:T(8,128)} %reshape.231.vec_ref, bf16[304,768]{1,0:T(8,128)(2,1)} %copy-done.16, bf16[304,768]{1,0:T(8,128)(2,1)} %copy-done.27, ...), custom_call_target="tpu_custom_call" | custom-call | flops 20000000000 | bytes 1048576 | tf_op jit(solution)/shard_map/project/pallas_call | solution.py:390
  71.6 15.8 %attend.1 = (bf16[1024,768]{1,0:T(8,128)(2,1)}, f32[6,8,1024]{2,1,0:T(8,128)}) custom-call(s32[16,1]{1,0:T(8,128)} %scatter.4.pos_ref, bf16[1024,768]{1,0:T(8,128)(2,1)} %get-tuple-element.100.q_ref, bf16[1024,768]{1,0:T(8,128)(2,1)} %get-tuple-element.101.k_ref, bf16[1024,768]{1,0:T(8,128)(2,1)} %get-tuple-element.102.v_ref), custom_call_target="tpu_custom_call" | custom-call | flops 20000000000 | bytes 1048576 | tf_op jit(solution)/shard_map/attend/pallas_call | solution.py:96
  87.4 17.1 %all-gather.3.cloned.1.call-done = bf16[9216,768]{1,0:T(8,128)(2,1)} async-done(((bf16[1152,768]{1,0:T(8,128)(2,1)}), bf16[9216,768]{1,0:T(8,128)(2,1)}) %all-gather.3.cloned.1.call-update) | async-done | bytes 14155792 | tf_op jit(solution)/shard_map/all_gather | solution.py:696
  104.5 6.4 %globals.1 = (bf16[16,768]{1,0:T(8,128)(2,1)}, f32[1024,64]{1,0:T(8,128)}, bf16[64,768]{1,0:T(8,128)(2,1)}, bf16[64,768]{1,0:T(8,128)(2,1)}, bf16[16,768]{1,0:T(8,128)(2,1)}, /*index=5*/bf16[16,768]{1,0:T(8,128)(2,1)}) custom-call(s32[16,1]{1,0:T(8,128)} %scatter.4.pos_ref, bf16[1024,768]{1,0:T(8,128)(2,1)} %bitcast.190, f32[16,768]{1,0:T(8,128)} %reshape.231.vec_ref, ...), custom_call_target="tpu_custom_call" | custom-call | flops 20000000000 | bytes 1048576 | tf_op jit(solution)/shard_map/globals/pallas_call | solution.py:437
  110.9 1.2 copy-done.11
  112.1 60.4 %layer.1 = (bf16[256,768]{1,0:T(8,128)(2,1)}, bf16[256,768]{1,0:T(8,128)(2,1)}, bf16[256,768]{1,0:T(8,128)(2,1)}, bf16[256,768]{1,0:T(8,128)(2,1)}, f32[1024,768...) custom-call(s32[1]{0:T(128)} %bitcast.1.me_ref, ...), custom_call_target="tpu_custom_call" | custom-call | flops 20000000000 | bytes 1048576 | tf_op jit(solution)/shard_map/layer/pallas_call | solution.py:317
  172.5 10.9 %globals_back.1 = (bf16[1024,256]{1,0:T(8,128)(2,1)}, bf16[256,768]{1,0:T(8,128)(2,1)}, bf16[4,576,384]{2,1,0:T(8,128)(2,1)}, bf16[4,576,384]{2,1,0:T(8,128)(2,1)}, f32[16,768]{1,0:T(8,128)}) custom-call(s32[1]{0:T(128)} %bitcast.1.me_ref, s32[16,1]{1,0:T(8,128)} %scatter.4.pos_ref, bf16[1024,768]{1,0:T(8,128)(2,1)} %bitcast.192, ...), custom_call_target="tpu_custom_call" | custom-call | flops 20000000000 | bytes 1048576 | tf_op jit(solution)/shard_map/globals_back/pallas_call | solution.py:492
  183.8 2.5 collective-permute-start.11
  186.3 16.6 %attend_back.2 = (bf16[1024,384]{1,0:T(8,128)(2,1)}, bf16[1024,384]{1,0:T(8,128)(2,1)}, bf16[1024,384]{1,0:T(8,128)(2,1)}) custom-call(s32[16,1]{1,0:T(8,128)} %scatter.4.pos_ref, bf16[1024,768]{1,0:T(8,128)(2,1)} %get-tuple-element.100.q_ref, bf16[1024,768]{1,0:T(8,128)(2,1)} %get-tuple-element.101.k_ref, bf16[1024,768]{1,0:T(8,128)(2,1)} %get-tuple-element.102.v_ref, ...), custom_call_target="tpu_custom_call" | custom-call | flops 20000000000 | bytes 1048576 | tf_op jit(solution)/shard_map/attend_back/pallas_call | solution.py:164
  202.9 6.0 %local_grads.2 = (bf16[4,480,384]{2,1,0:T(8,128)(2,1)}, bf16[4,480,384]{2,1,0:T(8,128)(2,1)}) custom-call(s32[1]{0:T(128)} %bitcast.1.me_ref, bf16[1024,768]{1,0:T(8,128)(2,1)} %bitcast.193, bf16[1024,384]{1,0:T(8,128)(2,1)} %get-tuple-element.118.refs_0_, ...), custom_call_target="tpu_custom_call", output_to_operand_aliasing={{0}: (5, {}), {1}: (6, {})} | custom-call | flops 20000000000 | bytes 1048576 | tf_op jit(solution)/shard_map/local_grads/pallas_call | solution.py:354
  209.0 1.8 collective-permute-start.10
  210.9 16.9 %attend_back.3 = (bf16[1024,384]{1,0:T(8,128)(2,1)}, bf16[1024,384]{1,0:T(8,128)(2,1)}, bf16[1024,384]{1,0:T(8,128)(2,1)}) custom-call(s32[16,1]{1,0:T(8,128)} %scatter.4.pos_ref, bf16[1024,768]{1,0:T(8,128)(2,1)} %get-tuple-element.100.q_ref, bf16[1024,768]{1,0:T(8,128)(2,1)} %get-tuple-element.101.k_ref, bf16[1024,768]{1,0:T(8,128)(2,1)} %get-tuple-element.102.v_ref, ...), custom_call_target="tpu_custom_call" | custom-call | flops 20000000000 | bytes 1048576 | tf_op jit(solution)/shard_map/attend_back/pallas_call | solution.py:164
  227.8 3.0 collective-permute-done.9.refs_1_
  230.8 1.3 fusion.1
  232.1 3.1 convert_add_fusion.1
  235.3 11.9 %inputs_back.1 = (bf16[256,768]{1,0:T(8,128)(2,1)}, bf16[256,768]{1,0:T(8,128)(2,1)}, bf16[256,768]{1,0:T(8,128)(2,1)}, bf16[256,768]{1,0:T(8,128)(2,1)}, f32[16,768]{1,0:T(8,128)}) custom-call(s32[1]{0:T(128)} %bitcast.1.me_ref, s32[1]{0:T(128)} %bitcast.mez_ref, f32[1024,768]{1,0:T(8,128)} %get-tuple-element.137.gs_ref, ...), custom_call_target="tpu_custom_call" | custom-call | flops 20000000000 | bytes 1048576 | tf_op jit(solution)/shard_map/inputs_back/pallas_call | solution.py:519
  250.1 1.3 collective-permute-start.12
  251.4 2.0 collective-permute-start.16
  253.4 2.2 collective-permute-start.17
  255.6 1.4 pad_add_fusion.refs_3_
  257.0 1.5 convert.6
  259.4 3.4 collective-permute-done.15.refs_1_
  262.8 6.2 %local_grads.3 = (bf16[4,304,384]{2,1,0:T(8,128)(2,1)}, bf16[4,304,384]{2,1,0:T(8,128)(2,1)}) custom-call(s32[1]{0:T(128)} %bitcast.1.me_ref, bf16[1024,768]{1,0:T(8,128)(2,1)} %bitcast.194, bf16[1024,384]{1,0:T(8,128)(2,1)} %get-tuple-element.128.refs_3_.refs_0_, bf16[1024,384]{1,0:T(8,128)(2,1)} %get-tuple-element.140.refs_4_.refs_1_, ...), custom_call_target="tpu_custom_call" | custom-call | flops 20000000000 | bytes 1048576 | tf_op jit(solution)/shard_map/local_grads/pallas_call | solution.py:354
  269.0 12.5 %collective-permute-done.16.refs_2_ = bf16[256,768]{1,0:T(8,128)(2,1)S(1)} collective-permute-done((bf16[256,768]{1,0:T(8,128)(2,1)}, bf16[256,768]{1,0:T(8,128)(2,1)S(1)}, u32[]{:S(2)}, u32[]{:S(2)}) %collective-permute-start.16) | collective-permute-done | bytes 393248 | tf_op jit(solution)/shard_map/ppermute | solution.py:527
  282.2 1.6 convert_add_fusion
  283.8 5.8 %collective-permute-done.14 = bf16[2,192,768]{2,1,0:T(8,128)(2,1)} collective-permute-done((bf16[2,192,768]{2,1,0:T(8,128)(2,1)}, bf16[2,192,768]{2,1,0:T(8,128)(2,1)}, u32[]{:S(2)}, u32[]{:S(2)}) %collective-permute-start.14) | collective-permute-done | bytes 589856 | tf_op jit(solution)/shard_map/ppermute | solution.py:527
  289.7 1.2 bitcast_add_fusion
  290.9 2.2 fusion.19
  293.1 1.9 fusion.16
  294.9 1.3 add_convert_fusion.2
  296.2 1.8 collective-permute-start.21
  298.3 1.8 collective-permute-start.19
  300.1 13.7 %collective-permute-done.22 = bf16[192,768]{1,0:T(8,128)(2,1)} collective-permute-done((bf16[192,768]{1,0:T(8,128)(2,1)S(1)}, bf16[192,768]{1,0:T(8,128)(2,1)}, u32[]{:S(2)}, u32[]{:S(2)}) %collective-permute-start.22) | collective-permute-done | bytes 294944 | tf_op jit(solution)/shard_map/ppermute | solution.py:527
  313.7 3.7 collective-permute-done.18
  317.4 1.3 fusion.6
  318.7 1.2 fusion.8
  322.2 1.9 collective-permute-start.24
  325.1 1.7 collective-permute-start.23
  326.8 3.3 collect.2
  330.1 1.2 collective-permute-done.23
  331.3 5.1 %collective-permute-done.24 = bf16[192,768]{1,0:T(8,128)(2,1)} collective-permute-done((bf16[192,768]{1,0:T(8,128)(2,1)S(1)}, bf16[192,768]{1,0:T(8,128)(2,1)}, u32[]{:S(2)}, u32[]{:S(2)}) %collective-permute-start.24) | collective-permute-done | bytes 294944 | tf_op jit(solution)/shard_map/ppermute | solution.py:527
  338.9 1.9 fusion.14
  342.6 1.5 collective-permute-start.27
  345.1 3.0 collect.3
  348.2 8.5 %collective-permute-done.27 = bf16[2,76,384]{2,1,0:T(8,128)(2,1)S(1)} collective-permute-done((bf16[2,76,384]{2,1,0:T(8,128)(2,1)}, bf16[2,76,384]{2,1,0:T(8,128)(2,1)S(1)}, u32[]{:S(2)}, u32[]{:S(2)}) %collective-permute-start.27) | collective-permute-done | bytes 116768 | tf_op jit(solution)/shard_map/ppermute | solution.py:527
  356.8 3.2 collective-permute-start.30
  360.1 1.1 select_bitcast_fusion.1
  361.4 1.5 collective-permute-done.30
  362.9 6.4 %collective-permute-done.29 = bf16[264,384]{1,0:T(8,128)(2,1)S(1)} collective-permute-done((bf16[264,384]{1,0:T(8,128)(2,1)S(1)}, bf16[264,384]{1,0:T(8,128)(2,1)S(1)}, u32[]{:S(2)}, u32[]{:S(2)}) %collective-permute-start.29) | collective-permute-done | bytes 202784 | tf_op jit(solution)/shard_map/ppermute | solution.py:527
  369.5 2.4 collective-permute-start.32
  371.9 1.2 fusion.35
  373.9 1.2 copy.52
  375.1 3.6 collective-permute-done.32
  378.7 2.2 collective-permute-done.31
  384.4 2.0 collective-permute-done.33
  (178 shorter events, 29.8 us)
Async XLA Ops:
  7.2 22.2 %copy-start = (s32[4,4]{1,0:T(4,128)S(1)}, s32[4,4]{1,0:T(4,128)}, u32[]{:S(2)}) copy-start(s32[4,4]{1,0:T(4,128)} %param.15) | copy-start | bytes 196
  7.2 97.3 %all-gather.3.cloned.1.call-start = ((), (), s32[]{:S(2)}) async-start(), calls=%async_computation.4 | async-start | bytes 15925248 | tf_op jit(solution)/shard_map/all_gather | solution.py:696
  12.1 42.3 %copy-start.16 = (bf16[304,768]{1,0:T(8,128)(2,1)}, bf16[304,768]{1,0:T(8,128)(2,1)S(1)}, u32[]{:S(2)}) copy-start(bf16[304,768]{1,0:T(8,128)(2,1)S(1)} %fusion.12.refs_0_.refs_6_) | copy-start | bytes 1400836
  12.1 16.0 %collective-permute-start.1 = (bf16[304,768]{1,0:T(8,128)(2,1)S(1)}, bf16[304,768]{1,0:T(8,128)(2,1)S(1)}, u32[]{:S(2)}, u32[]{:S(2)}) collective-permute-start(bf16[304,768]{1,0:T(8,128)(2,1)S(1)} %fusion.12.refs_0_.refs_6_), channel_id=1, source_target_pairs={{0,8},{4,12},{8,0},{12,4},{16,24},{20,28},{24,16},{28,20},{1,9},{5... | collective-permute-start | bytes 1400840 | tf_op jit(solution)/shard_map/ppermute | solution.py:527
  15.1 15.4 %collective-permute-start.3 = (bf16[304,768]{1,0:T(8,128)(2,1)S(1)}, bf16[304,768]{1,0:T(8,128)(2,1)S(1)}, u32[]{:S(2)}, u32[]{:S(2)}) collective-permute-start(bf16[304,768]{1,0:T(8,128)(2,1)S(1)} %fusion.12.refs_0_.refs_6_), channel_id=1, source_target_pairs={{0,16},{4,20},{8,24},{12,28},{16,0},{20,4},{24,8},{28,12},{1,17},{... | collective-permute-start | bytes 1400840 | tf_op jit(solution)/shard_map/ppermute | solution.py:527
  16.6 13.9 %collective-permute-start = (bf16[304,768]{1,0:T(8,128)(2,1)S(1)}, bf16[304,768]{1,0:T(8,128)(2,1)S(1)}, u32[]{:S(2)}, u32[]{:S(2)}) collective-permute-start(bf16[304,768]{1,0:T(8,128)(2,1)S(1)} %fusion.12.refs_0_.refs_6_), channel_id=1, source_target_pairs={{0,4},{4,0},{8,12},{12,8},{16,20},{20,16},{24,28},{28,24},{1,5},{5... | collective-permute-start | bytes 1400840 | tf_op jit(solution)/shard_map/ppermute | solution.py:527
  16.6 42.5 %all-to-all-start = ((bf16[4,256,768]{2,1,0:T(8,128)(2,1)}), bf16[4,256,768]{2,1,0:T(8,128)(2,1)S(1)}, u32[]{:S(2)}, u32[]{:S(2)}) async-start(bf16[4,256,768]{2,1,0:T(8,128)(2,1)} %param.14), calls=%async_computation | async-start | bytes 3145728 | tf_op jit(solution)/shard_map/all_to_all | solution.py:663
  28.0 31.1 %copy-start.25 = (bf16[304,768]{1,0:T(8,128)(2,1)}, bf16[304,768]{1,0:T(8,128)(2,1)S(1)}, u32[]{:S(2)}) copy-start(bf16[304,768]{1,0:T(8,128)(2,1)S(1)} %collective-permute-done.1.refs_2_.refs_8_) | copy-start | bytes 1400836
  28.0 23.5 %collective-permute-start.2 = (bf16[304,768]{1,0:T(8,128)(2,1)S(1)}, bf16[304,768]{1,0:T(8,128)(2,1)}, u32[]{:S(2)}, u32[]{:S(2)}) collective-permute-start(bf16[304,768]{1,0:T(8,128)(2,1)S(1)} %collective-permute-done.1.refs_2_.refs_8_), channel_id=1, source_target_pairs={{0,4},{4,0},{8,12},{12,8},{16,20},{20,16},{24,28},{28,24},{1,5},{5... | collective-permute-start | bytes 1400840 | tf_op jit(solution)/shard_map/ppermute | solution.py:527
  28.0 23.5 %collective-permute-start.5 = (bf16[304,768]{1,0:T(8,128)(2,1)S(1)}, bf16[304,768]{1,0:T(8,128)(2,1)}, u32[]{:S(2)}, u32[]{:S(2)}) collective-permute-start(bf16[304,768]{1,0:T(8,128)(2,1)S(1)} %collective-permute-done.1.refs_2_.refs_8_), channel_id=1, source_target_pairs={{0,16},{4,20},{8,24},{12,28},{16,0},{20,4},{24,8},{28,12},{1,17},{... | collective-permute-start | bytes 1400840 | tf_op jit(solution)/shard_map/ppermute | solution.py:527
  30.5 28.6 %copy-start.26 = (bf16[304,768]{1,0:T(8,128)(2,1)}, bf16[304,768]{1,0:T(8,128)(2,1)S(1)}, u32[]{:S(2)}) copy-start(bf16[304,768]{1,0:T(8,128)(2,1)S(1)} %collective-permute-done.3.refs_4_.refs_10_) | copy-start | bytes 1400836
  30.5 21.8 %collective-permute-start.4 = (bf16[304,768]{1,0:T(8,128)(2,1)S(1)}, bf16[304,768]{1,0:T(8,128)(2,1)S(1)}, u32[]{:S(2)}, u32[]{:S(2)}) collective-permute-start(bf16[304,768]{1,0:T(8,128)(2,1)S(1)} %collective-permute-done.3.refs_4_.refs_10_), channel_id=1, source_target_pairs={{0,4},{4,0},{8,12},{12,8},{16,20},{20,16},{24,28},{28,24},{1,5},{5... | collective-permute-start | bytes 1400840 | tf_op jit(solution)/shard_map/ppermute | solution.py:527
  30.5 28.6 %copy-start.27 = (bf16[304,768]{1,0:T(8,128)(2,1)}, bf16[304,768]{1,0:T(8,128)(2,1)S(1)}, u32[]{:S(2)}) copy-start(bf16[304,768]{1,0:T(8,128)(2,1)S(1)} %collective-permute-done.refs_1_.refs_7_) | copy-start | bytes 1400836
  51.5 2.0 collective-permute-start.6
  52.2 1.3 copy-start.28
  59.1 3.6 copy-start.10
  59.1 51.8 %all-to-all-start.1 = ((bf16[4,256,768]{2,1,0:T(8,128)(2,1)}), bf16[4,256,768]{2,1,0:T(8,128)(2,1)S(1)}, u32[]{:S(2)}, u32[]{:S(2)}) async-start(bf16[4,256,768]{2,1,0:T(8,128)(2,1)} %param.25), calls=%async_computation.1 | async-start | bytes 3145728 | tf_op jit(solution)/shard_map/all_to_all | solution.py:663
  62.7 194.3 %reduce-scatter.2.cloned.1.call-start = ((), (), s32[]{:S(2)}) async-start(), calls=%async_computation.3 | async-start | bytes 10616832 | tf_op jit(solution)/shard_map/reduce_scatter | solution.py:732
  110.9 1.2 copy-start.11
  183.5 47.3 %collective-permute-start.7 = (bf16[4,576,384]{2,1,0:T(8,128)(2,1)}, bf16[4,576,384]{2,1,0:T(8,128)(2,1)S(1)}, u32[]{:S(2)}, u32[]{:S(2)}) collective-permute-start(bf16[4,576,384]{2,1,0:T(8,128)(2,1)} %get-tuple-element.115), channel_id=1, source_target_pairs={{0,4},{4,0},{8,12},{12,8},{16,20},{20,16},{24,28},{28,24},{1,5},{5... | collective-permute-start | bytes 5308424 | tf_op jit(solution)/shard_map/ppermute | solution.py:527
  183.8 27.1 %collective-permute-start.11 = (bf16[256,768]{1,0:T(8,128)(2,1)}, bf16[256,768]{1,0:T(8,128)(2,1)S(1)}, u32[]{:S(2)}, u32[]{:S(2)}) collective-permute-start(bf16[256,768]{1,0:T(8,128)(2,1)} %get-tuple-element.126), channel_id=1, source_target_pairs={{0,2},{1,3},{2,0},{3,1},{4,6},{5,7},{6,4},{7,5},{8,10},{9,11},{10,... | collective-permute-start | bytes 1179656 | tf_op jit(solution)/shard_map/ppermute | solution.py:527
  208.9 21.9 %collective-permute-start.8 = (bf16[4,480,384]{2,1,0:T(8,128)(2,1)}, bf16[4,480,384]{2,1,0:T(8,128)(2,1)}, u32[]{:S(2)}, u32[]{:S(2)}) collective-permute-start(bf16[4,480,384]{2,1,0:T(8,128)(2,1)} %get-tuple-element.123), channel_id=1, source_target_pairs={{0,4},{4,0},{8,12},{12,8},{16,20},{20,16},{24,28},{28,24},{1,5},{5... | collective-permute-start | bytes 4423688 | tf_op jit(solution)/shard_map/ppermute | solution.py:527
  209.0 18.8 %collective-permute-start.10 = (bf16[256,768]{1,0:T(8,128)(2,1)}, bf16[256,768]{1,0:T(8,128)(2,1)}, u32[]{:S(2)}, u32[]{:S(2)}) collective-permute-start(bf16[256,768]{1,0:T(8,128)(2,1)} %get-tuple-element.125), channel_id=1, source_target_pairs={{0,3},{1,2},{2,1},{3,0},{4,7},{5,6},{6,5},{7,4},{8,11},{9,10},{10,... | collective-permute-start | bytes 1179656 | tf_op jit(solution)/shard_map/ppermute | solution.py:527
  210.8 19.9 %copy-start.8 = (bf16[4,576,384]{2,1,0:T(8,128)(2,1)S(1)}, bf16[4,576,384]{2,1,0:T(8,128)(2,1)}, u32[]{:S(2)}) copy-start(bf16[4,576,384]{2,1,0:T(8,128)(2,1)} %get-tuple-element.132) | copy-start | bytes 5308420
  210.9 19.9 %collective-permute-start.9 = (bf16[256,768]{1,0:T(8,128)(2,1)}, bf16[256,768]{1,0:T(8,128)(2,1)}, u32[]{:S(2)}, u32[]{:S(2)}) collective-permute-start(bf16[256,768]{1,0:T(8,128)(2,1)} %get-tuple-element.124), channel_id=1, source_target_pairs={{0,1},{1,0},{2,3},{3,2},{4,5},{5,4},{6,7},{7,6},{8,9},{9,8},{10,11... | collective-permute-start | bytes 1179656 | tf_op jit(solution)/shard_map/ppermute | solution.py:527
  210.9 16.9 %copy-start.30 = (bf16[256,768]{1,0:T(8,128)(2,1)}, bf16[256,768]{1,0:T(8,128)(2,1)S(1)}, u32[]{:S(2)}) copy-start(bf16[256,768]{1,0:T(8,128)(2,1)S(1)} %collective-permute-done.11.refs_2_) | copy-start | bytes 1179652
  227.8 4.3 %copy-start.14 = (bf16[4,480,384]{2,1,0:T(8,128)(2,1)S(1)}, bf16[4,480,384]{2,1,0:T(8,128)(2,1)}, u32[]{:S(2)}) copy-start(bf16[4,480,384]{2,1,0:T(8,128)(2,1)} %get-tuple-element.134) | copy-start | bytes 4423684
  230.8 4.5 %copy-start.9 = (bf16[4,576,384]{2,1,0:T(8,128)(2,1)}, bf16[4,576,384]{2,1,0:T(8,128)(2,1)S(1)}, u32[]{:S(2)}) copy-start(bf16[4,576,384]{2,1,0:T(8,128)(2,1)S(1)} %collective-permute-done.7) | copy-start | bytes 5308420
  235.2 13.4 %copy-start.20 = (f32[1,3072]{1,0:T(1,128)S(1)}, f32[1,3072]{1,0:T(1,128)}, u32[]{:S(2)}) copy-start(f32[1,3072]{1,0:T(1,128)} %get-tuple-element.152) | copy-start | bytes 36868
  235.2 20.3 %copy-start.18 = (f32[16,768]{1,0:T(8,128)S(1)}, f32[16,768]{1,0:T(8,128)}, u32[]{:S(2)}) copy-start(f32[16,768]{1,0:T(8,128)} %get-tuple-element.149) | copy-start | bytes 147460
  235.2 20.3 %copy-start.19 = (f32[16,768]{1,0:T(8,128)S(1)}, f32[16,768]{1,0:T(8,128)}, u32[]{:S(2)}) copy-start(f32[16,768]{1,0:T(8,128)} %get-tuple-element.150) | copy-start | bytes 147460
  247.1 15.6 %collective-permute-start.15 = (bf16[256,768]{1,0:T(8,128)(2,1)}, bf16[256,768]{1,0:T(8,128)(2,1)S(1)}, u32[]{:S(2)}, u32[]{:S(2)}) collective-permute-start(bf16[256,768]{1,0:T(8,128)(2,1)} %get-tuple-element.143), channel_id=1, source_target_pairs={{0,1},{1,0},{2,3},{3,2},{4,5},{5,4},{6,7},{7,6},{8,9},{9,8},{10,11... | collective-permute-start | bytes 1179656 | tf_op jit(solution)/shard_map/ppermute | solution.py:527
  249.5 34.4 %collective-permute-start.13 = (bf16[2,480,384]{2,1,0:T(8,128)(2,1)}, bf16[2,480,384]{2,1,0:T(8,128)(2,1)}, u32[]{:S(2)}, u32[]{:S(2)}) collective-permute-start(bf16[2,480,384]{2,1,0:T(8,128)(2,1)} %get-tuple-element.178), channel_id=1, source_target_pairs={{0,16},{4,20},{8,24},{12,28},{16,0},{20,4},{24,8},{28,12},{1,17},{... | collective-permute-start | bytes 2211848 | tf_op jit(solution)/shard_map/ppermute | solution.py:527
  250.1 33.8 %collective-permute-start.12 = (bf16[2,576,384]{2,1,0:T(8,128)(2,1)}, bf16[2,576,384]{2,1,0:T(8,128)(2,1)}, u32[]{:S(2)}, u32[]{:S(2)}) collective-permute-start(bf16[2,576,384]{2,1,0:T(8,128)(2,1)} %fusion.1), channel_id=1, source_target_pairs={{0,8},{4,12},{8,0},{12,4},{16,24},{20,28},{24,16},{28,20},{1,9},{5... | collective-permute-start | bytes 2654216 | tf_op jit(solution)/shard_map/ppermute | solution.py:527
  251.4 30.1 %collective-permute-start.16 = (bf16[256,768]{1,0:T(8,128)(2,1)}, bf16[256,768]{1,0:T(8,128)(2,1)S(1)}, u32[]{:S(2)}, u32[]{:S(2)}) collective-permute-start(bf16[256,768]{1,0:T(8,128)(2,1)} %get-tuple-element.144), channel_id=1, source_target_pairs={{0,2},{1,3},{2,0},{3,1},{4,6},{5,7},{6,4},{7,5},{8,10},{9,11},{10,... | collective-permute-start | bytes 1179656 | tf_op jit(solution)/shard_map/ppermute | solution.py:527
  253.4 30.4 %collective-permute-start.17 = (bf16[256,768]{1,0:T(8,128)(2,1)}, bf16[256,768]{1,0:T(8,128)(2,1)}, u32[]{:S(2)}, u32[]{:S(2)}) collective-permute-start(bf16[256,768]{1,0:T(8,128)(2,1)} %get-tuple-element.145), channel_id=1, source_target_pairs={{0,3},{1,2},{2,1},{3,0},{4,7},{5,6},{6,5},{7,4},{8,11},{9,10},{10,... | collective-permute-start | bytes 1179656 | tf_op jit(solution)/shard_map/ppermute | solution.py:527
  262.8 6.2 %copy-start.31 = (bf16[256,768]{1,0:T(8,128)(2,1)}, bf16[256,768]{1,0:T(8,128)(2,1)S(1)}, u32[]{:S(2)}) copy-start(bf16[256,768]{1,0:T(8,128)(2,1)S(1)} %collective-permute-done.15.refs_1_) | copy-start | bytes 1179652
  262.8 26.9 %collective-permute-start.14 = (bf16[2,192,768]{2,1,0:T(8,128)(2,1)}, bf16[2,192,768]{2,1,0:T(8,128)(2,1)}, u32[]{:S(2)}, u32[]{:S(2)}) collective-permute-start(bf16[2,192,768]{2,1,0:T(8,128)(2,1)} %fusion.10), channel_id=1, source_target_pairs={{0,1},{1,0},{2,3},{3,2},{4,5},{5,4},{6,7},{7,6},{8,9},{9,8},{10,11... | collective-permute-start | bytes 1769480 | tf_op jit(solution)/shard_map/ppermute | solution.py:527
  282.2 12.7 %collective-permute-start.20 = (bf16[4,304,384]{2,1,0:T(8,128)(2,1)}, bf16[4,304,384]{2,1,0:T(8,128)(2,1)S(1)}, u32[]{:S(2)}, u32[]{:S(2)}) collective-permute-start(bf16[4,304,384]{2,1,0:T(8,128)(2,1)} %get-tuple-element.153), channel_id=1, source_target_pairs={{0,4},{4,0},{8,12},{12,8},{16,20},{20,16},{24,28},{28,24},{1,5},{5... | collective-permute-start | bytes 2801672 | tf_op jit(solution)/shard_map/ppermute | solution.py:527
  283.8 7.1 %copy-start.3 = (f32[2,480,384]{2,1,0:T(8,128)S(1)}, f32[2,480,384]{2,1,0:T(8,128)}, u32[]{:S(2)}) copy-start(f32[2,480,384]{2,1,0:T(8,128)} %get-tuple-element.177) | copy-start | bytes 4423684
  290.8 4.1 %copy-start.6 = (f32[2,192,768]{2,1,0:T(8,128)}, f32[2,192,768]{2,1,0:T(8,128)S(1)}, u32[]{:S(2)}) copy-start(f32[2,192,768]{2,1,0:T(8,128)S(1)} %bitcast_add_fusion) | copy-start | bytes 3538948
  290.9 4.0 %copy-start.15 = (bf16[4,304,384]{2,1,0:T(8,128)(2,1)S(1)}, bf16[4,304,384]{2,1,0:T(8,128)(2,1)}, u32[]{:S(2)}) copy-start(bf16[4,304,384]{2,1,0:T(8,128)(2,1)} %get-tuple-element.160) | copy-start | bytes 2801668
  296.2 22.5 %copy-start.4 = (f32[2,480,384]{2,1,0:T(8,128)S(1)}, f32[2,480,384]{2,1,0:T(8,128)}, u32[]{:S(2)}) copy-start(f32[2,480,384]{2,1,0:T(8,128)} %get-tuple-element.177) | copy-start | bytes 4423684
  296.2 21.2 %collective-permute-start.21 = (bf16[2,304,384]{2,1,0:T(8,128)(2,1)}, bf16[2,304,384]{2,1,0:T(8,128)(2,1)}, u32[]{:S(2)}, u32[]{:S(2)}) collective-permute-start(bf16[2,304,384]{2,1,0:T(8,128)(2,1)} %get-tuple-element.181), channel_id=1, source_target_pairs={{0,16},{4,20},{8,24},{12,28},{16,0},{20,4},{24,8},{28,12},{1,17},{... | collective-permute-start | bytes 1400840 | tf_op jit(solution)/shard_map/ppermute | solution.py:527
  298.0 19.4 %collective-permute-start.18 = (bf16[576,384]{1,0:T(8,128)(2,1)}, bf16[576,384]{1,0:T(8,128)(2,1)}, u32[]{:S(2)}, u32[]{:S(2)}) collective-permute-start(bf16[576,384]{1,0:T(8,128)(2,1)} %fusion.16), channel_id=1, source_target_pairs={{0,16},{4,20},{8,24},{12,28},{16,0},{20,4},{24,8},{28,12},{1,17},{... | collective-permute-start | bytes 1327112 | tf_op jit(solution)/shard_map/ppermute | solution.py:527
  298.3 15.5 %collective-permute-start.19 = (bf16[480,384]{1,0:T(8,128)(2,1)}, bf16[480,384]{1,0:T(8,128)(2,1)}, u32[]{:S(2)}, u32[]{:S(2)}) collective-permute-start(bf16[480,384]{1,0:T(8,128)(2,1)} %fusion.19), channel_id=1, source_target_pairs={{0,8},{4,12},{8,0},{12,4},{16,24},{20,28},{24,16},{28,20},{1,9},{5... | collective-permute-start | bytes 1105928 | tf_op jit(solution)/shard_map/ppermute | solution.py:527
  300.0 13.7 %collective-permute-start.22 = (bf16[192,768]{1,0:T(8,128)(2,1)S(1)}, bf16[192,768]{1,0:T(8,128)(2,1)}, u32[]{:S(2)}, u32[]{:S(2)}) collective-permute-start(bf16[192,768]{1,0:T(8,128)(2,1)S(1)} %fusion.20), channel_id=1, source_target_pairs={{0,2},{1,3},{2,0},{3,1},{4,6},{5,7},{6,4},{7,5},{8,10},{9,11},{10,... | collective-permute-start | bytes 884744 | tf_op jit(solution)/shard_map/ppermute | solution.py:527
  319.9 1.3 copy-start.7
  320.1 4.1 %copy-start.5 = (f32[2,304,384]{2,1,0:T(8,128)S(1)}, f32[2,304,384]{2,1,0:T(8,128)}, u32[]{:S(2)}) copy-start(f32[2,304,384]{2,1,0:T(8,128)} %get-tuple-element.182) | copy-start | bytes 2801668
  320.1 16.3 %collective-permute-start.25 = (bf16[2,264,384]{2,1,0:T(8,128)(2,1)S(1)}, bf16[2,264,384]{2,1,0:T(8,128)(2,1)S(1)}, u32[]{:S(2)}, u32[]{:S(2)}) collective-permute-start(bf16[2,264,384]{2,1,0:T(8,128)(2,1)S(1)} %fusion.17), channel_id=1, source_target_pairs={{0,1},{1,0},{2,3},{3,2},{4,5},{5,4},{6,7},{7,6},{8,9},{9,8},{10,11... | collective-permute-start | bytes 1216520 | tf_op jit(solution)/shard_map/ppermute | solution.py:527
  322.2 14.2 %collective-permute-start.24 = (bf16[192,768]{1,0:T(8,128)(2,1)S(1)}, bf16[192,768]{1,0:T(8,128)(2,1)}, u32[]{:S(2)}, u32[]{:S(2)}) collective-permute-start(bf16[192,768]{1,0:T(8,128)(2,1)S(1)} %fusion.11), channel_id=1, source_target_pairs={{0,2},{1,3},{2,0},{3,1},{4,6},{5,7},{6,4},{7,5},{8,10},{9,11},{10,... | collective-permute-start | bytes 884744 | tf_op jit(solution)/shard_map/ppermute | solution.py:527
  325.1 6.2 %collective-permute-start.23 = (bf16[304,384]{1,0:T(8,128)(2,1)S(1)}, bf16[304,384]{1,0:T(8,128)(2,1)}, u32[]{:S(2)}, u32[]{:S(2)}) collective-permute-start(bf16[304,384]{1,0:T(8,128)(2,1)S(1)} %fusion.21), channel_id=1, source_target_pairs={{0,8},{4,12},{8,0},{12,4},{16,24},{20,28},{24,16},{28,20},{1,9},{5... | collective-permute-start | bytes 700424 | tf_op jit(solution)/shard_map/ppermute | solution.py:527
  338.3 18.4 %collective-permute-start.28 = (bf16[2,192,768]{2,1,0:T(8,128)(2,1)}, bf16[2,192,768]{2,1,0:T(8,128)(2,1)}, u32[]{:S(2)}, u32[]{:S(2)}) collective-permute-start(bf16[2,192,768]{2,1,0:T(8,128)(2,1)} %pad_maximum_fusion.4), channel_id=1, source_target_pairs={{0,1},{1,0},{2,3},{3,2},{4,5},{5,4},{6,7},{7,6},{8,9},{9,8},{10,11... | collective-permute-start | bytes 1769480 | tf_op jit(solution)/shard_map/ppermute | solution.py:527
  342.6 14.1 %collective-permute-start.27 = (bf16[2,76,384]{2,1,0:T(8,128)(2,1)}, bf16[2,76,384]{2,1,0:T(8,128)(2,1)S(1)}, u32[]{:S(2)}, u32[]{:S(2)}) collective-permute-start(bf16[2,76,384]{2,1,0:T(8,128)(2,1)} %fusion.23), channel_id=1, source_target_pairs={{0,1},{1,0},{2,3},{3,2},{4,5},{5,4},{6,7},{7,6},{8,9},{9,8},{10,11... | collective-permute-start | bytes 350216 | tf_op jit(solution)/shard_map/ppermute | solution.py:527
  344.3 12.5 %copy-start.13 = (f32[2,2,76,384]{3,2,1,0:T(8,128)S(1)}, f32[2,2,76,384]{3,2,1,0:T(8,128)}, u32[]{:S(2)}) copy-start(f32[2,2,76,384]{3,2,1,0:T(8,128)} %copy-done.12) | copy-start | bytes 1400836
  344.3 12.5 %collective-permute-start.26 = (bf16[264,384]{1,0:T(8,128)(2,1)S(1)}, bf16[264,384]{1,0:T(8,128)(2,1)S(1)}, u32[]{:S(2)}, u32[]{:S(2)}) collective-permute-start(bf16[264,384]{1,0:T(8,128)(2,1)S(1)} %fusion.22), channel_id=1, source_target_pairs={{0,2},{1,3},{2,0},{3,1},{4,6},{5,7},{6,4},{7,5},{8,10},{9,11},{10,... | collective-permute-start | bytes 608264 | tf_op jit(solution)/shard_map/ppermute | solution.py:527
  356.8 6.1 %collective-permute-start.30 = (bf16[76,384]{1,0:T(8,128)(2,1)S(1)}, bf16[76,384]{1,0:T(8,128)(2,1)S(1)}, u32[]{:S(2)}, u32[]{:S(2)}) collective-permute-start(bf16[76,384]{1,0:T(8,128)(2,1)S(1)} %fusion.25), channel_id=1, source_target_pairs={{0,2},{1,3},{2,0},{3,1},{4,6},{5,7},{6,4},{7,5},{8,10},{9,11},{10,... | collective-permute-start | bytes 175112 | tf_op jit(solution)/shard_map/ppermute | solution.py:527
  360.0 9.3 %collective-permute-start.29 = (bf16[264,384]{1,0:T(8,128)(2,1)S(1)}, bf16[264,384]{1,0:T(8,128)(2,1)S(1)}, u32[]{:S(2)}, u32[]{:S(2)}) collective-permute-start(bf16[264,384]{1,0:T(8,128)(2,1)S(1)} %fusion.18), channel_id=1, source_target_pairs={{0,2},{1,3},{2,0},{3,1},{4,6},{5,7},{6,4},{7,5},{8,10},{9,11},{10,... | collective-permute-start | bytes 608264 | tf_op jit(solution)/shard_map/ppermute | solution.py:527
  369.4 11.5 %collective-permute-start.31 = (bf16[2,264,384]{2,1,0:T(8,128)(2,1)S(1)}, bf16[2,264,384]{2,1,0:T(8,128)(2,1)S(1)}, u32[]{:S(2)}, u32[]{:S(2)}) collective-permute-start(bf16[2,264,384]{2,1,0:T(8,128)(2,1)S(1)} %pad_maximum_fusion.5), channel_id=1, source_target_pairs={{0,1},{1,0},{2,3},{3,2},{4,5},{5,4},{6,7},{7,6},{8,9},{9,8},{10,11... | collective-permute-start | bytes 1216520 | tf_op jit(solution)/shard_map/ppermute | solution.py:527
  369.5 9.2 %collective-permute-start.32 = (bf16[76,384]{1,0:T(8,128)(2,1)S(1)}, bf16[76,384]{1,0:T(8,128)(2,1)S(1)}, u32[]{:S(2)}, u32[]{:S(2)}) collective-permute-start(bf16[76,384]{1,0:T(8,128)(2,1)S(1)} %fusion.24), channel_id=1, source_target_pairs={{0,2},{1,3},{2,0},{3,1},{4,6},{5,7},{6,4},{7,5},{8,10},{9,11},{10,... | collective-permute-start | bytes 175112 | tf_op jit(solution)/shard_map/ppermute | solution.py:527
  381.3 1.2 copy-start.2
  381.5 4.9 %collective-permute-start.33 = (bf16[2,76,384]{2,1,0:T(8,128)(2,1)S(1)}, bf16[2,76,384]{2,1,0:T(8,128)(2,1)S(1)}, u32[]{:S(2)}, u32[]{:S(2)}) collective-permute-start(bf16[2,76,384]{2,1,0:T(8,128)(2,1)S(1)} %pad_maximum_fusion.6), channel_id=1, source_target_pairs={{0,1},{1,0},{2,3},{3,2},{4,5},{5,4},{6,7},{7,6},{8,9},{9,8},{10,11... | collective-permute-start | bytes 350216 | tf_op jit(solution)/shard_map/ppermute | solution.py:527
  384.4 4.0 %slice-start = ((f32[1056,384]{1,0:T(8,128)}), f32[288,384]{1,0:T(8,128)S(1)}, s32[]{:S(2)}) async-start(f32[1056,384]{1,0:T(8,128)} %copy-done.2), calls=%async_computation.5 | async-start | bytes 884736 | tf_op jit(solution)/shard_map/slice | solution.py:815
  386.4 3.0 copy-start.1
  (8 other events, 6.4 us)
Sparse Core Ops, SparseCore 0:
  11.1 93.3 all-gather.2
  172.6 78.3 reduce-scatter.1
